TPU v7x, 32 devices: a whole 2x2x4 slice. The times are simulated.
32 devices in a mesh: seq: 32 (over z, y, x, core), tp: 1.
Axes of the slice: x: 2, y: 2, z: 4, core: 2. Of those that a mesh axis runs over, the one named last changes fastest.
Arguments:
- band_qkv: bfloat16 [3, 8192, 3072], P(None, 'seq', 'tp'), may hold values from -5 to 5
- stride_qkv: bfloat16 [3, 8192, 3072], P(None, 'seq', 'tp'), may hold values from -5 to 5
- out_weight: bfloat16 [2, 3072, 6144], P(None, 'tp', 'seq'), may hold values from -1.25 to 1.25
- row_doc: int32 [32], replicated, may hold values from 0 to 3, never falling along the last dimension, each value on 1 to 16 neighbouring positions
Outputs:
- mixed: bfloat16 [8192, 6144], P('seq', 'tp')
Inputs may be any that keep to these rules, and one draw needn't show every extreme that they name: `row_doc`: document numbers never fall along the rows; a document spans 1 to 16 whole grid rows, one exactly that many.
All inputs are finite; a program needn't handle non-finite values.
Results may differ from a plain program's by a relative error of at most 0.014.
Values may be sent and summed in bfloat16 or wider, within the bound.
No kernel may reach another device: no remote copies, remote signals or barrier semaphores. Data moves between devices by JAX's collectives and lax.ppermute only.
A program may use at most 192 MiB of HBM per device.

v0:
```python
import math

import jax
import jax.numpy as jnp
from jax import lax
from jax.sharding import PartitionSpec as P

DH = 128
STRIDE = 256


NEGATIVE = -1e30


def shifted(array, axis, by):
    size = lax.axis_size(axis)
    pairs = [(i, i + by) for i in range(size) if 0 <= i + by < size]
    return lax.ppermute(array, axis, pairs)


def softmax_weights(scores, allowed):
    scores = jnp.where(allowed, scores, NEGATIVE)
    row_top = jnp.max(scores, axis=-1, keepdims=True)
    exponent = jnp.exp(scores - row_top)
    row_total = jnp.sum(exponent, axis=-1, keepdims=True)
    return (exponent / row_total).astype(jnp.bfloat16)


def per_device(band_qkv, stride_qkv, out_weight, row_doc):
    tokens = band_qkv.shape[1]
    feature_width = band_qkv.shape[2]
    head_count = feature_width // DH
    local_rows = tokens // STRIDE
    device_row = lax.axis_index("seq")
    last_row = band_qkv[1:, tokens - STRIDE :, :]
    before = shifted(last_row, "seq", 1)
    keys_all = jnp.concatenate([before, band_qkv[1:]], axis=1)
    padded_doc = jnp.concatenate([jnp.full((1,), -1, jnp.int32), row_doc])
    local_doc = lax.dynamic_slice_in_dim(padded_doc, device_row * local_rows, local_rows + 1)
    query_pos = jnp.arange(tokens, dtype=jnp.int32)
    key_pos = jnp.arange(tokens + STRIDE, dtype=jnp.int32) - STRIDE
    window = (key_pos[None, :] <= query_pos[:, None]) & (
        key_pos[None, :] > query_pos[:, None] - STRIDE
    )
    query_doc = jnp.repeat(local_doc[1:], STRIDE)
    key_doc = jnp.repeat(local_doc, STRIDE)
    allowed = window & (key_doc[None, :] == query_doc[:, None])
    queries = band_qkv[0].reshape(tokens, head_count, DH)
    band_keys = keys_all[0].reshape(tokens + STRIDE, head_count, DH)
    band_values = keys_all[1].reshape(tokens + STRIDE, head_count, DH)
    scores = jnp.einsum(
        "qhd,khd->hqk", queries, band_keys, preferred_element_type=jnp.float32
    ) / math.sqrt(DH)
    weights = softmax_weights(scores, allowed[None])
    band_out = jnp.einsum("hqk,khd->qhd", weights, band_values, preferred_element_type=jnp.float32)
    band_out = band_out.astype(jnp.bfloat16).reshape(tokens, feature_width)
    row_rank = jnp.arange(row_doc.shape[0], dtype=jnp.int32)
    column_mask = (row_rank[None, :] <= row_rank[:, None]) & (row_doc[None, :] == row_doc[:, None])
    stride_grid = stride_qkv.reshape(3, local_rows, STRIDE, head_count, DH)
    gathered = lax.all_to_all(stride_grid, "seq", split_axis=2, concat_axis=1, tiled=True)
    column_scores = jnp.einsum(
        "rchd,uchd->chru", gathered[0], gathered[1], preferred_element_type=jnp.float32
    ) / math.sqrt(DH)
    column_weights = softmax_weights(column_scores, column_mask)
    column_out = jnp.einsum(
        "chru,uchd->rchd", column_weights, gathered[2], preferred_element_type=jnp.float32
    )
    stride_out = lax.all_to_all(
        column_out.astype(jnp.bfloat16), "seq", split_axis=0, concat_axis=1, tiled=True
    )
    stride_out = stride_out.reshape(tokens, feature_width)
    weight_part = lax.all_gather(out_weight, "seq", axis=2, tiled=True)
    first = jnp.dot(band_out, weight_part[0], preferred_element_type=jnp.float32)
    terms = first + jnp.dot(stride_out, weight_part[1], preferred_element_type=jnp.float32)
    return lax.psum_scatter(terms.astype(jnp.bfloat16), "tp", scatter_dimension=1, tiled=True)


def solution(mesh):
    placed = (P(None, "seq", "tp"), P(None, "seq", "tp"), P(None, "tp", "seq"), P())
    return jax.shard_map(
        per_device, mesh=mesh, in_specs=placed, out_specs=P("seq", "tp"), check_vma=False
    )
```

profile of v0, /device:TPU:31, one launch (start us, length us, event | category | flops | bytes accessed | tf_op | source)
XLA Modules:
  0.0 599.4 jit_solution(3195221855767950033)
XLA Ops:
  6.5 0.0 all-gather.2.cloned.1.call-start
  6.5 0.7 all-gather.2.cloned.1.call-update
  7.3 6.6 %copy.37 = bf16[3,256,3072]{1,2,0:T(8,128)(2,1)} copy(bf16[3,256,3072]{2,1,0:T(8,128)(2,1)} %param.5) | data formatting | bytes 9437184 | tf_op args[1]
  13.9 7.1 %copy.38 = bf16[3,1,256,24,128]{4,3,1,0,2:T(8,128)(2,1)} copy(bf16[3,1,256,24,128]{2,4,3,0,1:T(8,128)(2,1)} %bitcast.51) | data formatting | bytes 9437184 | tf_op jit(solution)/shard_map/reshape | solution.py:59
  20.9 6.2 %all-to-all-start = ((bf16[3,1,256,24,128]{4,3,1,0,2:T(8,128)(2,1)}), bf16[3,1,256,24,128]{4,3,1,0,2:T(8,128)(2,1)}, u32[]{:S(2)}, u32[]{:S(2)}) async-start(bf16[3,1,256,24,128]{4,3,1,0,2:T(8,128)(2,1)} %copy.38), calls=%async_computation | async-start | bytes 9437184 | tf_op jit(solution)/shard_map/all_to_all | solution.py:60
  27.2 0.0 slice-start
  27.2 1.9 slice-done
  29.1 0.0 copy-start
  29.1 2.8 copy.51
  31.9 1.3 collective-permute-start
  33.2 0.0 copy-done
  33.2 0.1 pad_add_fusion
  33.3 0.1 dynamic_slice.3
  33.3 0.6 slice.39
  33.9 0.7 broadcast_compare_fusion
  34.7 0.1 broadcast_in_dim.20
  34.8 0.1 fusion.31
  34.8 191.1 %all-to-all-done = bf16[3,1,256,24,128]{4,3,1,0,2:T(8,128)(2,1)} async-done(((bf16[3,1,256,24,128]{4,3,1,0,2:T(8,128)(2,1)}), bf16[3,1,256,24,128]{4,3,1,0,2:T(8,128)(2,1)}, u32[]{:S(2)}, u32[]{:S(2)}) %all-to-all-start) | async-done | bytes 4718624 | tf_op jit(solution)/shard_map/all_to_all | solution.py:60
  225.9 3.2 fusion.36
  229.2 2.1 fusion.17
  231.3 1.1 fusion.37
  232.4 1.5 fusion.24
  233.9 1.8 copy.46
  235.6 0.0 slice-start.1
  235.7 17.6 %all-to-all-start.1 = ((bf16[32,8,24,128]{3,2,1,0:T(8,128)(2,1)}), bf16[32,8,24,128]{3,2,1,0:T(8,128)(2,1)}, u32[]{:S(2)}, u32[]{:S(2)}) async-start(bf16[32,8,24,128]{3,2,1,0:T(8,128)(2,1)} %copy.46), calls=%async_computation.1 | async-start | bytes 3145728 | tf_op jit(solution)/shard_map/all_to_all | solution.py:68
  253.3 0.2 fusion.30
  253.5 0.0 slice-done.1
  253.5 1.6 copy.52
  255.1 0.0 collective-permute-done
  255.1 4.2 pad_maximum_fusion
  259.3 11.1 %fusion.38 = (f32[24,256]{1,0:T(8,128)S(1)}, f32[24,256,512]{1,2,0:T(8,128)}) fusion(pred[256,512]{0,1:T(8,128)(4,1)S(1)} %fusion.30, bf16[512,24,128]{0,2,1:T(8,128)(2,1)} %bitcast.55, bf16[256,24,128]{0,2,1:T(8,128)(2,1)} %bitcast.57), kind=kOutput, calls=%fused_computation.53 | convolution fusion | flops 817889792 | bytes 17457152 | tf_op jit(solution)/shard_map/sub | solution.py:24
  270.3 6.8 %fusion.13 = bf16[24,128,256]{2,1,0:T(8,128)(2,1)} fusion(bf16[512,24,128]{0,2,1:T(8,128)(2,1)S(1)} %bitcast.54, f32[24,256,512]{1,2,0:T(8,128)} %get-tuple-element.13, f32[24,256]{1,0:T(8,128)S(1)} %get-tuple-element.12), kind=kOutput, calls=%fused_computation.24 | convolution fusion | flops 812384256 | bytes 17326080 | tf_op jit(solution)/shard_map/hqk,khd->qhd/dot_general | solution.py:55
  277.2 0.0 copy-start.1
  277.2 177.7 %all-to-all-done.1 = bf16[32,8,24,128]{3,2,1,0:T(8,128)(2,1)} async-done(((bf16[32,8,24,128]{3,2,1,0:T(8,128)(2,1)}), bf16[32,8,24,128]{3,2,1,0:T(8,128)(2,1)}, u32[]{:S(2)}, u32[]{:S(2)}) %all-to-all-start.1) | async-done | bytes 1572896 | tf_op jit(solution)/shard_map/all_to_all | solution.py:68
  454.9 98.8 %all-gather.2.cloned.1.call-done = bf16[2,3072,6144]{1,2,0:T(8,128)(2,1)} async-done(((bf16[2,3072,192]{1,2,0:T(8,128)(2,1)}), bf16[2,3072,6144]{1,2,0:T(8,128)(2,1)}) %all-gather.2.cloned.1.call-update) | async-done | bytes 75497488 | tf_op jit(solution)/shard_map/all_gather | solution.py:72
  553.6 19.4 %fusion.2 = f32[256,6144]{1,0:T(8,128)} fusion(bf16[2,3072,6144]{1,2,0:T(8,128)(2,1)} %all-gather.2.cloned.1.call-done, bf16[32,8,24,128]{3,2,1,0:T(8,128)(2,1)} %all-to-all-done.1), kind=kOutput, calls=%fused_computation.3 | convolution fusion | flops 9663676416 | bytes 45613056 | tf_op jit(solution)/shard_map/dot_general | solution.py:74
  573.0 0.0 copy-done.1
  573.0 19.5 %fusion.6 = bf16[256,6144]{1,0:T(8,128)(2,1)} fusion(f32[256,6144]{1,0:T(8,128)} %fusion.2, bf16[256,3072]{0,1:T(8,128)(2,1)S(1)} %bitcast.58, bf16[2,3072,6144]{1,2,0:T(8,128)(2,1)} %all-gather.2.cloned.1.call-done), kind=kOutput, calls=%fused_computation.11 | convolution fusion | flops 9666822144 | bytes 48758784 | tf_op jit(solution)/shard_map/dot_general | solution.py:73
  (3 shorter events, 0.0 us)
Async XLA Ops:
  6.5 547.1 %all-gather.2.cloned.1.call-start = ((), (), s32[]{:S(2)}) async-start(), calls=%async_computation.2 | async-start | bytes 77856768 | tf_op jit(solution)/shard_map/all_gather | solution.py:72
  20.9 205.0 %all-to-all-start = ((bf16[3,1,256,24,128]{4,3,1,0,2:T(8,128)(2,1)}), bf16[3,1,256,24,128]{4,3,1,0,2:T(8,128)(2,1)}, u32[]{:S(2)}, u32[]{:S(2)}) async-start(bf16[3,1,256,24,128]{4,3,1,0,2:T(8,128)(2,1)} %copy.38), calls=%async_computation | async-start | bytes 9437184 | tf_op jit(solution)/shard_map/all_to_all | solution.py:60
  27.2 1.9 slice-start
  29.1 4.1 copy-start
  31.9 223.2 %collective-permute-start = (bf16[2,256,3072]{1,2,0:T(8,128)(2,1)}, bf16[2,256,3072]{1,2,0:T(8,128)(2,1)}, u32[]{:S(2)}, u32[]{:S(2)}) collective-permute-start(bf16[2,256,3072]{1,2,0:T(8,128)(2,1)} %copy.51), channel_id=1, source_target_pairs={{0,1},{1,2},{2,3},{3,4},{4,5},{5,6},{6,7},{7,8},{8,9},{9,10},{10,1... | collective-permute-start | bytes 9437192 | tf_op jit(solution)/shard_map/ppermute | solution.py:18
  235.6 17.8 %slice-start.1 = ((bf16[3,256,3072]{2,1,0:T(8,128)(2,1)}), bf16[1,256,3072]{2,1,0:T(8,128)(2,1)S(1)}, s32[]{:S(2)}) async-start(bf16[3,256,3072]{2,1,0:T(8,128)(2,1)} %param.4), calls=%async_computation.4 | async-start | bytes 3145728 | tf_op jit(solution)/shard_map/slice | solution.py:48
  235.7 219.2 %all-to-all-start.1 = ((bf16[32,8,24,128]{3,2,1,0:T(8,128)(2,1)}), bf16[32,8,24,128]{3,2,1,0:T(8,128)(2,1)}, u32[]{:S(2)}, u32[]{:S(2)}) async-start(bf16[32,8,24,128]{3,2,1,0:T(8,128)(2,1)} %copy.46), calls=%async_computation.1 | async-start | bytes 3145728 | tf_op jit(solution)/shard_map/all_to_all | solution.py:68
  277.2 295.9 %copy-start.1 = (bf16[24,128,256]{2,1,0:T(8,128)(2,1)S(1)}, bf16[24,128,256]{2,1,0:T(8,128)(2,1)}, u32[]{:S(2)}) copy-start(bf16[24,128,256]{2,1,0:T(8,128)(2,1)} %fusion.13) | copy-start | bytes 4718596
Sparse Core Ops, SparseCore 0:
  10.3 543.2 all-gather.1
where the time goes:
time: 600 us; the launch traced here: 599 us
  waiting for transfers between devices  468 us (78%)
  matrix products  60.4 us (10%)
  local copies, waits for them, and re-layouts  25.7 us (4%)
  starting transfers between devices  25.2 us (4%)
  between operations  13.5 us (2%)
  other arithmetic  6.41 us (1%)
    all_to_all x1, waiting for transfers between devices, per_device(): lax.all_to_all(stride_grid, 'seq', split_axis=2, concat_axis=1, tiled=True)  191 us
    all_to_all x1, waiting for transfers between devices, per_device(): lax.all_to_all(column_out.astype(jnp.bfloat16), 'seq', split_axis=0, conc...  178 us
    all_gather x1, waiting for transfers between devices, per_device(): weight_part = lax.all_gather(out_weight, 'seq', axis=2, tiled=True)  98.8 us
    dot_general x1, matrix products, per_device(): jnp.dot(band_out, weight_part[0], preferred_element_type=jnp.float32)  19.5 us
    dot_general x1, matrix products, per_device(): jnp.dot(stride_out, weight_part[1], preferred_element_type=jnp.float32)  19.4 us
    all_to_all x1, starting transfers between devices, per_device(): lax.all_to_all(column_out.astype(jnp.bfloat16), 'seq', split_axis=0, conc...  17.6 us
  transfers between devices with their start and end apart: 4, of which 3 were waited for; matrix products, arithmetic and copies ran while one was open for 9% of the time, Pallas kernels for 0%

commit v1 on v0

v1 whole, which is shorter than its diff:
```python
import functools
import math

import jax
import jax.numpy as jnp
from jax import lax
from jax.experimental import pallas as pl
from jax.experimental.pallas import tpu as pltpu
from jax.sharding import PartitionSpec as P

DH = 128
STRIDE = 256
CORES = 2
MID = 4

NEGATIVE = -1e30


def scores_of(queries, keys):
    dims = (((1,), (1,)), ((), ()))
    return lax.dot_general(queries, keys, dims, preferred_element_type=jnp.float32)


def band_kernel(heads, joined_ref, own_ref, before_ref, out_ref):
    scale = 1.0 / math.sqrt(DH)
    tokens = own_ref.shape[1]
    row = lax.broadcasted_iota(jnp.int32, (tokens, tokens), 0)
    col = lax.broadcasted_iota(jnp.int32, (tokens, tokens), 1)
    own_mask = col <= row
    back_mask = (col > row) & (joined_ref[0] == 1)
    for head in range(heads):
        at = slice(head * DH, (head + 1) * DH)
        queries = own_ref[0, :, at]
        own_scores = jnp.where(own_mask, scores_of(queries, own_ref[1, :, at]) * scale, NEGATIVE)
        back_scores = jnp.where(back_mask, scores_of(queries, before_ref[0, :, at]) * scale, NEGATIVE)
        top = jnp.max(jnp.maximum(own_scores, back_scores), axis=-1, keepdims=True)
        own_exp = jnp.exp(own_scores - top)
        back_exp = jnp.exp(back_scores - top)
        total = jnp.sum(own_exp + back_exp, axis=-1, keepdims=True)
        inverse = 1.0 / total
        own_weights = (own_exp * inverse).astype(jnp.bfloat16)
        back_weights = (back_exp * inverse).astype(jnp.bfloat16)
        summed = jnp.dot(own_weights, own_ref[2, :, at], preferred_element_type=jnp.float32)
        summed += jnp.dot(back_weights, before_ref[1, :, at], preferred_element_type=jnp.float32)
        out_ref[:, at] = summed.astype(jnp.bfloat16)


def band_heads(joined, band_qkv, before):
    _, tokens, width = band_qkv.shape
    heads = math.gcd(width // DH, 3)
    block = heads * DH
    return pl.pallas_call(
        functools.partial(band_kernel, heads),
        out_shape=jax.ShapeDtypeStruct((tokens, width), jnp.bfloat16),
        grid_spec=pltpu.PrefetchScalarGridSpec(
            num_scalar_prefetch=1,
            grid=(width // block,),
            in_specs=[
                pl.BlockSpec((3, tokens, block), lambda h, joined: (0, 0, h)),
                pl.BlockSpec((2, tokens, block), lambda h, joined: (0, 0, h)),
            ],
            out_specs=pl.BlockSpec((tokens, block), lambda h, joined: (0, h)),
        ),
        cost_estimate=pl.CostEstimate(
            flops=8 * tokens * tokens * width,
            bytes_accessed=12 * tokens * width,
            transcendentals=2 * tokens * tokens * (width // DH),
        ),
        name="band",
    )(joined, band_qkv, before)


def stride_kernel(heads, cols, doc_row_ref, doc_col_ref, qkv_ref, out_ref, bias_ref):
    scale = 1.0 / math.sqrt(DH)
    rows = qkv_ref.shape[0]
    size = rows * cols

    @pl.when(pl.program_id(0) == 0)
    def _():
        row = lax.broadcasted_iota(jnp.int32, (size, size), 0)
        col = lax.broadcasted_iota(jnp.int32, (size, size), 1)
        allowed = (col <= row) & (lax.rem(col, cols) == lax.rem(row, cols))
        allowed &= doc_row_ref[...] == doc_col_ref[...]
        bias_ref[...] = jnp.where(allowed, 0.0, NEGATIVE)

    for head in range(heads):
        at = slice(head * DH, (head + 1) * DH)

        def part(which):
            got = qkv_ref[:, which, :, at].astype(jnp.float32)
            return got.reshape(size, DH).astype(jnp.bfloat16)

        scores = scores_of(part(0), part(1)) * scale
        scores = jnp.where(bias_ref[...] == 0.0, scores, NEGATIVE)
        top = jnp.max(scores, axis=-1, keepdims=True)
        exponent = jnp.exp(scores - top)
        inverse = 1.0 / jnp.sum(exponent, axis=-1, keepdims=True)
        weights = (exponent * inverse).astype(jnp.bfloat16)
        summed = jnp.dot(weights, part(2), preferred_element_type=jnp.float32)
        out_ref[:, :, at] = summed.reshape(rows, cols, DH).astype(jnp.bfloat16)


def stride_heads(row_doc, gathered):
    rows, _, cols, width = gathered.shape
    heads = math.gcd(width // DH, 3)
    block = heads * DH
    size = rows * cols
    docs = jnp.repeat(row_doc, cols)
    return pl.pallas_call(
        functools.partial(stride_kernel, heads, cols),
        out_shape=jax.ShapeDtypeStruct((rows, cols, width), jnp.bfloat16),
        grid=(width // block,),
        in_specs=[
            pl.BlockSpec((size, 1), lambda h: (0, 0)),
            pl.BlockSpec((1, size), lambda h: (0, 0)),
            pl.BlockSpec((rows, 3, cols, block), lambda h: (0, 0, 0, h)),
        ],
        out_specs=pl.BlockSpec((rows, cols, block), lambda h: (0, 0, h)),
        scratch_shapes=[pltpu.VMEM((size, size), jnp.float32)],
        cost_estimate=pl.CostEstimate(
            flops=4 * size * size * width,
            bytes_accessed=8 * size * width,
            transcendentals=size * size * (width // DH),
        ),
        name="strided",
    )(docs[:, None], docs[None, :], gathered)


def moved(array, step):
    size = lax.axis_size("seq")
    return lax.ppermute(array, "seq", [(i, i ^ (step * CORES)) for i in range(size)])


def spread(block):
    half = block.shape[0] // 2
    over_x = moved(block, 1)
    over_y = moved(block, 2)
    low = moved(over_x[:half], 2)
    high = moved(over_y[half:], 1)
    return [block, over_x, over_y, jnp.concatenate([low, high], axis=0)]


def per_device(band_qkv, stride_qkv, out_weight, row_doc):
    tokens, width = band_qkv.shape[1:]
    size = lax.axis_size("seq")
    me = lax.axis_index("seq")
    outer = size // (MID * CORES)
    share = out_weight.shape[2]
    cols = STRIDE // size

    grid = jnp.transpose(stride_qkv.reshape(3, size, cols, width), (1, 0, 2, 3))
    gathered = lax.all_to_all(grid, "seq", split_axis=0, concat_axis=0, tiled=True)

    before = lax.ppermute(band_qkv[1:], "seq", [(i, i + 1) for i in range(size - 1)])

    groups = [
        [(z * MID + m) * CORES + c for z in range(outer) for c in range(CORES)] for m in range(MID)
    ]
    turned = jnp.transpose(out_weight, (0, 2, 1))
    weights = [
        lax.all_gather(turned[i], "seq", axis=0, tiled=True, axis_index_groups=groups)
        for i in range(2)
    ]

    previous = jnp.where(me > 0, row_doc[jnp.maximum(me - 1, 0)], -1)
    joined = (previous == row_doc[me]).astype(jnp.int32).reshape(1)
    band_out = band_heads(joined, band_qkv, before)
    band_parts = spread(band_out)

    column_out = stride_heads(row_doc, gathered)
    stride_out = lax.all_to_all(column_out, "seq", split_axis=0, concat_axis=0, tiled=True)
    stride_parts = spread(stride_out.reshape(tokens, width))

    sent = []
    for step in (3, 1, 2, 0):
        terms = scores_of(band_parts[step], weights[0]) + scores_of(stride_parts[step], weights[1])
        block = terms.astype(jnp.bfloat16)
        sent.append((step, moved(block, step) if step else block))
    by_step = dict(sent)

    mine = (me // CORES) % MID
    stacked = jnp.stack([by_step[step] for step in range(MID)])
    picked = [lax.dynamic_index_in_dim(stacked, mine ^ m, 0, keepdims=False) for m in range(MID)]
    span = CORES * share
    pieces = []
    for z in range(outer):
        for m in range(MID):
            pieces.append(picked[m][:, z * span : (z + 1) * span])
    result = jnp.concatenate(pieces, axis=1)
    return lax.psum_scatter(result, "tp", scatter_dimension=1, tiled=True)


def solution(mesh):
    placed = (P(None, "seq", "tp"), P(None, "seq", "tp"), P(None, "tp", "seq"), P())
    return jax.shard_map(
        per_device, mesh=mesh, in_specs=placed, out_specs=P("seq", "tp"), check_vma=False
    )
```

time: 600 us -> 484 us (0.81)
  waiting for transfers between devices: 468 us -> 294 us
  starting transfers between devices: 25.2 us -> 80.7 us
  Pallas kernels: 0 us -> 24 us
  matrix products: 60.4 us -> 45.6 us
    all_to_all x2, waiting for transfers between devices: 369 us -> 244 us  [the longest x1 175 us: per_device(): lax.all_to_all(grid, 'seq', split_axis=0, concat_axis=0, tiled=True)]
    all_gather x1 -> x2, waiting for transfers between devices: 98.8 us -> 0.01 us  [per_device(): lax.all_gather(turned[i], 'seq', axis=0, tiled=True, axis_index_groups=gr...]
    ppermute x1 -> x12, starting transfers between devices: 1.28 us -> 68.3 us  [the longest x11 67 us: moved(): lax.ppermute(array, 'seq', [(i, i ^ step * CORES) for i in range(size)])]
    ppermute x1 -> x12, waiting for transfers between devices: 0.01 us -> 49.5 us  [the longest x11 49.5 us: moved(): lax.ppermute(array, 'seq', [(i, i ^ step * CORES) for i in range(size)])]
    pallas_call x0 -> x2, Pallas kernels: none -> 24 us  [the longest x1 13.4 us: band_heads(): pl.pallas_call(functools.partial(band_kernel, heads), out_shape=jax.Shape...]
    all_to_all x2, starting transfers between devices: 23.9 us -> 12.4 us  [the longest x1 6.19 us: per_device(): lax.all_to_all(column_out, 'seq', split_axis=0, concat_axis=0, tiled=True)]
    sub x1 -> x0, matrix products: 11.1 us -> none  [softmax_weights(): exponent = jnp.exp(scores - row_top)]
    unnamed x7 -> x23, local copies, waits for them, and re-layouts: 11 us -> 2.26 us
  transfers between devices with their start and end apart: 4 -> 16, of which waited for: 3 -> 8; matrix products, arithmetic and copies ran while one was open for 9% -> 11% of each run, Pallas kernels for 0% -> 5%
where the time goes in v1:
time: 484 us; the launch traced here: 480 us
  waiting for transfers between devices  294 us (61%)
  starting transfers between devices  80.7 us (17%)
  matrix products  45.6 us (9%)
  Pallas kernels  24 us (5%)
  local copies, waits for them, and re-layouts  20.2 us (4%)
  between operations  14.9 us (3%)
    all_to_all x1, waiting for transfers between devices, per_device(): lax.all_to_all(grid, 'seq', split_axis=0, concat_axis=0, tiled=True)  175 us
    all_to_all x1, waiting for transfers between devices, per_device(): lax.all_to_all(column_out, 'seq', split_axis=0, concat_axis=0, tiled=True)  68.9 us
    ppermute x11, starting transfers between devices, moved(): lax.ppermute(array, 'seq', [(i, i ^ step * CORES) for i in range(size)])  67 us
    ppermute x11, waiting for transfers between devices, moved(): lax.ppermute(array, 'seq', [(i, i ^ step * CORES) for i in range(size)])  49.5 us
    dot_general x8, matrix products, scores_of(): lax.dot_general(queries, keys, dims, preferred_element_type=jnp.float32)  45.6 us
    pallas_call x1, Pallas kernels, band_heads(): pl.pallas_call(functools.partial(band_kernel, heads), out_shape=jax.Shape...  13.4 us
    pallas_call x1, Pallas kernels, stride_heads(): pl.pallas_call(functools.partial(stride_kernel, heads, cols), out_shape=j...  10.6 us
  transfers between devices with their start and end apart: 16, of which 8 were waited for; matrix products, arithmetic and copies ran while one was open for 11% of the time, Pallas kernels for 5%

profile of v1, /device:TPU:31, one launch (start us, length us, event | category | flops | bytes accessed | tf_op | source)
XLA Modules:
  0.0 480.1 jit_solution(13058722089145096170)
XLA Ops:
  6.5 3.2 fusion.52
  9.9 0.7 all-gather.5.cloned.1.call-update
  10.6 4.9 %copy_bitcast_fusion = bf16[32,3,8,3072]{3,2,1,0:T(8,128)(2,1)} fusion(bf16[3,256,3072]{2,1,0:T(8,128)(2,1)} %param.5), kind=kLoop, calls=%fused_computation.16 | loop fusion | bytes 9437184 | tf_op jit(solution)/shard_map/transpose | solution.py:151
  15.4 6.2 %all-to-all-start = ((bf16[32,3,8,3072]{3,2,1,0:T(8,128)(2,1)}), bf16[32,3,8,3072]{3,2,1,0:T(8,128)(2,1)}, u32[]{:S(2)}, u32[]{:S(2)}) async-start(bf16[32,3,8,3072]{3,2,1,0:T(8,128)(2,1)} %copy_bitcast_fusion), calls=%async_computation | async-start | bytes 9437184 | tf_op jit(solution)/shard_map/all_to_all | solution.py:152
  21.6 0.1 broadcast_in_dim.3
  21.7 0.8 broadcast_in_dim_reshape.8.doc_row_ref
  22.4 0.7 broadcast_in_dim_reshape.7.doc_col_ref
  23.1 175.2 %all-to-all-done.qkv_ref = bf16[32,3,8,3072]{3,2,1,0:T(8,128)(2,1)} async-done(((bf16[32,3,8,3072]{3,2,1,0:T(8,128)(2,1)}), bf16[32,3,8,3072]{3,2,1,0:T(8,128)(2,1)}, u32[]{:S(2)}, u32[]{:S(2)}) %all-to-all-start) | async-done | bytes 4718624 | tf_op jit(solution)/shard_map/all_to_all | solution.py:152
  198.3 10.6 %strided.1 = bf16[32,8,3072]{2,1,0:T(8,128)(2,1)} custom-call(s32[256,1]{1,0:T(8,128)} %broadcast_in_dim_reshape.8.doc_row_ref, s32[1,256]{1,0:T(1,128)} %broadcast_in_dim_reshape.7.doc_col_ref, bf16[32,3,8,3072]{3,2,1,0:T(8,128)(2,1)} %all-to-all-done.qkv_ref), custom_call_target="tpu_custom_call" | custom-call | flops 805306368 | bytes 6291456 | tf_op jit(solution)/shard_map/strided/pallas_call | solution.py:109
  208.9 6.2 %all-to-all-start.1 = ((bf16[32,8,3072]{2,1,0:T(8,128)(2,1)}), bf16[32,8,3072]{2,1,0:T(8,128)(2,1)}, u32[]{:S(2)}, u32[]{:S(2)}) async-start(bf16[32,8,3072]{2,1,0:T(8,128)(2,1)} %strided.1), calls=%async_computation.1 | async-start | bytes 3145728 | tf_op jit(solution)/shard_map/all_to_all | solution.py:171
  215.1 2.2 slice.69
  217.3 1.3 collective-permute-start
  218.6 68.9 %all-to-all-done.1 = bf16[32,8,3072]{2,1,0:T(8,128)(2,1)} async-done(((bf16[32,8,3072]{2,1,0:T(8,128)(2,1)}), bf16[32,8,3072]{2,1,0:T(8,128)(2,1)}, u32[]{:S(2)}, u32[]{:S(2)}) %all-to-all-start.1) | async-done | bytes 1572896 | tf_op jit(solution)/shard_map/all_to_all | solution.py:171
  287.5 5.3 %collective-permute-start.5 = (bf16[256,3072]{1,0:T(8,128)(2,1)}, bf16[256,3072]{1,0:T(8,128)(2,1)}, u32[]{:S(2)}, u32[]{:S(2)}) collective-permute-start(bf16[256,3072]{1,0:T(8,128)(2,1)} %bitcast.7), channel_id=1, source_target_pairs={{0,4},{1,5},{2,6},{3,7},{4,0},{5,1},{6,2},{7,3},{8,12},{9,13},{10,... | collective-permute-start | bytes 4718600 | tf_op jit(solution)/shard_map/ppermute | solution.py:131
  292.8 0.4 collective-permute-start.2
  293.2 0.6 fusion.53
  295.0 13.4 %band.1 = bf16[256,3072]{1,0:T(8,128)(2,1)} custom-call(s32[1]{0:T(128)} %bitcast.2.joined_ref, bf16[3,256,3072]{2,1,0:T(8,128)(2,1)} %own_ref.1, bf16[2,256,3072]{2,1,0:T(8,128)(2,1)} %collective-permute-done.before_ref), custom_call_target="tpu_custom_call" | custom-call | flops 1610612736 | bytes 9437184 | tf_op jit(solution)/shard_map/band/pallas_call | solution.py:52
  308.3 1.1 collective-permute-start.4
  309.4 0.1 collective-permute-start.1
  309.5 17.6 %collective-permute-done.5 = bf16[256,3072]{1,0:T(8,128)(2,1)} collective-permute-done((bf16[256,3072]{1,0:T(8,128)(2,1)}, bf16[256,3072]{1,0:T(8,128)(2,1)}, u32[]{:S(2)}, u32[]{:S(2)}) %collective-permute-start.5) | collective-permute-done | bytes 1572896 | tf_op jit(solution)/shard_map/ppermute | solution.py:131
  327.0 1.2 slice.97
  328.2 26.0 %collective-permute-start.10 = (bf16[128,3072]{1,0:T(8,128)(2,1)S(1)}, bf16[128,3072]{1,0:T(8,128)(2,1)}, u32[]{:S(2)}, u32[]{:S(2)}) collective-permute-start(bf16[128,3072]{1,0:T(8,128)(2,1)S(1)} %slice.97), channel_id=1, source_target_pairs={{0,2},{1,3},{2,0},{3,1},{4,6},{5,7},{6,4},{7,5},{8,10},{9,11},{10,... | collective-permute-start | bytes 2359304 | tf_op jit(solution)/shard_map/ppermute | solution.py:131
  354.2 1.2 slice.96
  355.4 2.3 collective-permute-start.9
  357.6 3.1 collective-permute-done.4
  360.7 1.2 slice.95
  361.9 26.0 %collective-permute-start.8 = (bf16[128,3072]{1,0:T(8,128)(2,1)S(1)}, bf16[128,3072]{1,0:T(8,128)(2,1)}, u32[]{:S(2)}, u32[]{:S(2)}) collective-permute-start(bf16[128,3072]{1,0:T(8,128)(2,1)S(1)} %slice.95), channel_id=1, source_target_pairs={{0,2},{1,3},{2,0},{3,1},{4,6},{5,7},{6,4},{7,5},{8,10},{9,11},{10,... | collective-permute-start | bytes 2359304 | tf_op jit(solution)/shard_map/ppermute | solution.py:131
  387.9 1.2 slice.94
  389.1 2.3 collective-permute-start.7
  391.3 11.5 %collective-permute-done.10 = bf16[128,3072]{1,0:T(8,128)(2,1)} collective-permute-done((bf16[128,3072]{1,0:T(8,128)(2,1)S(1)}, bf16[128,3072]{1,0:T(8,128)(2,1)}, u32[]{:S(2)}, u32[]{:S(2)}) %collective-permute-start.10) | collective-permute-done | bytes 786464 | tf_op jit(solution)/shard_map/ppermute | solution.py:131
  402.8 5.9 %fusion = f32[256,1536]{1,0:T(8,128)S(1)} fusion(bf16[1,1536,3072]{2,1,0:T(8,128)(2,1)} %all-gather.7.cloned.1.call-done, bf16[128,3072]{1,0:T(8,128)(2,1)} %collective-permute-done.10, bf16[128,3072]{1,0:T(8,128)(2,1)} %collective-permute-done.9), kind=kOutput, calls=%fused_computation | convolution fusion | flops 2419064832 | bytes 12582912 | tf_op jit(solution)/shard_map/dot_general | solution.py:21
  408.7 11.0 %collective-permute-done.8 = bf16[128,3072]{1,0:T(8,128)(2,1)} collective-permute-done((bf16[128,3072]{1,0:T(8,128)(2,1)S(1)}, bf16[128,3072]{1,0:T(8,128)(2,1)}, u32[]{:S(2)}, u32[]{:S(2)}) %collective-permute-start.8) | collective-permute-done | bytes 786464 | tf_op jit(solution)/shard_map/ppermute | solution.py:131
  419.7 6.9 %fusion.28 = bf16[256,1536]{1,0:T(8,128)(2,1)S(1)} fusion(f32[256,1536]{1,0:T(8,128)S(1)} %fusion, bf16[1,1536,3072]{2,1,0:T(8,128)(2,1)} %all-gather.5.cloned.1.call-done, bf16[128,3072]{1,0:T(8,128)(2,1)} %collective-permute-done.8, bf16[128,3072]{1,0:T(8,128)(2,1)} %collective-permute-done.7), kind=kOutput, calls=%fused_computation.22 | convolution fusion | flops 2419851264 | bytes 13369344 | tf_op jit(solution)/shard_map/dot_general | solution.py:21
  426.6 2.7 collective-permute-start.11
  429.3 4.2 fusion.2
  433.4 6.8 %fusion.31 = bf16[256,1536]{1,0:T(8,128)(2,1)S(1)} fusion(f32[256,1536]{1,0:T(8,128)S(1)} %fusion.2, bf16[256,3072]{1,0:T(8,128)(2,1)} %collective-permute-done.4, bf16[1,1536,3072]{2,1,0:T(8,128)(2,1)} %all-gather.5.cloned.1.call-done), kind=kOutput, calls=%fused_computation.23 | convolution fusion | flops 2416705536 | bytes 13369344 | tf_op jit(solution)/shard_map/dot_general | solution.py:21
  440.3 1.0 collective-permute-start.6
  441.2 4.2 fusion.4
  445.4 7.1 %fusion.34 = bf16[256,1536]{1,0:T(8,128)(2,1)S(1)} fusion(f32[256,1536]{1,0:T(8,128)S(1)} %fusion.4, bf16[256,3072]{1,0:T(8,128)(2,1)} %collective-permute-done.1, bf16[1,1536,3072]{2,1,0:T(8,128)(2,1)} %all-gather.5.cloned.1.call-done), kind=kOutput, calls=%fused_computation.24 | convolution fusion | flops 2416705536 | bytes 13369344 | tf_op jit(solution)/shard_map/dot_general | solution.py:21
  452.5 0.1 collective-permute-start.3
  452.6 4.3 fusion.6
  456.8 6.3 %fusion.40 = bf16[1,256,1536]{2,1,0:T(8,128)(2,1)S(1)} fusion(f32[256,1536]{1,0:T(8,128)S(1)} %fusion.6, bf16[256,3072]{1,0:T(8,128)(2,1)S(1)} %copy-done, bf16[1,1536,3072]{2,1,0:T(8,128)(2,1)} %all-gather.5.cloned.1.call-done), kind=kOutput, calls=%fused_computation.26 | convolution fusion | flops 2416705536 | bytes 13369344 | tf_op jit(solution)/shard_map/dot_general | solution.py:21
  463.2 0.9 collective-permute-done.6
  464.1 5.4 %collective-permute-done.3 = bf16[256,1536]{1,0:T(8,128)(2,1)S(1)} collective-permute-done((bf16[256,1536]{1,0:T(8,128)(2,1)S(1)}, bf16[256,1536]{1,0:T(8,128)(2,1)S(1)}, u32[]{:S(2)}, u32[]{:S(2)}) %collective-permute-start.3) | collective-permute-done | bytes 786464 | tf_op jit(solution)/shard_map/ppermute | solution.py:131
  469.5 0.4 pad_maximum_fusion
  470.0 0.2 dynamic-slice_bitcast_fusion
  470.9 1.7 copy-done.1
  472.6 0.7 slice_dynamic-update-slice_fusion
  (33 shorter events, 0.7 us)
Async XLA Ops:
  6.5 396.3 %all-gather.7.cloned.1.call-start = ((), (), s32[]{:S(2)}) async-start(), calls=%async_computation.3 | async-start | bytes 10616832 | tf_op jit(solution)/shard_map/all_gather | solution.py:161
  9.8 409.9 %all-gather.5.cloned.1.call-start = ((), (), s32[]{:S(2)}) async-start(), calls=%async_computation.2 | async-start | bytes 10616832 | tf_op jit(solution)/shard_map/all_gather | solution.py:161
  15.4 6.2 %copy-start.2 = (s32[32]{0:T(128)S(1)}, s32[32]{0:T(128)}, u32[]{:S(2)}) copy-start(s32[32]{0:T(128)} %param.7) | copy-start | bytes 388
  15.4 182.9 %all-to-all-start = ((bf16[32,3,8,3072]{3,2,1,0:T(8,128)(2,1)}), bf16[32,3,8,3072]{3,2,1,0:T(8,128)(2,1)}, u32[]{:S(2)}, u32[]{:S(2)}) async-start(bf16[32,3,8,3072]{3,2,1,0:T(8,128)(2,1)} %copy_bitcast_fusion), calls=%async_computation | async-start | bytes 9437184 | tf_op jit(solution)/shard_map/all_to_all | solution.py:152
  208.9 78.5 %all-to-all-start.1 = ((bf16[32,8,3072]{2,1,0:T(8,128)(2,1)}), bf16[32,8,3072]{2,1,0:T(8,128)(2,1)}, u32[]{:S(2)}, u32[]{:S(2)}) async-start(bf16[32,8,3072]{2,1,0:T(8,128)(2,1)} %strided.1), calls=%async_computation.1 | async-start | bytes 3145728 | tf_op jit(solution)/shard_map/all_to_all | solution.py:171
  217.3 77.6 %collective-permute-start = (bf16[2,256,3072]{2,1,0:T(8,128)(2,1)S(1)}, bf16[2,256,3072]{2,1,0:T(8,128)(2,1)}, u32[]{:S(2)}, u32[]{:S(2)}) collective-permute-start(bf16[2,256,3072]{2,1,0:T(8,128)(2,1)S(1)} %slice.69), channel_id=1, source_target_pairs={{0,1},{1,2},{2,3},{3,4},{4,5},{5,6},{6,7},{7,8},{8,9},{9,10},{10,1... | collective-permute-start | bytes 9437192 | tf_op jit(solution)/shard_map/ppermute | solution.py:154
  287.5 39.5 %collective-permute-start.5 = (bf16[256,3072]{1,0:T(8,128)(2,1)}, bf16[256,3072]{1,0:T(8,128)(2,1)}, u32[]{:S(2)}, u32[]{:S(2)}) collective-permute-start(bf16[256,3072]{1,0:T(8,128)(2,1)} %bitcast.7), channel_id=1, source_target_pairs={{0,4},{1,5},{2,6},{3,7},{4,0},{5,1},{6,2},{7,3},{8,12},{9,13},{10,... | collective-permute-start | bytes 4718600 | tf_op jit(solution)/shard_map/ppermute | solution.py:131
  292.8 61.4 %collective-permute-start.2 = (bf16[256,3072]{1,0:T(8,128)(2,1)}, bf16[256,3072]{1,0:T(8,128)(2,1)}, u32[]{:S(2)}, u32[]{:S(2)}) collective-permute-start(bf16[256,3072]{1,0:T(8,128)(2,1)} %bitcast.7), channel_id=1, source_target_pairs={{0,2},{1,3},{2,0},{3,1},{4,6},{5,7},{6,4},{7,5},{8,10},{9,11},{10,... | collective-permute-start | bytes 4718600 | tf_op jit(solution)/shard_map/ppermute | solution.py:131
  308.3 52.4 %collective-permute-start.4 = (bf16[256,3072]{1,0:T(8,128)(2,1)}, bf16[256,3072]{1,0:T(8,128)(2,1)}, u32[]{:S(2)}, u32[]{:S(2)}) collective-permute-start(bf16[256,3072]{1,0:T(8,128)(2,1)} %band.1), channel_id=1, source_target_pairs={{0,4},{1,5},{2,6},{3,7},{4,0},{5,1},{6,2},{7,3},{8,12},{9,13},{10,... | collective-permute-start | bytes 4718600 | tf_op jit(solution)/shard_map/ppermute | solution.py:131
  309.4 78.5 %collective-permute-start.1 = (bf16[256,3072]{1,0:T(8,128)(2,1)}, bf16[256,3072]{1,0:T(8,128)(2,1)}, u32[]{:S(2)}, u32[]{:S(2)}) collective-permute-start(bf16[256,3072]{1,0:T(8,128)(2,1)} %band.1), channel_id=1, source_target_pairs={{0,2},{1,3},{2,0},{3,1},{4,6},{5,7},{6,4},{7,5},{8,10},{9,11},{10,... | collective-permute-start | bytes 4718600 | tf_op jit(solution)/shard_map/ppermute | solution.py:131
  328.2 74.6 %collective-permute-start.10 = (bf16[128,3072]{1,0:T(8,128)(2,1)S(1)}, bf16[128,3072]{1,0:T(8,128)(2,1)}, u32[]{:S(2)}, u32[]{:S(2)}) collective-permute-start(bf16[128,3072]{1,0:T(8,128)(2,1)S(1)} %slice.97), channel_id=1, source_target_pairs={{0,2},{1,3},{2,0},{3,1},{4,6},{5,7},{6,4},{7,5},{8,10},{9,11},{10,... | collective-permute-start | bytes 2359304 | tf_op jit(solution)/shard_map/ppermute | solution.py:131
  355.4 47.4 %collective-permute-start.9 = (bf16[128,3072]{1,0:T(8,128)(2,1)S(1)}, bf16[128,3072]{1,0:T(8,128)(2,1)}, u32[]{:S(2)}, u32[]{:S(2)}) collective-permute-start(bf16[128,3072]{1,0:T(8,128)(2,1)S(1)} %slice.96), channel_id=1, source_target_pairs={{0,4},{1,5},{2,6},{3,7},{4,0},{5,1},{6,2},{7,3},{8,12},{9,13},{10,... | collective-permute-start | bytes 2359304 | tf_op jit(solution)/shard_map/ppermute | solution.py:131
  361.9 57.8 %collective-permute-start.8 = (bf16[128,3072]{1,0:T(8,128)(2,1)S(1)}, bf16[128,3072]{1,0:T(8,128)(2,1)}, u32[]{:S(2)}, u32[]{:S(2)}) collective-permute-start(bf16[128,3072]{1,0:T(8,128)(2,1)S(1)} %slice.95), channel_id=1, source_target_pairs={{0,2},{1,3},{2,0},{3,1},{4,6},{5,7},{6,4},{7,5},{8,10},{9,11},{10,... | collective-permute-start | bytes 2359304 | tf_op jit(solution)/shard_map/ppermute | solution.py:131
  389.1 30.6 %collective-permute-start.7 = (bf16[128,3072]{1,0:T(8,128)(2,1)S(1)}, bf16[128,3072]{1,0:T(8,128)(2,1)}, u32[]{:S(2)}, u32[]{:S(2)}) collective-permute-start(bf16[128,3072]{1,0:T(8,128)(2,1)S(1)} %slice.94), channel_id=1, source_target_pairs={{0,4},{1,5},{2,6},{3,7},{4,0},{5,1},{6,2},{7,3},{8,12},{9,13},{10,... | collective-permute-start | bytes 2359304 | tf_op jit(solution)/shard_map/ppermute | solution.py:131
  419.7 9.6 %copy-start.3 = (bf16[1,1536,3072]{2,1,0:T(8,128)(2,1)S(1)}, bf16[1,1536,3072]{2,1,0:T(8,128)(2,1)}, u32[]{:S(2)}) copy-start(bf16[1,1536,3072]{2,1,0:T(8,128)(2,1)} %all-gather.7.cloned.1.call-done) | copy-start | bytes 28311556
  426.6 36.6 %collective-permute-start.11 = (bf16[256,1536]{1,0:T(8,128)(2,1)S(1)}, bf16[256,1536]{1,0:T(8,128)(2,1)S(1)}, u32[]{:S(2)}, u32[]{:S(2)}) collective-permute-start(bf16[256,1536]{1,0:T(8,128)(2,1)S(1)} %fusion.28), channel_id=1, source_target_pairs={{0,6},{1,7},{2,4},{3,5},{4,2},{5,3},{6,0},{7,1},{8,14},{9,15},{10,... | collective-permute-start | bytes 2359304 | tf_op jit(solution)/shard_map/ppermute | solution.py:131
  440.3 23.9 %collective-permute-start.6 = (bf16[256,1536]{1,0:T(8,128)(2,1)S(1)}, bf16[256,1536]{1,0:T(8,128)(2,1)S(1)}, u32[]{:S(2)}, u32[]{:S(2)}) collective-permute-start(bf16[256,1536]{1,0:T(8,128)(2,1)S(1)} %fusion.31), channel_id=1, source_target_pairs={{0,4},{1,5},{2,6},{3,7},{4,0},{5,1},{6,2},{7,3},{8,12},{9,13},{10,... | collective-permute-start | bytes 2359304 | tf_op jit(solution)/shard_map/ppermute | solution.py:131
  452.5 4.4 copy-start
  452.5 17.1 %collective-permute-start.3 = (bf16[256,1536]{1,0:T(8,128)(2,1)S(1)}, bf16[256,1536]{1,0:T(8,128)(2,1)S(1)}, u32[]{:S(2)}, u32[]{:S(2)}) collective-permute-start(bf16[256,1536]{1,0:T(8,128)(2,1)S(1)} %fusion.34), channel_id=1, source_target_pairs={{0,2},{1,3},{2,0},{3,1},{4,6},{5,7},{6,4},{7,5},{8,10},{9,11},{10,... | collective-permute-start | bytes 2359304 | tf_op jit(solution)/shard_map/ppermute | solution.py:131
  470.9 1.7 copy-start.1
Sparse Core Ops, SparseCore 0:
  9.9 177.3 all-gather.6
  189.0 129.2 all-gather.4

commit v2 on v1

--- a/solution.py
+++ b/solution.py
@@ -8,6 +8,7 @@
 from jax.experimental.pallas import tpu as pltpu
 from jax.sharding import PartitionSpec as P
 
+
 DH = 128
 STRIDE = 256
 CORES = 2
@@ -21,7 +22,8 @@
     return lax.dot_general(queries, keys, dims, preferred_element_type=jnp.float32)
 
 
-def band_kernel(heads, joined_ref, own_ref, before_ref, out_ref):
+def band_kernel(heads, joined_ref, own_ref, twin_ref, keys_ref, values_ref, out_ref):
+    paired = joined_ref[1] == 1
     scale = 1.0 / math.sqrt(DH)
     tokens = own_ref.shape[1]
     row = lax.broadcasted_iota(jnp.int32, (tokens, tokens), 0)
@@ -31,8 +33,10 @@
     for head in range(heads):
         at = slice(head * DH, (head + 1) * DH)
         queries = own_ref[0, :, at]
+        before_keys = jnp.where(paired, twin_ref[0, :, at], keys_ref[:, at])
+        before_values = jnp.where(paired, twin_ref[1, :, at], values_ref[:, at])
         own_scores = jnp.where(own_mask, scores_of(queries, own_ref[1, :, at]) * scale, NEGATIVE)
-        back_scores = jnp.where(back_mask, scores_of(queries, before_ref[0, :, at]) * scale, NEGATIVE)
+        back_scores = jnp.where(back_mask, scores_of(queries, before_keys) * scale, NEGATIVE)
         top = jnp.max(jnp.maximum(own_scores, back_scores), axis=-1, keepdims=True)
         own_exp = jnp.exp(own_scores - top)
         back_exp = jnp.exp(back_scores - top)
@@ -41,11 +45,11 @@
         own_weights = (own_exp * inverse).astype(jnp.bfloat16)
         back_weights = (back_exp * inverse).astype(jnp.bfloat16)
         summed = jnp.dot(own_weights, own_ref[2, :, at], preferred_element_type=jnp.float32)
-        summed += jnp.dot(back_weights, before_ref[1, :, at], preferred_element_type=jnp.float32)
+        summed += jnp.dot(back_weights, before_values, preferred_element_type=jnp.float32)
         out_ref[:, at] = summed.astype(jnp.bfloat16)
 
 
-def band_heads(joined, band_qkv, before):
+def band_heads(joined, band_qkv, twin, keys, values):
     _, tokens, width = band_qkv.shape
     heads = math.gcd(width // DH, 3)
     block = heads * DH
@@ -58,6 +62,8 @@
             in_specs=[
                 pl.BlockSpec((3, tokens, block), lambda h, joined: (0, 0, h)),
                 pl.BlockSpec((2, tokens, block), lambda h, joined: (0, 0, h)),
+                pl.BlockSpec((tokens, block), lambda h, joined: (0, h)),
+                pl.BlockSpec((tokens, block), lambda h, joined: (0, h)),
             ],
             out_specs=pl.BlockSpec((tokens, block), lambda h, joined: (0, h)),
         ),
@@ -67,7 +73,7 @@
             transcendentals=2 * tokens * tokens * (width // DH),
         ),
         name="band",
-    )(joined, band_qkv, before)
+    )(joined, band_qkv, twin, keys, values)
 
 
 def stride_kernel(heads, cols, doc_row_ref, doc_col_ref, qkv_ref, out_ref, bias_ref):
@@ -131,13 +137,126 @@
     return lax.ppermute(array, "seq", [(i, i ^ (step * CORES)) for i in range(size)])
 
 
-def spread(block):
-    half = block.shape[0] // 2
-    over_x = moved(block, 1)
-    over_y = moved(block, 2)
-    low = moved(over_x[:half], 2)
-    high = moved(over_y[half:], 1)
-    return [block, over_x, over_y, jnp.concatenate([low, high], axis=0)]
+def near_parts(block):
+    return moved(block, 1), moved(block, 2)
+
+
+def far_parts(over_x, over_y):
+    half = over_x.shape[0] // 2
+    return moved(over_x[:half], 2), moved(over_y[half:], 1)
+
+
+def sent_back(blocks):
+    return [moved(block, step) if step else block for step, block in enumerate(blocks)]
+
+
+def project_kernel(*refs):
+    count = MID + 1
+    sources = (refs[:count], refs[count : 2 * count])
+    weight_ref = refs[2 * count]
+    out_refs = refs[2 * count + 1 : 2 * count + 1 + MID]
+    held_ref, sems = refs[-2:]
+    tokens = out_refs[0].shape[0]
+    first = pl.program_id(0) == 0
+
+    def copies(which):
+        place = 0
+        for index, source in enumerate(sources[which]):
+            rows = source.shape[0]
+            target = held_ref.at[which, pl.ds(place, rows)]
+            yield pltpu.make_async_copy(source, target, sems.at[which, index])
+            place += rows
+
+    @pl.when(first)
+    def _():
+        for which in range(2):
+            for copy in copies(which):
+                copy.start()
+
+    terms = None
+    for which in range(2):
+
+        @pl.when(first)
+        def _():
+            for copy in copies(which):
+                copy.wait()
+
+        weight = weight_ref[:, :, which]
+        weight = weight.reshape(-1, weight.shape[-1])
+        found = scores_of(held_ref[which], weight)
+        terms = found if terms is None else terms + found
+    for part in range(MID):
+        out_refs[part][...] = terms[part * tokens : (part + 1) * tokens].astype(jnp.bfloat16)
+
+
+def project(band_parts, stride_parts, weight):
+    tokens, depth = band_parts[0].shape
+    outer, cores, _, rows, _ = weight.shape
+    block = cores * rows
+    columns = outer * block
+    if block % 128:
+        terms = 0.0
+        for which, parts in enumerate((band_parts, stride_parts)):
+            flat = weight[:, :, which].reshape(columns, depth)
+            terms = terms + scores_of(jnp.concatenate(parts, axis=0), flat)
+        return list(terms.astype(jnp.bfloat16).reshape(MID, tokens, columns))
+    group = max(1, min(outer, 256 // block))
+    return pl.pallas_call(
+        project_kernel,
+        out_shape=[jax.ShapeDtypeStruct((tokens, columns), jnp.bfloat16)] * MID,
+        grid=(outer // group,),
+        in_specs=[pl.BlockSpec(memory_space=pl.ANY)] * (2 * MID + 2)
+        + [pl.BlockSpec((group, cores, 2, rows, depth), lambda z: (z, 0, 0, 0, 0))],
+        out_specs=[pl.BlockSpec((tokens, group * block), lambda z: (0, z))] * MID,
+        scratch_shapes=[
+            pltpu.VMEM((2, MID * tokens, depth), jnp.bfloat16),
+            pltpu.SemaphoreType.DMA((2, MID + 1)),
+        ],
+        cost_estimate=pl.CostEstimate(
+            flops=4 * MID * tokens * depth * columns,
+            bytes_accessed=4 * (MID * tokens + columns) * depth + 2 * MID * tokens * columns,
+            transcendentals=0,
+        ),
+        name="project",
+    )(*band_parts, *stride_parts, weight)
+
+
+def assemble_kernel(cuts, mine_ref, *refs):
+    out_ref = refs[-1]
+    span = sum(cut[1] for cut in cuts)
+    for step in range(MID):
+        base = (mine_ref[0] ^ step) * span
+        for chunk, size, source, target in cuts:
+            at = pl.multiple_of(base + target, 128)
+            out_ref[:, pl.ds(at, size)] = refs[chunk * MID + step][:, source : source + size]
+
+
+def assemble(mine, chunks, outer):
+    tokens = chunks[0][0].shape[0]
+    widths = [chunk[0].shape[1] // outer for chunk in chunks]
+    span = sum(widths)
+    if len(chunks) == 1:
+        cuts = ((0, span, 0, 0),)
+    else:
+        side = widths[0] // 2
+        cuts = ((0, side, 0, 0), (1, widths[1], 0, side), (0, side, side, side + widths[1]))
+    if len(chunks) == 1 and span % 128:
+        stacked = jnp.stack(chunks[0])
+        picked = [lax.dynamic_index_in_dim(stacked, mine ^ m, 0, keepdims=False) for m in range(MID)]
+        pieces = [picked[m][:, z * span : (z + 1) * span] for z in range(outer) for m in range(MID)]
+        return jnp.concatenate(pieces, axis=1)
+    specs = [pl.BlockSpec((tokens, width), lambda z, mine: (0, z)) for width in widths for _ in range(MID)]
+    return pl.pallas_call(
+        functools.partial(assemble_kernel, cuts),
+        out_shape=jax.ShapeDtypeStruct((tokens, MID * outer * span), jnp.bfloat16),
+        grid_spec=pltpu.PrefetchScalarGridSpec(
+            num_scalar_prefetch=1,
+            grid=(outer,),
+            in_specs=specs,
+            out_specs=pl.BlockSpec((tokens, MID * span), lambda z, mine: (0, z)),
+        ),
+        name="assemble",
+    )(mine.reshape(1), *[block for chunk in chunks for block in chunk])
 
 
 def per_device(band_qkv, stride_qkv, out_weight, row_doc):
@@ -145,48 +264,56 @@
     size = lax.axis_size("seq")
     me = lax.axis_index("seq")
     outer = size // (MID * CORES)
+    cols = STRIDE // size
     share = out_weight.shape[2]
-    cols = STRIDE // size
-
+
+    twin = lax.ppermute(band_qkv[1:], "seq", [(i, i ^ 1) for i in range(size)])
+    last = range(CORES - 1, size - 1, CORES)
+    keys = lax.ppermute(band_qkv[1], "seq", [(i, i + 1) for i in last])
+    values = lax.ppermute(twin[1], "seq", [(i - 1, i + 1) for i in last])
     grid = jnp.transpose(stride_qkv.reshape(3, size, cols, width), (1, 0, 2, 3))
     gathered = lax.all_to_all(grid, "seq", split_axis=0, concat_axis=0, tiled=True)
 
-    before = lax.ppermute(band_qkv[1:], "seq", [(i, i + 1) for i in range(size - 1)])
+    core = me % CORES
+    previous = jnp.where(me > 0, row_doc[jnp.maximum(me - 1, 0)], -1)
+    joined = jnp.stack([(previous == row_doc[me]).astype(jnp.int32), core])
+    band_out = band_heads(joined, band_qkv, twin, keys, values)
+    near = near_parts(band_out)
 
     groups = [
         [(z * MID + m) * CORES + c for z in range(outer) for c in range(CORES)] for m in range(MID)
     ]
     turned = jnp.transpose(out_weight, (0, 2, 1))
-    weights = [
-        lax.all_gather(turned[i], "seq", axis=0, tiled=True, axis_index_groups=groups)
-        for i in range(2)
-    ]
-
-    previous = jnp.where(me > 0, row_doc[jnp.maximum(me - 1, 0)], -1)
-    joined = (previous == row_doc[me]).astype(jnp.int32).reshape(1)
-    band_out = band_heads(joined, band_qkv, before)
-    band_parts = spread(band_out)
+    if share % 192 == 0:
+        small = share // 3
+        turned = jnp.where(core == 1, jnp.roll(turned, -small, axis=1), turned)
+        pieces = [turned[:, : share - small], turned[:, share - small :]]
+    else:
+        pieces = [turned]
+    gathered, pieces = lax.optimization_barrier((gathered, pieces))
+    weights = []
+    for piece in pieces:
+        part = lax.all_gather(piece, "seq", axis=0, axis_index_groups=groups)
+        weights.append(part.reshape(outer, CORES, *piece.shape))
 
     column_out = stride_heads(row_doc, gathered)
     stride_out = lax.all_to_all(column_out, "seq", split_axis=0, concat_axis=0, tiled=True)
-    stride_parts = spread(stride_out.reshape(tokens, width))
-
-    sent = []
-    for step in (3, 1, 2, 0):
-        terms = scores_of(band_parts[step], weights[0]) + scores_of(stride_parts[step], weights[1])
-        block = terms.astype(jnp.bfloat16)
-        sent.append((step, moved(block, step) if step else block))
-    by_step = dict(sent)
-
+    near, column_out = lax.optimization_barrier((near, column_out))
+    band_parts = (band_out, *near, *far_parts(*near))
+    stride_out, band_parts = lax.optimization_barrier((stride_out, band_parts))
+    stride_out = stride_out.reshape(tokens, width)
+    near = near_parts(stride_out)
+    stride_parts = (stride_out, *near, *far_parts(*near))
+
+    chunks = []
+    for index, weight in enumerate(weights):
+        if index:
+            chunks.append(sent_back(blocks))
+            weight, _ = lax.optimization_barrier((weight, blocks))
+        blocks = project(band_parts, stride_parts, weight)
+    chunks.append(sent_back(blocks))
     mine = (me // CORES) % MID
-    stacked = jnp.stack([by_step[step] for step in range(MID)])
-    picked = [lax.dynamic_index_in_dim(stacked, mine ^ m, 0, keepdims=False) for m in range(MID)]
-    span = CORES * share
-    pieces = []
-    for z in range(outer):
-        for m in range(MID):
-            pieces.append(picked[m][:, z * span : (z + 1) * span])
-    result = jnp.concatenate(pieces, axis=1)
+    result = assemble(mine, chunks, outer)
     return lax.psum_scatter(result, "tp", scatter_dimension=1, tiled=True)
 
 

time: 484 us -> 444 us (0.917)
  the two profiles are of different devices: /device:TPU:31 before, /device:TPU:16 now
where the time goes in v2:
time: 444 us; the launch traced here: 443 us
  waiting for transfers between devices  302 us (68%)
  Pallas kernels  67.4 us (15%)
  starting transfers between devices  30.2 us (7%)
  local copies, waits for them, and re-layouts  26 us (6%)
  between operations  14.9 us (3%)
    ppermute x14, waiting for transfers between devices, moved(): lax.ppermute(array, 'seq', [(i, i ^ step * CORES) for i in range(size)])  114 us
    all_to_all x1, waiting for transfers between devices, per_device(): lax.all_to_all(grid, 'seq', split_axis=0, concat_axis=0, tiled=True)  93.6 us
    ppermute x1, waiting for transfers between devices, per_device(): keys = lax.ppermute(band_qkv[1], 'seq', [(i, i + 1) for i in last])  74 us
    pallas_call x2, Pallas kernels, project(): pl.pallas_call(project_kernel, out_shape=[jax.ShapeDtypeStruct((tokens, c...  38 us
    ppermute x1, waiting for transfers between devices, per_device(): values = lax.ppermute(twin[1], 'seq', [(i - 1, i + 1) for i in last])  17.9 us
    pallas_call x1, Pallas kernels, band_heads(): pl.pallas_call(functools.partial(band_kernel, heads), out_shape=jax.Shape...  14.5 us
    ppermute x14, starting transfers between devices, moved(): lax.ppermute(array, 'seq', [(i, i ^ step * CORES) for i in range(size)])  12.4 us
    pallas_call x1, Pallas kernels, stride_heads(): pl.pallas_call(functools.partial(stride_kernel, heads, cols), out_shape=j...  10.5 us
  transfers between devices with their start and end apart: 21, of which 13 were waited for; matrix products, arithmetic and copies ran while one was open for 4% of the time, Pallas kernels for 11%

profile of v2, /device:TPU:16, one launch (start us, length us, event | category | flops | bytes accessed | tf_op | source)
XLA Modules:
  0.0 443.0 jit_solution(17378072291619745410)
XLA Ops:
  6.5 4.8 %copy_bitcast_fusion = bf16[32,3,8,3072]{3,2,1,0:T(8,128)(2,1)} fusion(bf16[3,256,3072]{2,1,0:T(8,128)(2,1)} %param.5), kind=kLoop, calls=%fused_computation | loop fusion | bytes 9437184 | tf_op jit(solution)/shard_map/transpose | solution.py:274
  11.3 6.0 %all-to-all-start = ((bf16[32,3,8,3072]{3,2,1,0:T(8,128)(2,1)}), bf16[32,3,8,3072]{3,2,1,0:T(8,128)(2,1)}, u32[]{:S(2)}, u32[]{:S(2)}) async-start(bf16[32,3,8,3072]{3,2,1,0:T(8,128)(2,1)} %copy_bitcast_fusion), calls=%async_computation | async-start | bytes 9437184 | tf_op jit(solution)/shard_map/all_to_all | solution.py:275
  17.4 1.2 slice.46
  18.7 2.2 maximum_select_fusion
  21.0 1.4 copy-done.1
  22.4 1.3 slice.48
  23.7 2.1 slice.49
  25.8 93.6 %all-to-all-done.qkv_ref = bf16[32,3,8,3072]{3,2,1,0:T(8,128)(2,1)} async-done(((bf16[32,3,8,3072]{3,2,1,0:T(8,128)(2,1)}), bf16[32,3,8,3072]{3,2,1,0:T(8,128)(2,1)}, u32[]{:S(2)}, u32[]{:S(2)}) %all-to-all-start) | async-done | bytes 4718624 | tf_op jit(solution)/shard_map/all_to_all | solution.py:275
  119.4 3.8 slice.39
  123.2 2.7 slice_bitcast_fusion.1
  125.9 1.4 collective-permute-start.1
  127.3 1.8 collective-permute-done.twin_ref
  129.0 1.3 slice_bitcast_fusion
  130.4 3.2 collective-permute-start.2
  133.7 0.7 broadcast_in_dim_reshape.8.doc_row_ref
  134.4 0.7 broadcast_in_dim_reshape.7.doc_col_ref
  135.1 10.5 %strided.1 = bf16[32,8,3072]{2,1,0:T(8,128)(2,1)} custom-call(s32[256,1]{1,0:T(8,128)} %broadcast_in_dim_reshape.8.doc_row_ref, s32[1,256]{1,0:T(1,128)} %broadcast_in_dim_reshape.7.doc_col_ref, bf16[32,3,8,3072]{3,2,1,0:T(8,128)(2,1)} %all-to-all-done.qkv_ref), custom_call_target="tpu_custom_call" | custom-call | flops 805306368 | bytes 6291456 | tf_op jit(solution)/shard_map/strided/pallas_call | solution.py:115
  145.6 7.1 %all-to-all-start.1 = ((bf16[32,8,3072]{2,1,0:T(8,128)(2,1)}), bf16[32,8,3072]{2,1,0:T(8,128)(2,1)S(1)}, u32[]{:S(2)}, u32[]{:S(2)}) async-start(bf16[32,8,3072]{2,1,0:T(8,128)(2,1)} %strided.1), calls=%async_computation.1 | async-start | bytes 3145728 | tf_op jit(solution)/shard_map/all_to_all | solution.py:300
  152.8 0.6 fusion
  154.6 0.6 pad_add_fusion.joined_ref
  155.2 74.0 %collective-permute-done.1.keys_ref = bf16[256,3072]{1,0:T(8,128)(2,1)} collective-permute-done((bf16[256,3072]{1,0:T(8,128)(2,1)}, bf16[256,3072]{1,0:T(8,128)(2,1)}, u32[]{:S(2)}, u32[]{:S(2)}) %collective-permute-start.1) | collective-permute-done | bytes 1572896 | tf_op jit(solution)/shard_map/ppermute | solution.py:272
  229.2 17.9 %collective-permute-done.2.values_ref = bf16[256,3072]{1,0:T(8,128)(2,1)} collective-permute-done((bf16[256,3072]{1,0:T(8,128)(2,1)}, bf16[256,3072]{1,0:T(8,128)(2,1)}, u32[]{:S(2)}, u32[]{:S(2)}) %collective-permute-start.2) | collective-permute-done | bytes 1572896 | tf_op jit(solution)/shard_map/ppermute | solution.py:273
  247.1 14.5 %band.1.refs_0_ = bf16[256,3072]{1,0:T(8,128)(2,1)} custom-call(s32[2]{0:T(128)} %pad_add_fusion.joined_ref, bf16[3,256,3072]{2,1,0:T(8,128)(2,1)} %own_ref.1, bf16[2,256,3072]{2,1,0:T(8,128)(2,1)} %copy-done.2, bf16[256,3072]{1,0:T(8,128)(2,1)} %collective-permute-done.1.keys_ref, bf16[256,3072]{1,0:T(8,128)(2,1)} %collective-permute-done.2.values_ref), custom_call_target="tpu_custom_call" | custom-call | flops 1610612736 | bytes 9437184 | tf_op jit(solution)/shard_map/band/pallas_call | solution.py:56
  261.6 3.7 collective-permute-start.4
  265.4 19.6 %collective-permute-done.3.refs_1_ = bf16[256,3072]{1,0:T(8,128)(2,1)S(1)} collective-permute-done((bf16[256,3072]{1,0:T(8,128)(2,1)}, bf16[256,3072]{1,0:T(8,128)(2,1)S(1)}, u32[]{:S(2)}, u32[]{:S(2)}) %collective-permute-start.3) | collective-permute-done | bytes 1572896 | tf_op jit(solution)/shard_map/ppermute | solution.py:137
  284.9 12.6 %collective-permute-done.4.refs_2_ = bf16[256,3072]{1,0:T(8,128)(2,1)S(1)} collective-permute-done((bf16[256,3072]{1,0:T(8,128)(2,1)}, bf16[256,3072]{1,0:T(8,128)(2,1)S(1)}, u32[]{:S(2)}, u32[]{:S(2)}) %collective-permute-start.4) | collective-permute-done | bytes 1572896 | tf_op jit(solution)/shard_map/ppermute | solution.py:137
  297.6 1.7 collective-permute-start.5
  299.4 17.5 %collective-permute-done.5.refs_3_ = bf16[128,3072]{1,0:T(8,128)(2,1)S(1)} collective-permute-done((bf16[128,3072]{1,0:T(8,128)(2,1)S(1)}, bf16[128,3072]{1,0:T(8,128)(2,1)S(1)}, u32[]{:S(2)}, u32[]{:S(2)}) %collective-permute-start.5) | collective-permute-done | bytes 786464 | tf_op jit(solution)/shard_map/ppermute | solution.py:137
  316.9 0.9 copy-done.15
  317.8 2.1 collective-permute-done.6.refs_4_
  319.9 1.7 collective-permute-start.8
  321.6 31.6 %collective-permute-done.7.refs_6_ = bf16[256,3072]{1,0:T(8,128)(2,1)S(1)} collective-permute-done((bf16[256,3072]{1,0:T(8,128)(2,1)S(1)}, bf16[256,3072]{1,0:T(8,128)(2,1)S(1)}, u32[]{:S(2)}, u32[]{:S(2)}) %collective-permute-start.7) | collective-permute-done | bytes 1572896 | tf_op jit(solution)/shard_map/ppermute | solution.py:137
  353.3 1.0 copy-done.9
  354.5 10.8 %collective-permute-done.9.refs_8_ = bf16[128,3072]{1,0:T(8,128)(2,1)S(1)} collective-permute-done((bf16[128,3072]{1,0:T(8,128)(2,1)S(1)}, bf16[128,3072]{1,0:T(8,128)(2,1)S(1)}, u32[]{:S(2)}, u32[]{:S(2)}) %collective-permute-start.9) | collective-permute-done | bytes 786464 | tf_op jit(solution)/shard_map/ppermute | solution.py:137
  365.3 0.9 copy-done.16
  366.2 0.3 collective-permute-done.10.refs_9_
  366.5 0.9 copy-done.17
  367.4 22.9 %project.2 = (bf16[256,1024]{1,0:T(8,128)(2,1)}, bf16[256,1024]{1,0:T(8,128)(2,1)}, bf16[256,1024]{1,0:T(8,128)(2,1)}, bf16[256,1024]{1,0:T(8,128)(2,1)}) custom-call(bf16[256,3072]{1,0:T(8,128)(2,1)} %band.1.refs_0_, bf16[256,3072]{1,0:T(8,128)(2,1)} %copy-done.7, bf16[256,3072]{1,0:T(8,128)(2,1)} %copy-done.8, bf16[128,3072]{1,0:T(8,128)(2,1)} %copy-done.15, ...), custom_call_target="tpu_custom_call" | custom-call | flops 12884901888 | bytes 27262976 | tf_op jit(solution)/shard_map/project/pallas_call | solution.py:204
  390.3 15.1 %project.3 = (bf16[256,512]{1,0:T(8,128)(2,1)}, bf16[256,512]{1,0:T(8,128)(2,1)}, bf16[256,512]{1,0:T(8,128)(2,1)}, bf16[256,512]{1,0:T(8,128)(2,1)}) custom-call(bf16[256,3072]{1,0:T(8,128)(2,1)} %band.1.refs_0_, bf16[256,3072]{1,0:T(8,128)(2,1)} %copy-done.7, bf16[256,3072]{1,0:T(8,128)(2,1)} %copy-done.8, bf16[128,3072]{1,0:T(8,128)(2,1)} %copy-done.15, ...), custom_call_target="tpu_custom_call" | custom-call | flops 6442450944 | bytes 19922944 | tf_op jit(solution)/shard_map/project/pallas_call | solution.py:204
  405.5 2.0 collective-permute-start.11
  407.5 1.0 collective-permute-start.12
  408.5 0.5 collective-permute-start.13
  409.1 1.0 collective-permute-start.15
  410.1 4.8 %collective-permute-done.14.refs_5_ = bf16[256,512]{1,0:T(8,128)(2,1)S(1)} collective-permute-done((bf16[256,512]{1,0:T(8,128)(2,1)}, bf16[256,512]{1,0:T(8,128)(2,1)S(1)}, u32[]{:S(2)}, u32[]{:S(2)}) %collective-permute-start.14) | collective-permute-done | bytes 262176 | tf_op jit(solution)/shard_map/ppermute | solution.py:137
  414.9 0.4 collective-permute-start.16
  415.3 15.2 %collective-permute-done.15.refs_6_ = bf16[256,512]{1,0:T(8,128)(2,1)S(1)} collective-permute-done((bf16[256,512]{1,0:T(8,128)(2,1)}, bf16[256,512]{1,0:T(8,128)(2,1)S(1)}, u32[]{:S(2)}, u32[]{:S(2)}) %collective-permute-start.15) | collective-permute-done | bytes 262176 | tf_op jit(solution)/shard_map/ppermute | solution.py:137
  430.6 0.7 copy-done.12
  431.9 4.3 assemble.1
  (59 shorter events, 1.5 us)
Async XLA Ops:
  11.3 6.0 %copy-start = (bf16[2,3072,192]{1,2,0:T(8,128)(2,1)S(1)}, bf16[2,3072,192]{1,2,0:T(8,128)(2,1)}, u32[]{:S(2)}) copy-start(bf16[2,3072,192]{1,2,0:T(8,128)(2,1)} %param.6) | copy-start | bytes 7077892
  11.3 108.0 %all-to-all-start = ((bf16[32,3,8,3072]{3,2,1,0:T(8,128)(2,1)}), bf16[32,3,8,3072]{3,2,1,0:T(8,128)(2,1)}, u32[]{:S(2)}, u32[]{:S(2)}) async-start(bf16[32,3,8,3072]{3,2,1,0:T(8,128)(2,1)} %copy_bitcast_fusion), calls=%async_computation | async-start | bytes 9437184 | tf_op jit(solution)/shard_map/all_to_all | solution.py:275
  17.3 349.2 %all-gather.5.cloned.1.call-start = ((), (), s32[]{:S(2)}) async-start(), calls=%async_computation.2 | async-start | bytes 14155776 | tf_op jit(solution)/shard_map/all_gather | solution.py:296
  21.0 1.4 copy-start.1
  119.4 270.9 %all-gather.7.cloned.1.call-start = ((), (), s32[]{:S(2)}) async-start(), calls=%async_computation.3 | async-start | bytes 7077888 | tf_op jit(solution)/shard_map/all_gather | solution.py:296
  123.2 5.9 %collective-permute-start = (bf16[2,256,3072]{2,1,0:T(8,128)(2,1)}, bf16[2,256,3072]{2,1,0:T(8,128)(2,1)S(1)}, u32[]{:S(2)}, u32[]{:S(2)}) collective-permute-start(bf16[2,256,3072]{2,1,0:T(8,128)(2,1)} %slice.39), channel_id=1, source_target_pairs={{0,1},{1,0},{2,3},{3,2},{4,5},{5,4},{6,7},{7,6},{8,9},{9,8},{10,11... | collective-permute-start | bytes 9437192 | tf_op jit(solution)/shard_map/ppermute | solution.py:270
  125.9 7.7 %copy-start.14 = (s32[32]{0:T(128)S(1)}, s32[32]{0:T(128)}, u32[]{:S(2)}) copy-start(s32[32]{0:T(128)} %param.7) | copy-start | bytes 388
  125.9 103.3 %collective-permute-start.1 = (bf16[256,3072]{1,0:T(8,128)(2,1)}, bf16[256,3072]{1,0:T(8,128)(2,1)}, u32[]{:S(2)}, u32[]{:S(2)}) collective-permute-start(bf16[256,3072]{1,0:T(8,128)(2,1)} %slice_bitcast_fusion.1), channel_id=1, source_target_pairs={{1,2},{3,4},{5,6},{7,8},{9,10},{11,12},{13,14},{15,16},{17,18},{19... | collective-permute-start | bytes 4718600 | tf_op jit(solution)/shard_map/ppermute | solution.py:272
  129.0 16.6 %copy-start.2 = (bf16[2,256,3072]{2,1,0:T(8,128)(2,1)}, bf16[2,256,3072]{2,1,0:T(8,128)(2,1)S(1)}, u32[]{:S(2)}) copy-start(bf16[2,256,3072]{2,1,0:T(8,128)(2,1)S(1)} %collective-permute-done.twin_ref) | copy-start | bytes 9437188
  130.4 116.7 %collective-permute-start.2 = (bf16[256,3072]{1,0:T(8,128)(2,1)}, bf16[256,3072]{1,0:T(8,128)(2,1)}, u32[]{:S(2)}, u32[]{:S(2)}) collective-permute-start(bf16[256,3072]{1,0:T(8,128)(2,1)} %slice_bitcast_fusion), channel_id=1, source_target_pairs={{0,2},{2,4},{4,6},{6,8},{8,10},{10,12},{12,14},{14,16},{16,18},{18... | collective-permute-start | bytes 4718600 | tf_op jit(solution)/shard_map/ppermute | solution.py:273
  145.6 174.3 %all-to-all-start.1 = ((bf16[32,8,3072]{2,1,0:T(8,128)(2,1)}), bf16[32,8,3072]{2,1,0:T(8,128)(2,1)S(1)}, u32[]{:S(2)}, u32[]{:S(2)}) async-start(bf16[32,8,3072]{2,1,0:T(8,128)(2,1)} %strided.1), calls=%async_computation.1 | async-start | bytes 3145728 | tf_op jit(solution)/shard_map/all_to_all | solution.py:300
  261.6 23.3 %collective-permute-start.3 = (bf16[256,3072]{1,0:T(8,128)(2,1)}, bf16[256,3072]{1,0:T(8,128)(2,1)S(1)}, u32[]{:S(2)}, u32[]{:S(2)}) collective-permute-start(bf16[256,3072]{1,0:T(8,128)(2,1)} %band.1.refs_0_), channel_id=1, source_target_pairs={{0,2},{1,3},{2,0},{3,1},{4,6},{5,7},{6,4},{7,5},{8,10},{9,11},{10,... | collective-permute-start | bytes 4718600 | tf_op jit(solution)/shard_map/ppermute | solution.py:137
  261.6 35.9 %collective-permute-start.4 = (bf16[256,3072]{1,0:T(8,128)(2,1)}, bf16[256,3072]{1,0:T(8,128)(2,1)S(1)}, u32[]{:S(2)}, u32[]{:S(2)}) collective-permute-start(bf16[256,3072]{1,0:T(8,128)(2,1)} %band.1.refs_0_), channel_id=1, source_target_pairs={{0,4},{1,5},{2,6},{3,7},{4,0},{5,1},{6,2},{7,3},{8,12},{9,13},{10,... | collective-permute-start | bytes 4718600 | tf_op jit(solution)/shard_map/ppermute | solution.py:137
  284.9 68.4 %copy-start.7 = (bf16[256,3072]{1,0:T(8,128)(2,1)}, bf16[256,3072]{1,0:T(8,128)(2,1)S(1)}, u32[]{:S(2)}) copy-start(bf16[256,3072]{1,0:T(8,128)(2,1)S(1)} %collective-permute-done.3.refs_1_) | copy-start | bytes 4718596
  297.5 19.4 %copy-start.8 = (bf16[256,3072]{1,0:T(8,128)(2,1)}, bf16[256,3072]{1,0:T(8,128)(2,1)S(1)}, u32[]{:S(2)}) copy-start(bf16[256,3072]{1,0:T(8,128)(2,1)S(1)} %collective-permute-done.4.refs_2_) | copy-start | bytes 4718596
  297.6 19.3 %collective-permute-start.5 = (bf16[128,3072]{1,0:T(8,128)(2,1)S(1)}, bf16[128,3072]{1,0:T(8,128)(2,1)S(1)}, u32[]{:S(2)}, u32[]{:S(2)}) collective-permute-start(bf16[128,3072]{1,0:T(8,128)(2,1)S(1)} %slice.42), channel_id=1, source_target_pairs={{0,4},{1,5},{2,6},{3,7},{4,0},{5,1},{6,2},{7,3},{8,12},{9,13},{10,... | collective-permute-start | bytes 2359304 | tf_op jit(solution)/shard_map/ppermute | solution.py:137
  299.3 20.6 %collective-permute-start.6 = (bf16[128,3072]{1,0:T(8,128)(2,1)S(1)}, bf16[128,3072]{1,0:T(8,128)(2,1)}, u32[]{:S(2)}, u32[]{:S(2)}) collective-permute-start(bf16[128,3072]{1,0:T(8,128)(2,1)S(1)} %slice.43), channel_id=1, source_target_pairs={{0,2},{1,3},{2,0},{3,1},{4,6},{5,7},{6,4},{7,5},{8,10},{9,11},{10,... | collective-permute-start | bytes 2359304 | tf_op jit(solution)/shard_map/ppermute | solution.py:137
  316.9 0.9 copy-start.15
  319.9 46.6 %copy-start.3 = (bf16[32,8,3072]{2,1,0:T(8,128)(2,1)}, bf16[32,8,3072]{2,1,0:T(8,128)(2,1)S(1)}, u32[]{:S(2)}) copy-start(bf16[32,8,3072]{2,1,0:T(8,128)(2,1)S(1)} %all-to-all-done.1) | copy-start | bytes 4718596
  319.9 33.3 %collective-permute-start.7 = (bf16[256,3072]{1,0:T(8,128)(2,1)S(1)}, bf16[256,3072]{1,0:T(8,128)(2,1)S(1)}, u32[]{:S(2)}, u32[]{:S(2)}) collective-permute-start(bf16[256,3072]{1,0:T(8,128)(2,1)S(1)} %bitcast.21), channel_id=1, source_target_pairs={{0,2},{1,3},{2,0},{3,1},{4,6},{5,7},{6,4},{7,5},{8,10},{9,11},{10,... | collective-permute-start | bytes 4718600 | tf_op jit(solution)/shard_map/ppermute | solution.py:137
  319.9 34.4 %collective-permute-start.8 = (bf16[256,3072]{1,0:T(8,128)(2,1)S(1)}, bf16[256,3072]{1,0:T(8,128)(2,1)S(1)}, u32[]{:S(2)}, u32[]{:S(2)}) collective-permute-start(bf16[256,3072]{1,0:T(8,128)(2,1)S(1)} %bitcast.22), channel_id=1, source_target_pairs={{0,4},{1,5},{2,6},{3,7},{4,0},{5,1},{6,2},{7,3},{8,12},{9,13},{10,... | collective-permute-start | bytes 4718600 | tf_op jit(solution)/shard_map/ppermute | solution.py:137
  353.2 1.2 copy-start.9
  353.3 12.1 %collective-permute-start.9 = (bf16[128,3072]{1,0:T(8,128)(2,1)S(1)}, bf16[128,3072]{1,0:T(8,128)(2,1)S(1)}, u32[]{:S(2)}, u32[]{:S(2)}) collective-permute-start(bf16[128,3072]{1,0:T(8,128)(2,1)S(1)} %slice.51), channel_id=1, source_target_pairs={{0,4},{1,5},{2,6},{3,7},{4,0},{5,1},{6,2},{7,3},{8,12},{9,13},{10,... | collective-permute-start | bytes 2359304 | tf_op jit(solution)/shard_map/ppermute | solution.py:137
  354.4 11.0 %copy-start.10 = (bf16[256,3072]{1,0:T(8,128)(2,1)}, bf16[256,3072]{1,0:T(8,128)(2,1)S(1)}, u32[]{:S(2)}) copy-start(bf16[256,3072]{1,0:T(8,128)(2,1)S(1)} %collective-permute-done.8.refs_7_) | copy-start | bytes 4718596
  354.4 12.1 %collective-permute-start.10 = (bf16[128,3072]{1,0:T(8,128)(2,1)S(1)}, bf16[128,3072]{1,0:T(8,128)(2,1)S(1)}, u32[]{:S(2)}, u32[]{:S(2)}) collective-permute-start(bf16[128,3072]{1,0:T(8,128)(2,1)S(1)} %slice.52), channel_id=1, source_target_pairs={{0,2},{1,3},{2,0},{3,1},{4,6},{5,7},{6,4},{7,5},{8,10},{9,11},{10,... | collective-permute-start | bytes 2359304 | tf_op jit(solution)/shard_map/ppermute | solution.py:137
  365.3 0.9 copy-start.16
  366.5 0.9 copy-start.17
  390.3 17.2 %copy-start.19 = (bf16[256,1024]{1,0:T(8,128)(2,1)S(1)}, bf16[256,1024]{1,0:T(8,128)(2,1)}, u32[]{:S(2)}) copy-start(bf16[256,1024]{1,0:T(8,128)(2,1)} %get-tuple-element.37) | copy-start | bytes 1572868
  390.3 18.2 %copy-start.18 = (bf16[256,1024]{1,0:T(8,128)(2,1)S(1)}, bf16[256,1024]{1,0:T(8,128)(2,1)}, u32[]{:S(2)}) copy-start(bf16[256,1024]{1,0:T(8,128)(2,1)} %get-tuple-element.38) | copy-start | bytes 1572868
  405.4 9.5 %collective-permute-start.14 = (bf16[256,512]{1,0:T(8,128)(2,1)}, bf16[256,512]{1,0:T(8,128)(2,1)S(1)}, u32[]{:S(2)}, u32[]{:S(2)}) collective-permute-start(bf16[256,512]{1,0:T(8,128)(2,1)} %get-tuple-element.42), channel_id=1, source_target_pairs={{0,2},{1,3},{2,0},{3,1},{4,6},{5,7},{6,4},{7,5},{8,10},{9,11},{10,... | collective-permute-start | bytes 786440 | tf_op jit(solution)/shard_map/ppermute | solution.py:137
  405.5 25.0 %collective-permute-start.11 = (bf16[256,1024]{1,0:T(8,128)(2,1)}, bf16[256,1024]{1,0:T(8,128)(2,1)S(1)}, u32[]{:S(2)}, u32[]{:S(2)}) collective-permute-start(bf16[256,1024]{1,0:T(8,128)(2,1)} %get-tuple-element.36), channel_id=1, source_target_pairs={{0,2},{1,3},{2,0},{3,1},{4,6},{5,7},{6,4},{7,5},{8,10},{9,11},{10,... | collective-permute-start | bytes 1572872 | tf_op jit(solution)/shard_map/ppermute | solution.py:137
  407.5 23.0 %collective-permute-start.12 = (bf16[256,1024]{1,0:T(8,128)(2,1)S(1)}, bf16[256,1024]{1,0:T(8,128)(2,1)S(1)}, u32[]{:S(2)}, u32[]{:S(2)}) collective-permute-start(bf16[256,1024]{1,0:T(8,128)(2,1)S(1)} %copy-done.19), channel_id=1, source_target_pairs={{0,4},{1,5},{2,6},{3,7},{4,0},{5,1},{6,2},{7,3},{8,12},{9,13},{10,... | collective-permute-start | bytes 1572872 | tf_op jit(solution)/shard_map/ppermute | solution.py:137
  408.5 22.0 %collective-permute-start.13 = (bf16[256,1024]{1,0:T(8,128)(2,1)S(1)}, bf16[256,1024]{1,0:T(8,128)(2,1)S(1)}, u32[]{:S(2)}, u32[]{:S(2)}) collective-permute-start(bf16[256,1024]{1,0:T(8,128)(2,1)S(1)} %copy-done.18), channel_id=1, source_target_pairs={{0,6},{1,7},{2,4},{3,5},{4,2},{5,3},{6,0},{7,1},{8,14},{9,15},{10,... | collective-permute-start | bytes 1572872 | tf_op jit(solution)/shard_map/ppermute | solution.py:137
  409.1 21.5 %collective-permute-start.15 = (bf16[256,512]{1,0:T(8,128)(2,1)}, bf16[256,512]{1,0:T(8,128)(2,1)S(1)}, u32[]{:S(2)}, u32[]{:S(2)}) collective-permute-start(bf16[256,512]{1,0:T(8,128)(2,1)} %get-tuple-element.43), channel_id=1, source_target_pairs={{0,4},{1,5},{2,6},{3,7},{4,0},{5,1},{6,2},{7,3},{8,12},{9,13},{10,... | collective-permute-start | bytes 786440 | tf_op jit(solution)/shard_map/ppermute | solution.py:137
  414.9 15.7 %copy-start.11 = (bf16[256,512]{1,0:T(8,128)(2,1)}, bf16[256,512]{1,0:T(8,128)(2,1)S(1)}, u32[]{:S(2)}) copy-start(bf16[256,512]{1,0:T(8,128)(2,1)S(1)} %collective-permute-done.14.refs_5_) | copy-start | bytes 786436
  414.9 15.6 %collective-permute-start.16 = (bf16[256,512]{1,0:T(8,128)(2,1)}, bf16[256,512]{1,0:T(8,128)(2,1)S(1)}, u32[]{:S(2)}, u32[]{:S(2)}) collective-permute-start(bf16[256,512]{1,0:T(8,128)(2,1)} %get-tuple-element.44), channel_id=1, source_target_pairs={{0,6},{1,7},{2,4},{3,5},{4,2},{5,3},{6,0},{7,1},{8,14},{9,15},{10,... | collective-permute-start | bytes 786440 | tf_op jit(solution)/shard_map/ppermute | solution.py:137
  430.5 0.7 copy-start.12
  430.5 0.8 copy-start.13
  430.5 1.0 copy-start.4
  430.6 1.2 copy-start.5
  430.6 1.3 copy-start.6
Sparse Core Ops, SparseCore 0:
  119.5 147.8 all-gather.4
  269.0 97.8 all-gather.6

commit v3 on v2

--- a/solution.py
+++ b/solution.py
@@ -221,6 +221,108 @@
     )(*band_parts, *stride_parts, weight)
 
 
+def slots_kernel(low, rows, place_ref, *refs):
+    count = MID + 1
+    parts = (refs[:count], refs[count : 2 * count])
+    slots = refs[2 * count : 2 * count + 6]
+    out_refs = refs[2 * count + len(slots) : 2 * count + len(slots) + MID]
+    held_ref, weight_ref, sems, slot_sems = refs[-4:]
+    tokens = out_refs[0].shape[0]
+    depth = held_ref.shape[2]
+    outer = weight_ref.shape[1]
+    block = CORES * rows
+    group = max(1, 512 // block)
+    step = pl.program_id(0)
+    line, core = place_ref[0], place_ref[1]
+
+    def copies(which):
+        place = 0
+        for index, source in enumerate(parts[which]):
+            size = source.shape[0]
+            target = held_ref.at[which, pl.ds(place, size)]
+            yield pltpu.make_async_copy(source, target, sems.at[which, index])
+            place += size
+
+    def arrival(source, slot, role):
+        side = core if role == 0 else 1 - core
+        return pltpu.make_async_copy(source, weight_ref.at[:, slot, side], slot_sems.at[slot, role])
+
+    def source_of(slot, role):
+        first, middle, ends = slots[role], slots[2 + role], slots[4 + role]
+        if slot == 0:
+            return first.at[:, pl.ds(low, rows)]
+        if slot == 2:
+            return middle.at[:, pl.ds(low, rows)]
+        return ends.at[slot // 2]
+
+    @pl.when(step == 0)
+    def _():
+        for copy in copies(0):
+            copy.start()
+        for slot in range(group):
+            for role in range(CORES):
+                arrival(source_of(slot, role), slot, role).start()
+        for copy in copies(1):
+            copy.start()
+        for slot in range(group, outer):
+            for role in range(CORES):
+                arrival(source_of(slot, role), slot, role).start()
+
+    for index in range(group):
+        for role in range(CORES):
+            arrival(slots[role].at[:, pl.ds(low, rows)], step * group + index, role).wait()
+
+    @pl.when(step == 0)
+    def _():
+        for which in range(2):
+            for copy in copies(which):
+                copy.wait()
+
+    for half in range(2):
+        span = MID * tokens // 2
+        terms = None
+        for which in range(2):
+            weight = weight_ref[which, pl.ds(step * group, group)].reshape(group * block, depth)
+            found = scores_of(held_ref[which, half * span : (half + 1) * span], weight)
+            terms = found if terms is None else terms + found
+        for index in range(group):
+            slot = step * group + index
+            column = pl.multiple_of(lax.rem(line - slot + outer, outer) * block, 128)
+            for part in range(MID // 2):
+                piece = terms[part * tokens : (part + 1) * tokens, index * block : (index + 1) * block]
+                target = out_refs[half * MID // 2 + part]
+                target[:, pl.ds(column, block)] = piece.astype(jnp.bfloat16)
+
+
+def project_slots(place, band_parts, stride_parts, slots, low, rows, outer):
+    tokens, depth = band_parts[0].shape
+    block = CORES * rows
+    group = max(1, 512 // block)
+    columns = outer * block
+    return pl.pallas_call(
+        functools.partial(slots_kernel, low, rows),
+        out_shape=[jax.ShapeDtypeStruct((tokens, columns), jnp.bfloat16)] * MID,
+        grid_spec=pltpu.PrefetchScalarGridSpec(
+            num_scalar_prefetch=1,
+            grid=(outer // group,),
+            in_specs=[pl.BlockSpec(memory_space=pl.ANY)] * (2 * MID + 2 + len(slots)),
+            out_specs=[pl.BlockSpec((tokens, columns), lambda t, place: (0, 0))] * MID,
+            scratch_shapes=[
+                pltpu.VMEM((2, MID * tokens, depth), jnp.bfloat16),
+                pltpu.VMEM((2, outer, CORES, rows, depth), jnp.bfloat16),
+                pltpu.SemaphoreType.DMA((2, MID + 1)),
+                pltpu.SemaphoreType.DMA((outer, CORES)),
+            ],
+        ),
+        cost_estimate=pl.CostEstimate(
+            flops=4 * MID * tokens * depth * columns,
+            bytes_accessed=4 * (MID * tokens + columns) * depth + 2 * MID * tokens * columns,
+            transcendentals=0,
+        ),
+        name="project",
+    )(place, *band_parts, *stride_parts, *slots)
+
+
 def assemble_kernel(cuts, mine_ref, *refs):
     out_ref = refs[-1]
     span = sum(cut[1] for cut in cuts)
@@ -267,50 +369,102 @@
     cols = STRIDE // size
     share = out_weight.shape[2]
 
-    twin = lax.ppermute(band_qkv[1:], "seq", [(i, i ^ 1) for i in range(size)])
+    line = me // (MID * CORES)
+    core = me % CORES
+    relay = share % 192 == 0 and outer == 4
+    turned = jnp.transpose(out_weight, (0, 2, 1))
+    if share % 192 == 0:
+        small = share // 3
+        sizes = [share - small, small]
+        turned = jnp.where(core == 1, jnp.roll(turned, -small, axis=1), turned)
+    else:
+        sizes = [share]
+
+    def along(array, by):
+        plane = MID * CORES * by
+        return lax.ppermute(array, "seq", [(i, i + plane) for i in range(size) if 0 <= i + plane < size])
+
+    def twin_of(array):
+        return lax.ppermute(array, "seq", [(i, i ^ 1) for i in range(size)])
+
+    twin = twin_of(band_qkv[1:])
     last = range(CORES - 1, size - 1, CORES)
     keys = lax.ppermute(band_qkv[1], "seq", [(i, i + 1) for i in last])
     values = lax.ppermute(twin[1], "seq", [(i - 1, i + 1) for i in last])
     grid = jnp.transpose(stride_qkv.reshape(3, size, cols, width), (1, 0, 2, 3))
     gathered = lax.all_to_all(grid, "seq", split_axis=0, concat_axis=0, tiled=True)
 
-    core = me % CORES
+    if relay:
+        turned, gathered = lax.optimization_barrier((turned, gathered))
+        up, down = [along(turned, 1)], [along(turned, -1)]
+    column_out = stride_heads(row_doc, gathered)
+    stride_out = lax.all_to_all(column_out, "seq", split_axis=0, concat_axis=0, tiled=True)
+    keys, values, column_out = lax.optimization_barrier((keys, values, column_out))
     previous = jnp.where(me > 0, row_doc[jnp.maximum(me - 1, 0)], -1)
     joined = jnp.stack([(previous == row_doc[me]).astype(jnp.int32), core])
     band_out = band_heads(joined, band_qkv, twin, keys, values)
     near = near_parts(band_out)
-
-    groups = [
-        [(z * MID + m) * CORES + c for z in range(outer) for c in range(CORES)] for m in range(MID)
-    ]
-    turned = jnp.transpose(out_weight, (0, 2, 1))
-    if share % 192 == 0:
-        small = share // 3
-        turned = jnp.where(core == 1, jnp.roll(turned, -small, axis=1), turned)
-        pieces = [turned[:, : share - small], turned[:, share - small :]]
-    else:
-        pieces = [turned]
-    gathered, pieces = lax.optimization_barrier((gathered, pieces))
-    weights = []
-    for piece in pieces:
-        part = lax.all_gather(piece, "seq", axis=0, axis_index_groups=groups)
-        weights.append(part.reshape(outer, CORES, *piece.shape))
-
-    column_out = stride_heads(row_doc, gathered)
-    stride_out = lax.all_to_all(column_out, "seq", split_axis=0, concat_axis=0, tiled=True)
-    near, column_out = lax.optimization_barrier((near, column_out))
+    if relay:
+        up[0], down[0], _ = lax.optimization_barrier((up[0], down[0], band_out))
+        up.append(along(up[0], 1))
+        down.append(along(down[0], -1))
+        own_twin = twin_of(turned)
     band_parts = (band_out, *near, *far_parts(*near))
     stride_out, band_parts = lax.optimization_barrier((stride_out, band_parts))
     stride_out = stride_out.reshape(tokens, width)
+    if relay:
+        stride_out, own_twin = lax.optimization_barrier((stride_out, own_twin))
     near = near_parts(stride_out)
+    if relay:
+        up[1], down[1], _ = lax.optimization_barrier((up[1], down[1], stride_out))
+        ends = []
+        low = 0
+        for rows in sizes:
+            cut = slice(low, low + rows)
+            ends.append((along(up[1][:, cut], 1), along(down[1][:, cut], -1)))
+            low += rows
+        middle = jnp.where(line >= 2, up[1], down[1])
+        middle_twin = twin_of(middle)
+        near, middle_twin = lax.optimization_barrier((near, middle_twin))
     stride_parts = (stride_out, *near, *far_parts(*near))
 
+    if not relay:
+        groups = [
+            [(z * MID + m) * CORES + c for z in range(outer) for c in range(CORES)]
+            for m in range(MID)
+        ]
     chunks = []
-    for index, weight in enumerate(weights):
+    low = 0
+    place = jnp.stack([line, core])
+    for index, rows in enumerate(sizes):
+        cut = slice(low, low + rows)
+        if relay:
+            up_end, down_end = ends[index]
+            if index:
+                up_end, down_end, _ = lax.optimization_barrier((up_end, down_end, blocks))
+            edge = jnp.stack(
+                [
+                    jnp.where(line >= 1, up[0][:, cut], down_end),
+                    jnp.where(line >= 3, up_end, down[0][:, cut]),
+                ]
+            )
+            slots = [turned, own_twin, middle, middle_twin, edge, twin_of(edge)]
+        else:
+            part = lax.all_gather(turned[:, cut], "seq", axis=0, axis_index_groups=groups)
+            weight = part.reshape(outer, CORES, 2, rows, width)
         if index:
             chunks.append(sent_back(blocks))
-            weight, _ = lax.optimization_barrier((weight, blocks))
-        blocks = project(band_parts, stride_parts, weight)
+        if relay:
+            if index:
+                slots, _ = lax.optimization_barrier((slots, blocks))
+            blocks = project_slots(
+                place, band_parts, stride_parts, slots, low, rows, outer
+            )
+        else:
+            if index:
+                weight, _ = lax.optimization_barrier((weight, blocks))
+            blocks = project(band_parts, stride_parts, weight)
+        low += rows
     chunks.append(sent_back(blocks))
     mine = (me // CORES) % MID
     result = assemble(mine, chunks, outer)

time: 444 us -> 474 us (1.068)
  the two profiles are of different devices: /device:TPU:16 before, /device:TPU:31 now
where the time goes in v3:
time: 474 us; the launch traced here: 470 us
  waiting for transfers between devices  231 us (49%)
  starting transfers between devices  132 us (28%)
  Pallas kernels  67.5 us (14%)
  local copies, waits for them, and re-layouts  29 us (6%)
  other arithmetic  8.98 us (2%)
    all_to_all x1, waiting for transfers between devices, per_device(): lax.all_to_all(grid, 'seq', split_axis=0, concat_axis=0, tiled=True)  89.3 us
    ppermute x14, waiting for transfers between devices, moved(): lax.ppermute(array, 'seq', [(i, i ^ step * CORES) for i in range(size)])  81.1 us
    ppermute x8, waiting for transfers between devices, along(): lax.ppermute(array, 'seq', [(i, i + plane) for i in range(size) if 0 <= i...  60.2 us
    ppermute x5, starting transfers between devices, twin_of(): return lax.ppermute(array, 'seq', [(i, i ^ 1) for i in range(size)])  60.2 us
    ppermute x8, starting transfers between devices, along(): lax.ppermute(array, 'seq', [(i, i + plane) for i in range(size) if 0 <= i...  43.4 us
    pallas_call x2, Pallas kernels, project_slots(): pl.pallas_call(functools.partial(slots_kernel, low, rows), out_shape=[jax...  38 us
    pallas_call x1, Pallas kernels, band_heads(): pl.pallas_call(functools.partial(band_kernel, heads), out_shape=jax.Shape...  14.5 us
    all_to_all x1, starting transfers between devices, per_device(): lax.all_to_all(column_out, 'seq', split_axis=0, concat_axis=0, tiled=True)  10.9 us
  transfers between devices with their start and end apart: 31, of which 15 were waited for; matrix products, arithmetic and copies ran while one was open for 5% of the time, Pallas kernels for 13%

profile of v3, /device:TPU:31, one launch (start us, length us, event | category | flops | bytes accessed | tf_op | source)
XLA Modules:
  0.0 470.0 jit_solution(12484773891895706994)
XLA Ops:
  0.0 4.8 %copy_bitcast_fusion = bf16[32,3,8,3072]{3,2,1,0:T(8,128)(2,1)} fusion(bf16[3,256,3072]{2,1,0:T(8,128)(2,1)} %param.5), kind=kLoop, calls=%fused_computation | loop fusion | bytes 9437184 | tf_op jit(solution)/shard_map/transpose | solution.py:394
  4.8 6.2 %all-to-all-start = ((bf16[32,3,8,3072]{3,2,1,0:T(8,128)(2,1)}), bf16[32,3,8,3072]{3,2,1,0:T(8,128)(2,1)}, u32[]{:S(2)}, u32[]{:S(2)}) async-start(bf16[32,3,8,3072]{3,2,1,0:T(8,128)(2,1)} %copy_bitcast_fusion), calls=%async_computation | async-start | bytes 9437184 | tf_op jit(solution)/shard_map/all_to_all | solution.py:395
  11.0 3.8 slice.55
  15.2 2.9 slice_bitcast_fusion.1
  18.1 1.9 collective-permute-start.1
  20.0 1.3 slice.70
  21.3 3.7 maximum_select_fusion.refs_10_
  25.0 89.3 %all-to-all-done.qkv_ref = bf16[32,3,8,3072]{3,2,1,0:T(8,128)(2,1)} async-done(((bf16[32,3,8,3072]{3,2,1,0:T(8,128)(2,1)}), bf16[32,3,8,3072]{3,2,1,0:T(8,128)(2,1)}, u32[]{:S(2)}, u32[]{:S(2)}) %all-to-all-start) | async-done | bytes 4718624 | tf_op jit(solution)/shard_map/all_to_all | solution.py:395
  114.3 3.3 collective-permute-start.11
  117.7 1.3 collective-permute-start.10
  119.0 2.7 slice_bitcast_fusion
  121.6 1.8 collective-permute-start.2
  125.0 10.5 %strided.1 = bf16[32,8,3072]{2,1,0:T(8,128)(2,1)} custom-call(s32[256,1]{1,0:T(8,128)} %broadcast_in_dim_reshape.8.doc_row_ref, s32[1,256]{1,0:T(1,128)} %broadcast_in_dim_reshape.7.doc_col_ref, bf16[32,3,8,3072]{3,2,1,0:T(8,128)(2,1)} %all-to-all-done.qkv_ref), custom_call_target="tpu_custom_call" | custom-call | flops 805306368 | bytes 6291456 | tf_op jit(solution)/shard_map/strided/pallas_call | solution.py:115
  135.5 10.9 %all-to-all-start.1 = ((bf16[32,8,3072]{2,1,0:T(8,128)(2,1)}), bf16[32,8,3072]{2,1,0:T(8,128)(2,1)}, u32[]{:S(2)}, u32[]{:S(2)}) async-start(bf16[32,8,3072]{2,1,0:T(8,128)(2,1)} %strided.1), calls=%async_computation.1 | async-start | bytes 3145728 | tf_op jit(solution)/shard_map/all_to_all | solution.py:401
  148.9 14.5 %band.1.refs_0_ = bf16[256,3072]{1,0:T(8,128)(2,1)} custom-call(s32[2]{0:T(128)} %pad_add_fusion.1.joined_ref, bf16[3,256,3072]{2,1,0:T(8,128)(2,1)} %own_ref.1, bf16[2,256,3072]{2,1,0:T(8,128)(2,1)} %collective-permute-done.twin_ref, bf16[256,3072]{1,0:T(8,128)(2,1)} %collective-permute-done.1.keys_ref, bf16[256,3072]{1,0:T(8,128)(2,1)} %collective-permute-done.2.values_ref), custom_call_target="tpu_custom_call" | custom-call | flops 1610612736 | bytes 9437184 | tf_op jit(solution)/shard_map/band/pallas_call | solution.py:56
  164.0 54.8 %collective-permute-start.7 = (bf16[2,192,3072]{2,1,0:T(8,128)(2,1)}, bf16[2,192,3072]{2,1,0:T(8,128)(2,1)}, u32[]{:S(2)}, u32[]{:S(2)}) collective-permute-start(bf16[2,192,3072]{2,1,0:T(8,128)(2,1)} %maximum_select_fusion.refs_10_), channel_id=1, source_target_pairs={{0,1},{1,0},{2,3},{3,2},{4,5},{5,4},{6,7},{7,6},{8,9},{9,8},{10,11... | collective-permute-start | bytes 7077896 | tf_op jit(solution)/shard_map/ppermute | solution.py:388
  218.7 1.4 copy-done.8
  220.1 1.3 collective-permute-start.12
  221.4 27.4 %collective-permute-start.13 = (bf16[2,192,3072]{2,1,0:T(8,128)(2,1)}, bf16[2,192,3072]{2,1,0:T(8,128)(2,1)}, u32[]{:S(2)}, u32[]{:S(2)}) collective-permute-start(bf16[2,192,3072]{2,1,0:T(8,128)(2,1)} %copy-done.8), channel_id=1, source_target_pairs={{8,0},{9,1},{10,2},{11,3},{12,4},{13,5},{14,6},{15,7},{16,8},{17,9... | collective-permute-start | bytes 7077896 | tf_op jit(solution)/shard_map/ppermute | solution.py:385
  248.9 1.2 copy-done.3
  251.5 17.6 %collective-permute-done.6.refs_4_ = bf16[128,3072]{1,0:T(8,128)(2,1)S(1)} collective-permute-done((bf16[128,3072]{1,0:T(8,128)(2,1)S(1)}, bf16[128,3072]{1,0:T(8,128)(2,1)S(1)}, u32[]{:S(2)}, u32[]{:S(2)}) %collective-permute-start.6) | collective-permute-done | bytes 786464 | tf_op jit(solution)/shard_map/ppermute | solution.py:137
  269.1 1.3 collective-permute-done.5.refs_3_
  270.4 26.9 %collective-permute-done.12 = bf16[2,192,3072]{2,1,0:T(8,128)(2,1)S(1)} collective-permute-done((bf16[2,192,3072]{2,1,0:T(8,128)(2,1)}, bf16[2,192,3072]{2,1,0:T(8,128)(2,1)S(1)}, u32[]{:S(2)}, u32[]{:S(2)}) %collective-permute-start.12) | collective-permute-done | bytes 2359328 | tf_op jit(solution)/shard_map/ppermute | solution.py:385
  298.3 2.7 slice.63
  300.9 5.2 %collective-permute-start.17 = (bf16[2,128,3072]{2,1,0:T(8,128)(2,1)}, bf16[2,128,3072]{2,1,0:T(8,128)(2,1)}, u32[]{:S(2)}, u32[]{:S(2)}) collective-permute-start(bf16[2,128,3072]{2,1,0:T(8,128)(2,1)} %slice.63), channel_id=1, source_target_pairs={{8,0},{9,1},{10,2},{11,3},{12,4},{13,5},{14,6},{15,7},{16,8},{17,9... | collective-permute-start | bytes 4718600 | tf_op jit(solution)/shard_map/ppermute | solution.py:385
  306.3 1.3 collective-permute-start.18
  307.9 1.2 collective-permute-start.14
  309.1 29.1 %collective-permute-done.17 = bf16[2,128,3072]{2,1,0:T(8,128)(2,1)} collective-permute-done((bf16[2,128,3072]{2,1,0:T(8,128)(2,1)}, bf16[2,128,3072]{2,1,0:T(8,128)(2,1)}, u32[]{:S(2)}, u32[]{:S(2)}) %collective-permute-start.17) | collective-permute-done | bytes 1572896 | tf_op jit(solution)/shard_map/ppermute | solution.py:385
  338.2 1.6 select_bitcast_fusion.1
  339.8 3.2 collective-permute-done.18
  343.5 2.1 collective-permute-start.19
  345.6 36.1 %collective-permute-done.9.refs_7_ = bf16[256,3072]{1,0:T(8,128)(2,1)S(1)} collective-permute-done((bf16[256,3072]{1,0:T(8,128)(2,1)}, bf16[256,3072]{1,0:T(8,128)(2,1)S(1)}, u32[]{:S(2)}, u32[]{:S(2)}) %collective-permute-start.9) | collective-permute-done | bytes 1572896 | tf_op jit(solution)/shard_map/ppermute | solution.py:137
  382.1 1.2 collective-permute-start.15
  385.0 1.2 slice.68
  386.2 2.0 collective-permute-start.24
  388.2 1.5 collective-permute-start.23
  389.7 10.4 %collective-permute-done.16.refs_9_ = bf16[128,3072]{1,0:T(8,128)(2,1)S(1)} collective-permute-done((bf16[128,3072]{1,0:T(8,128)(2,1)S(1)}, bf16[128,3072]{1,0:T(8,128)(2,1)S(1)}, u32[]{:S(2)}, u32[]{:S(2)}) %collective-permute-start.16) | collective-permute-done | bytes 786464 | tf_op jit(solution)/shard_map/ppermute | solution.py:137
  401.0 23.4 %project.2 = (bf16[256,1024]{1,0:T(8,128)(2,1)}, bf16[256,1024]{1,0:T(8,128)(2,1)}, bf16[256,1024]{1,0:T(8,128)(2,1)}, bf16[256,1024]{1,0:T(8,128)(2,1)}) custom-call(s32[2]{0:T(128)} %pad_add_fusion.place_ref, bf16[256,3072]{1,0:T(8,128)(2,1)} %band.1.refs_0_, bf16[256,3072]{1,0:T(8,128)(2,1)} %copy-done.4, bf16[256,3072]{1,0:T(8,128)(2,1)} %copy-done.3, ...), custom_call_target="tpu_custom_call" | custom-call | flops 12884901888 | bytes 27262976 | tf_op jit(solution)/shard_map/project/pallas_call | solution.py:302
  424.5 1.5 select_bitcast_fusion.2
  426.2 1.8 collective-permute-start.25
  428.6 1.2 collective-permute-start.21
  432.1 14.6 %project.3 = (bf16[256,512]{1,0:T(8,128)(2,1)}, bf16[256,512]{1,0:T(8,128)(2,1)}, bf16[256,512]{1,0:T(8,128)(2,1)}, bf16[256,512]{1,0:T(8,128)(2,1)}) custom-call(s32[2]{0:T(128)} %pad_add_fusion.place_ref, bf16[256,3072]{1,0:T(8,128)(2,1)} %band.1.refs_0_, bf16[256,3072]{1,0:T(8,128)(2,1)} %copy-done.4, bf16[256,3072]{1,0:T(8,128)(2,1)} %copy-done.3, ...), custom_call_target="tpu_custom_call" | custom-call | flops 6442450944 | bytes 19922944 | tf_op jit(solution)/shard_map/project/pallas_call | solution.py:302
  447.5 1.2 collective-permute-start.27
  449.5 4.4 collective-permute-done.22.refs_3_
  453.8 4.6 collective-permute-done.26.refs_5_
  458.4 1.7 collective-permute-done.27.refs_6_
  460.1 4.8 %collective-permute-done.28.refs_7_ = bf16[256,512]{1,0:T(8,128)(2,1)S(1)} collective-permute-done((bf16[256,512]{1,0:T(8,128)(2,1)}, bf16[256,512]{1,0:T(8,128)(2,1)S(1)}, u32[]{:S(2)}, u32[]{:S(2)}) %collective-permute-start.28) | collective-permute-done | bytes 262176 | tf_op jit(solution)/shard_map/ppermute | solution.py:137
  465.6 4.3 assemble.1
  (82 shorter events, 15.4 us)
Async XLA Ops:
  4.8 109.5 %all-to-all-start = ((bf16[32,3,8,3072]{3,2,1,0:T(8,128)(2,1)}), bf16[32,3,8,3072]{3,2,1,0:T(8,128)(2,1)}, u32[]{:S(2)}, u32[]{:S(2)}) async-start(bf16[32,3,8,3072]{3,2,1,0:T(8,128)(2,1)} %copy_bitcast_fusion), calls=%async_computation | async-start | bytes 9437184 | tf_op jit(solution)/shard_map/all_to_all | solution.py:395
  14.8 5.2 %copy-start = (bf16[2,3072,192]{1,2,0:T(8,128)(2,1)S(1)}, bf16[2,3072,192]{1,2,0:T(8,128)(2,1)}, u32[]{:S(2)}) copy-start(bf16[2,3072,192]{1,2,0:T(8,128)(2,1)} %param.6) | copy-start | bytes 7077892
  14.8 104.2 %collective-permute-start = (bf16[2,256,3072]{2,1,0:T(8,128)(2,1)}, bf16[2,256,3072]{2,1,0:T(8,128)(2,1)}, u32[]{:S(2)}, u32[]{:S(2)}) collective-permute-start(bf16[2,256,3072]{2,1,0:T(8,128)(2,1)} %slice.55), channel_id=1, source_target_pairs={{0,1},{1,0},{2,3},{3,2},{4,5},{5,4},{6,7},{7,6},{8,9},{9,8},{10,11... | collective-permute-start | bytes 9437192 | tf_op jit(solution)/shard_map/ppermute | solution.py:388
  18.1 130.8 %collective-permute-start.1 = (bf16[256,3072]{1,0:T(8,128)(2,1)}, bf16[256,3072]{1,0:T(8,128)(2,1)}, u32[]{:S(2)}, u32[]{:S(2)}) collective-permute-start(bf16[256,3072]{1,0:T(8,128)(2,1)} %slice_bitcast_fusion.1), channel_id=1, source_target_pairs={{1,2},{3,4},{5,6},{7,8},{9,10},{11,12},{13,14},{15,16},{17,18},{19... | collective-permute-start | bytes 4718600 | tf_op jit(solution)/shard_map/ppermute | solution.py:392
  25.0 98.5 %copy-start.17 = (s32[32]{0:T(128)S(1)}, s32[32]{0:T(128)}, u32[]{:S(2)}) copy-start(s32[32]{0:T(128)} %param.7) | copy-start | bytes 388
  114.3 104.4 %collective-permute-start.11 = (bf16[2,192,3072]{2,1,0:T(8,128)(2,1)}, bf16[2,192,3072]{2,1,0:T(8,128)(2,1)S(1)}, u32[]{:S(2)}, u32[]{:S(2)}) collective-permute-start(bf16[2,192,3072]{2,1,0:T(8,128)(2,1)} %maximum_select_fusion.refs_10_), channel_id=1, source_target_pairs={{8,0},{9,1},{10,2},{11,3},{12,4},{13,5},{14,6},{15,7},{16,8},{17,9... | collective-permute-start | bytes 7077896 | tf_op jit(solution)/shard_map/ppermute | solution.py:385
  117.7 102.5 %collective-permute-start.10 = (bf16[2,192,3072]{2,1,0:T(8,128)(2,1)}, bf16[2,192,3072]{2,1,0:T(8,128)(2,1)}, u32[]{:S(2)}, u32[]{:S(2)}) collective-permute-start(bf16[2,192,3072]{2,1,0:T(8,128)(2,1)} %maximum_select_fusion.refs_10_), channel_id=1, source_target_pairs={{0,8},{1,9},{2,10},{3,11},{4,12},{5,13},{6,14},{7,15},{8,16},{9,17... | collective-permute-start | bytes 7077896 | tf_op jit(solution)/shard_map/ppermute | solution.py:385
  121.6 27.3 %collective-permute-start.2 = (bf16[256,3072]{1,0:T(8,128)(2,1)}, bf16[256,3072]{1,0:T(8,128)(2,1)}, u32[]{:S(2)}, u32[]{:S(2)}) collective-permute-start(bf16[256,3072]{1,0:T(8,128)(2,1)} %slice_bitcast_fusion), channel_id=1, source_target_pairs={{0,2},{2,4},{4,6},{6,8},{8,10},{10,12},{12,14},{14,16},{16,18},{18... | collective-permute-start | bytes 4718600 | tf_op jit(solution)/shard_map/ppermute | solution.py:393
  135.5 134.9 %all-to-all-start.1 = ((bf16[32,8,3072]{2,1,0:T(8,128)(2,1)}), bf16[32,8,3072]{2,1,0:T(8,128)(2,1)}, u32[]{:S(2)}, u32[]{:S(2)}) async-start(bf16[32,8,3072]{2,1,0:T(8,128)(2,1)} %strided.1), calls=%async_computation.1 | async-start | bytes 3145728 | tf_op jit(solution)/shard_map/all_to_all | solution.py:401
  163.4 85.5 %collective-permute-start.4 = (bf16[256,3072]{1,0:T(8,128)(2,1)}, bf16[256,3072]{1,0:T(8,128)(2,1)S(1)}, u32[]{:S(2)}, u32[]{:S(2)}) collective-permute-start(bf16[256,3072]{1,0:T(8,128)(2,1)} %band.1.refs_0_), channel_id=1, source_target_pairs={{0,4},{1,5},{2,6},{3,7},{4,0},{5,1},{6,2},{7,3},{8,12},{9,13},{10,... | collective-permute-start | bytes 4718600 | tf_op jit(solution)/shard_map/ppermute | solution.py:137
  163.7 86.5 %collective-permute-start.3 = (bf16[256,3072]{1,0:T(8,128)(2,1)}, bf16[256,3072]{1,0:T(8,128)(2,1)S(1)}, u32[]{:S(2)}, u32[]{:S(2)}) collective-permute-start(bf16[256,3072]{1,0:T(8,128)(2,1)} %band.1.refs_0_), channel_id=1, source_target_pairs={{0,2},{1,3},{2,0},{3,1},{4,6},{5,7},{6,4},{7,5},{8,10},{9,11},{10,... | collective-permute-start | bytes 4718600 | tf_op jit(solution)/shard_map/ppermute | solution.py:137
  164.0 106.5 %collective-permute-start.7 = (bf16[2,192,3072]{2,1,0:T(8,128)(2,1)}, bf16[2,192,3072]{2,1,0:T(8,128)(2,1)}, u32[]{:S(2)}, u32[]{:S(2)}) collective-permute-start(bf16[2,192,3072]{2,1,0:T(8,128)(2,1)} %maximum_select_fusion.refs_10_), channel_id=1, source_target_pairs={{0,1},{1,0},{2,3},{3,2},{4,5},{5,4},{6,7},{7,6},{8,9},{9,8},{10,11... | collective-permute-start | bytes 7077896 | tf_op jit(solution)/shard_map/ppermute | solution.py:388
  218.7 1.4 copy-start.8
  220.1 77.1 %collective-permute-start.12 = (bf16[2,192,3072]{2,1,0:T(8,128)(2,1)}, bf16[2,192,3072]{2,1,0:T(8,128)(2,1)S(1)}, u32[]{:S(2)}, u32[]{:S(2)}) collective-permute-start(bf16[2,192,3072]{2,1,0:T(8,128)(2,1)} %collective-permute-done.10), channel_id=1, source_target_pairs={{0,8},{1,9},{2,10},{3,11},{4,12},{5,13},{6,14},{7,15},{8,16},{9,17... | collective-permute-start | bytes 7077896 | tf_op jit(solution)/shard_map/ppermute | solution.py:385
  221.4 76.9 %collective-permute-start.13 = (bf16[2,192,3072]{2,1,0:T(8,128)(2,1)}, bf16[2,192,3072]{2,1,0:T(8,128)(2,1)}, u32[]{:S(2)}, u32[]{:S(2)}) collective-permute-start(bf16[2,192,3072]{2,1,0:T(8,128)(2,1)} %copy-done.8), channel_id=1, source_target_pairs={{8,0},{9,1},{10,2},{11,3},{12,4},{13,5},{14,6},{15,7},{16,8},{17,9... | collective-permute-start | bytes 7077896 | tf_op jit(solution)/shard_map/ppermute | solution.py:385
  248.9 1.2 copy-start.3
  250.1 19.0 %collective-permute-start.6 = (bf16[128,3072]{1,0:T(8,128)(2,1)S(1)}, bf16[128,3072]{1,0:T(8,128)(2,1)S(1)}, u32[]{:S(2)}, u32[]{:S(2)}) collective-permute-start(bf16[128,3072]{1,0:T(8,128)(2,1)S(1)} %slice.74), channel_id=1, source_target_pairs={{0,2},{1,3},{2,0},{3,1},{4,6},{5,7},{6,4},{7,5},{8,10},{9,11},{10,... | collective-permute-start | bytes 2359304 | tf_op jit(solution)/shard_map/ppermute | solution.py:137
  250.2 1.2 copy-start.4
  251.4 19.0 %collective-permute-start.5 = (bf16[128,3072]{1,0:T(8,128)(2,1)S(1)}, bf16[128,3072]{1,0:T(8,128)(2,1)}, u32[]{:S(2)}, u32[]{:S(2)}) collective-permute-start(bf16[128,3072]{1,0:T(8,128)(2,1)S(1)} %slice.73), channel_id=1, source_target_pairs={{0,4},{1,5},{2,6},{3,7},{4,0},{5,1},{6,2},{7,3},{8,12},{9,13},{10,... | collective-permute-start | bytes 2359304 | tf_op jit(solution)/shard_map/ppermute | solution.py:137
  269.1 37.2 %copy-start.12 = (bf16[128,3072]{1,0:T(8,128)(2,1)}, bf16[128,3072]{1,0:T(8,128)(2,1)S(1)}, u32[]{:S(2)}) copy-start(bf16[128,3072]{1,0:T(8,128)(2,1)S(1)} %collective-permute-done.6.refs_4_) | copy-start | bytes 2359300
  300.9 37.3 %collective-permute-start.17 = (bf16[2,128,3072]{2,1,0:T(8,128)(2,1)}, bf16[2,128,3072]{2,1,0:T(8,128)(2,1)}, u32[]{:S(2)}, u32[]{:S(2)}) collective-permute-start(bf16[2,128,3072]{2,1,0:T(8,128)(2,1)} %slice.63), channel_id=1, source_target_pairs={{8,0},{9,1},{10,2},{11,3},{12,4},{13,5},{14,6},{15,7},{16,8},{17,9... | collective-permute-start | bytes 4718600 | tf_op jit(solution)/shard_map/ppermute | solution.py:385
  306.3 36.7 %collective-permute-start.18 = (bf16[2,128,3072]{2,1,0:T(8,128)(2,1)S(1)}, bf16[2,128,3072]{2,1,0:T(8,128)(2,1)S(1)}, u32[]{:S(2)}, u32[]{:S(2)}) collective-permute-start(bf16[2,128,3072]{2,1,0:T(8,128)(2,1)S(1)} %slice.64), channel_id=1, source_target_pairs={{0,8},{1,9},{2,10},{3,11},{4,12},{5,13},{6,14},{7,15},{8,16},{9,17... | collective-permute-start | bytes 4718600 | tf_op jit(solution)/shard_map/ppermute | solution.py:385
  307.9 31.9 %copy-start.1 = (bf16[2,192,3072]{2,1,0:T(8,128)(2,1)}, bf16[2,192,3072]{2,1,0:T(8,128)(2,1)S(1)}, u32[]{:S(2)}) copy-start(bf16[2,192,3072]{2,1,0:T(8,128)(2,1)S(1)} %broadcast_select_fusion.refs_12_) | copy-start | bytes 7077892
  307.9 35.1 %copy-start.9 = (bf16[2,192,3072]{2,1,0:T(8,128)(2,1)S(1)}, bf16[2,192,3072]{2,1,0:T(8,128)(2,1)}, u32[]{:S(2)}) copy-start(bf16[2,192,3072]{2,1,0:T(8,128)(2,1)} %copy-done.8) | copy-start | bytes 7077892
  307.9 73.8 %collective-permute-start.14 = (bf16[2,192,3072]{2,1,0:T(8,128)(2,1)S(1)}, bf16[2,192,3072]{2,1,0:T(8,128)(2,1)S(1)}, u32[]{:S(2)}, u32[]{:S(2)}) collective-permute-start(bf16[2,192,3072]{2,1,0:T(8,128)(2,1)S(1)} %broadcast_select_fusion.refs_12_), channel_id=1, source_target_pairs={{0,1},{1,0},{2,3},{3,2},{4,5},{5,4},{6,7},{7,6},{8,9},{9,8},{10,11... | collective-permute-start | bytes 7077896 | tf_op jit(solution)/shard_map/ppermute | solution.py:388
  343.5 42.7 %copy-start.7 = (bf16[2,2,128,3072]{3,2,1,0:T(8,128)(2,1)}, bf16[2,2,128,3072]{3,2,1,0:T(8,128)(2,1)S(1)}, u32[]{:S(2)}) copy-start(bf16[2,2,128,3072]{3,2,1,0:T(8,128)(2,1)S(1)} %pad_maximum_fusion.refs_14_) | copy-start | bytes 9437188
  343.5 56.8 %collective-permute-start.19 = (bf16[2,2,128,3072]{3,2,1,0:T(8,128)(2,1)S(1)}, bf16[2,2,128,3072]{3,2,1,0:T(8,128)(2,1)}, u32[]{:S(2)}, u32[]{:S(2)}) collective-permute-start(bf16[2,2,128,3072]{3,2,1,0:T(8,128)(2,1)S(1)} %pad_maximum_fusion.refs_14_), channel_id=1, source_target_pairs={{0,1},{1,0},{2,3},{3,2},{4,5},{5,4},{6,7},{7,6},{8,9},{9,8},{10,11... | collective-permute-start | bytes 9437192 | tf_op jit(solution)/shard_map/ppermute | solution.py:388
  345.6 36.1 %collective-permute-start.9 = (bf16[256,3072]{1,0:T(8,128)(2,1)}, bf16[256,3072]{1,0:T(8,128)(2,1)S(1)}, u32[]{:S(2)}, u32[]{:S(2)}) collective-permute-start(bf16[256,3072]{1,0:T(8,128)(2,1)} %bitcast.11.refs_5_), channel_id=1, source_target_pairs={{0,4},{1,5},{2,6},{3,7},{4,0},{5,1},{6,2},{7,3},{8,12},{9,13},{10,... | collective-permute-start | bytes 4718600 | tf_op jit(solution)/shard_map/ppermute | solution.py:137
  345.6 36.1 %collective-permute-start.8 = (bf16[256,3072]{1,0:T(8,128)(2,1)}, bf16[256,3072]{1,0:T(8,128)(2,1)S(1)}, u32[]{:S(2)}, u32[]{:S(2)}) collective-permute-start(bf16[256,3072]{1,0:T(8,128)(2,1)} %bitcast.11.refs_5_), channel_id=1, source_target_pairs={{0,2},{1,3},{2,0},{3,1},{4,6},{5,7},{6,4},{7,5},{8,10},{9,11},{10,... | collective-permute-start | bytes 4718600 | tf_op jit(solution)/shard_map/ppermute | solution.py:137
  381.7 3.3 copy-start.5
  381.7 3.3 copy-start.6
  381.7 6.5 %copy-start.10 = (bf16[2,192,3072]{2,1,0:T(8,128)(2,1)}, bf16[2,192,3072]{2,1,0:T(8,128)(2,1)S(1)}, u32[]{:S(2)}) copy-start(bf16[2,192,3072]{2,1,0:T(8,128)(2,1)S(1)} %collective-permute-done.14.refs_13_) | copy-start | bytes 7077892
  381.8 18.3 %collective-permute-start.16 = (bf16[128,3072]{1,0:T(8,128)(2,1)S(1)}, bf16[128,3072]{1,0:T(8,128)(2,1)S(1)}, u32[]{:S(2)}, u32[]{:S(2)}) collective-permute-start(bf16[128,3072]{1,0:T(8,128)(2,1)S(1)} %slice.61), channel_id=1, source_target_pairs={{0,2},{1,3},{2,0},{3,1},{4,6},{5,7},{6,4},{7,5},{8,10},{9,11},{10,... | collective-permute-start | bytes 2359304 | tf_op jit(solution)/shard_map/ppermute | solution.py:137
  382.1 18.2 %collective-permute-start.15 = (bf16[128,3072]{1,0:T(8,128)(2,1)S(1)}, bf16[128,3072]{1,0:T(8,128)(2,1)}, u32[]{:S(2)}, u32[]{:S(2)}) collective-permute-start(bf16[128,3072]{1,0:T(8,128)(2,1)S(1)} %slice.60), channel_id=1, source_target_pairs={{0,4},{1,5},{2,6},{3,7},{4,0},{5,1},{6,2},{7,3},{8,12},{9,13},{10,... | collective-permute-start | bytes 2359304 | tf_op jit(solution)/shard_map/ppermute | solution.py:137
  386.2 38.3 %collective-permute-start.24 = (bf16[2,64,3072]{2,1,0:T(8,128)(2,1)S(1)}, bf16[2,64,3072]{2,1,0:T(8,128)(2,1)S(1)}, u32[]{:S(2)}, u32[]{:S(2)}) collective-permute-start(bf16[2,64,3072]{2,1,0:T(8,128)(2,1)S(1)} %slice.68), channel_id=1, source_target_pairs={{8,0},{9,1},{10,2},{11,3},{12,4},{13,5},{14,6},{15,7},{16,8},{17,9... | collective-permute-start | bytes 2359304 | tf_op jit(solution)/shard_map/ppermute | solution.py:385
  388.2 36.2 %collective-permute-start.23 = (bf16[2,64,3072]{2,1,0:T(8,128)(2,1)}, bf16[2,64,3072]{2,1,0:T(8,128)(2,1)S(1)}, u32[]{:S(2)}, u32[]{:S(2)}) collective-permute-start(bf16[2,64,3072]{2,1,0:T(8,128)(2,1)} %slice.67), channel_id=1, source_target_pairs={{0,8},{1,9},{2,10},{3,11},{4,12},{5,13},{6,14},{7,15},{8,16},{9,17... | collective-permute-start | bytes 2359304 | tf_op jit(solution)/shard_map/ppermute | solution.py:385
  400.2 0.9 copy-start.13
  426.2 4.8 %copy-start.2 = (bf16[2,2,64,3072]{3,2,1,0:T(8,128)(2,1)}, bf16[2,2,64,3072]{3,2,1,0:T(8,128)(2,1)S(1)}, u32[]{:S(2)}) copy-start(bf16[2,2,64,3072]{3,2,1,0:T(8,128)(2,1)S(1)} %pad_maximum_fusion.1.refs_14_) | copy-start | bytes 4718596
  426.2 4.8 %collective-permute-start.25 = (bf16[2,2,64,3072]{3,2,1,0:T(8,128)(2,1)S(1)}, bf16[2,2,64,3072]{3,2,1,0:T(8,128)(2,1)S(1)}, u32[]{:S(2)}, u32[]{:S(2)}) collective-permute-start(bf16[2,2,64,3072]{3,2,1,0:T(8,128)(2,1)S(1)} %pad_maximum_fusion.1.refs_14_), channel_id=1, source_target_pairs={{0,1},{1,0},{2,3},{3,2},{4,5},{5,4},{6,7},{7,6},{8,9},{9,8},{10,11... | collective-permute-start | bytes 4718600 | tf_op jit(solution)/shard_map/ppermute | solution.py:388
  427.9 20.8 %collective-permute-start.20 = (bf16[256,1024]{1,0:T(8,128)(2,1)}, bf16[256,1024]{1,0:T(8,128)(2,1)}, u32[]{:S(2)}, u32[]{:S(2)}) collective-permute-start(bf16[256,1024]{1,0:T(8,128)(2,1)} %get-tuple-element.60), channel_id=1, source_target_pairs={{0,2},{1,3},{2,0},{3,1},{4,6},{5,7},{6,4},{7,5},{8,10},{9,11},{10,... | collective-permute-start | bytes 1572872 | tf_op jit(solution)/shard_map/ppermute | solution.py:137
  428.6 20.8 %collective-permute-start.21 = (bf16[256,1024]{1,0:T(8,128)(2,1)}, bf16[256,1024]{1,0:T(8,128)(2,1)}, u32[]{:S(2)}, u32[]{:S(2)}) collective-permute-start(bf16[256,1024]{1,0:T(8,128)(2,1)} %get-tuple-element.61), channel_id=1, source_target_pairs={{0,4},{1,5},{2,6},{3,7},{4,0},{5,1},{6,2},{7,3},{8,12},{9,13},{10,... | collective-permute-start | bytes 1572872 | tf_op jit(solution)/shard_map/ppermute | solution.py:137
  429.8 24.0 %collective-permute-start.22 = (bf16[256,1024]{1,0:T(8,128)(2,1)}, bf16[256,1024]{1,0:T(8,128)(2,1)}, u32[]{:S(2)}, u32[]{:S(2)}) collective-permute-start(bf16[256,1024]{1,0:T(8,128)(2,1)} %get-tuple-element.62), channel_id=1, source_target_pairs={{0,6},{1,7},{2,4},{3,5},{4,2},{5,3},{6,0},{7,1},{8,14},{9,15},{10,... | collective-permute-start | bytes 1572872 | tf_op jit(solution)/shard_map/ppermute | solution.py:137
  431.0 1.1 copy-start.11
  446.7 11.7 %collective-permute-start.26 = (bf16[256,512]{1,0:T(8,128)(2,1)}, bf16[256,512]{1,0:T(8,128)(2,1)S(1)}, u32[]{:S(2)}, u32[]{:S(2)}) collective-permute-start(bf16[256,512]{1,0:T(8,128)(2,1)} %get-tuple-element.72), channel_id=1, source_target_pairs={{0,2},{1,3},{2,0},{3,1},{4,6},{5,7},{6,4},{7,5},{8,10},{9,11},{10,... | collective-permute-start | bytes 786440 | tf_op jit(solution)/shard_map/ppermute | solution.py:137
  447.5 12.6 %collective-permute-start.27 = (bf16[256,512]{1,0:T(8,128)(2,1)}, bf16[256,512]{1,0:T(8,128)(2,1)S(1)}, u32[]{:S(2)}, u32[]{:S(2)}) collective-permute-start(bf16[256,512]{1,0:T(8,128)(2,1)} %get-tuple-element.73), channel_id=1, source_target_pairs={{0,4},{1,5},{2,6},{3,7},{4,0},{5,1},{6,2},{7,3},{8,12},{9,13},{10,... | collective-permute-start | bytes 786440 | tf_op jit(solution)/shard_map/ppermute | solution.py:137
  448.7 16.2 %collective-permute-start.28 = (bf16[256,512]{1,0:T(8,128)(2,1)}, bf16[256,512]{1,0:T(8,128)(2,1)S(1)}, u32[]{:S(2)}, u32[]{:S(2)}) collective-permute-start(bf16[256,512]{1,0:T(8,128)(2,1)} %get-tuple-element.74), channel_id=1, source_target_pairs={{0,6},{1,7},{2,4},{3,5},{4,2},{5,3},{6,0},{7,1},{8,14},{9,15},{10,... | collective-permute-start | bytes 786440 | tf_op jit(solution)/shard_map/ppermute | solution.py:137
  458.4 6.5 %copy-start.14 = (bf16[256,512]{1,0:T(8,128)(2,1)}, bf16[256,512]{1,0:T(8,128)(2,1)S(1)}, u32[]{:S(2)}) copy-start(bf16[256,512]{1,0:T(8,128)(2,1)S(1)} %collective-permute-done.26.refs_5_) | copy-start | bytes 786436
  460.1 4.8 %copy-start.15 = (bf16[256,512]{1,0:T(8,128)(2,1)}, bf16[256,512]{1,0:T(8,128)(2,1)S(1)}, u32[]{:S(2)}) copy-start(bf16[256,512]{1,0:T(8,128)(2,1)S(1)} %collective-permute-done.27.refs_6_) | copy-start | bytes 786436
  (1 other events, 0.7 us)

commit v4 on v3

--- a/solution.py
+++ b/solution.py
@@ -252,7 +252,7 @@
         if slot == 0:
             return first.at[:, pl.ds(low, rows)]
         if slot == 2:
-            return middle.at[:, pl.ds(low, rows)]
+            return middle
         return ends.at[slot // 2]
 
     @pl.when(step == 0)
@@ -396,35 +396,38 @@
 
     if relay:
         turned, gathered = lax.optimization_barrier((turned, gathered))
-        up, down = [along(turned, 1)], [along(turned, -1)]
+        cuts = [slice(0, sizes[0]), slice(sizes[0], share)]
+        up = [[along(turned[:, cut], 1) for cut in cuts]]
+        down = [[along(turned[:, cut], -1) for cut in cuts]]
     column_out = stride_heads(row_doc, gathered)
     stride_out = lax.all_to_all(column_out, "seq", split_axis=0, concat_axis=0, tiled=True)
-    keys, values, column_out = lax.optimization_barrier((keys, values, column_out))
     previous = jnp.where(me > 0, row_doc[jnp.maximum(me - 1, 0)], -1)
     joined = jnp.stack([(previous == row_doc[me]).astype(jnp.int32), core])
     band_out = band_heads(joined, band_qkv, twin, keys, values)
     near = near_parts(band_out)
+    half = tokens // 2
+    lower, upper = near[0][:half], near[1][half:]
     if relay:
-        up[0], down[0], _ = lax.optimization_barrier((up[0], down[0], band_out))
-        up.append(along(up[0], 1))
-        down.append(along(down[0], -1))
+        up[0][0], down[0][0], lower = lax.optimization_barrier((up[0][0], down[0][0], lower))
+        up.append([])
+        down.append([])
+        for index in range(2):
+            up[1].append(along(up[0][index], 1))
+            down[1].append(along(down[0][index], -1))
         own_twin = twin_of(turned)
-    band_parts = (band_out, *near, *far_parts(*near))
+    band_parts = (band_out, *near, moved(lower, 2), moved(upper, 1))
     stride_out, band_parts = lax.optimization_barrier((stride_out, band_parts))
     stride_out = stride_out.reshape(tokens, width)
     if relay:
         stride_out, own_twin = lax.optimization_barrier((stride_out, own_twin))
     near = near_parts(stride_out)
     if relay:
-        up[1], down[1], _ = lax.optimization_barrier((up[1], down[1], stride_out))
+        up[1][0], down[1][0], _ = lax.optimization_barrier((up[1][0], down[1][0], stride_out))
         ends = []
-        low = 0
-        for rows in sizes:
-            cut = slice(low, low + rows)
-            ends.append((along(up[1][:, cut], 1), along(down[1][:, cut], -1)))
-            low += rows
-        middle = jnp.where(line >= 2, up[1], down[1])
-        middle_twin = twin_of(middle)
+        for upper_piece, lower_piece in zip(up[1], down[1]):
+            ends.append((along(upper_piece, 1), along(lower_piece, -1)))
+        middle = [jnp.where(line >= 2, *pair) for pair in zip(up[1], down[1])]
+        middle_twin = [twin_of(piece) for piece in middle]
         near, middle_twin = lax.optimization_barrier((near, middle_twin))
     stride_parts = (stride_out, *near, *far_parts(*near))
 
@@ -444,11 +447,11 @@
                 up_end, down_end, _ = lax.optimization_barrier((up_end, down_end, blocks))
             edge = jnp.stack(
                 [
-                    jnp.where(line >= 1, up[0][:, cut], down_end),
-                    jnp.where(line >= 3, up_end, down[0][:, cut]),
+                    jnp.where(line >= 1, up[0][index], down_end),
+                    jnp.where(line >= 3, up_end, down[0][index]),
                 ]
             )
-            slots = [turned, own_twin, middle, middle_twin, edge, twin_of(edge)]
+            slots = [turned, own_twin, middle[index], middle_twin[index], edge, twin_of(edge)]
         else:
             part = lax.all_gather(turned[:, cut], "seq", axis=0, axis_index_groups=groups)
             weight = part.reshape(outer, CORES, 2, rows, width)

time: 474 us -> 454 us (0.958)
  waiting for transfers between devices: 231 us -> 144 us
  starting transfers between devices: 132 us -> 199 us
  local copies, waits for them, and re-layouts: 29 us -> 22.4 us
    all_to_all x1, waiting for transfers between devices: 89.3 us -> 10.2 us  [per_device(): lax.all_to_all(grid, 'seq', split_axis=0, concat_axis=0, tiled=True)]
    ppermute x14, starting transfers between devices: 7.58 us -> 68.4 us  [moved(): lax.ppermute(array, 'seq', [(i, i ^ step * CORES) for i in range(size)])]
    ppermute x5 -> x6, starting transfers between devices: 60.2 us -> 12.4 us  [twin_of(): return lax.ppermute(array, 'seq', [(i, i ^ 1) for i in range(size)])]
    ppermute x8 -> x12, starting transfers between devices: 43.4 us -> 73.3 us  [along(): lax.ppermute(array, 'seq', [(i, i + plane) for i in range(size) if 0 <= i...]
    all_to_all x1, starting transfers between devices: 10.9 us -> 35.2 us  [per_device(): lax.all_to_all(column_out, 'seq', split_axis=0, concat_axis=0, tiled=True)]
    ppermute x8 -> x12, waiting for transfers between devices: 60.2 us -> 54.4 us  [along(): lax.ppermute(array, 'seq', [(i, i + plane) for i in range(size) if 0 <= i...]
    ppermute x14, waiting for transfers between devices: 81.1 us -> 76.3 us  [moved(): lax.ppermute(array, 'seq', [(i, i ^ step * CORES) for i in range(size)])]
  transfers between devices with their start and end apart: 31 -> 36, of which waited for: 15 -> 17; matrix products, arithmetic and copies ran while one was open for 5% -> 5% of each run, Pallas kernels for 13% -> 14%
where the time goes in v4:
time: 454 us; the launch traced here: 447 us
  starting transfers between devices  199 us (44%)
  waiting for transfers between devices  144 us (32%)
  Pallas kernels  67.4 us (15%)
  local copies, waits for them, and re-layouts  22.4 us (5%)
  other arithmetic  12.8 us (3%)
    ppermute x14, waiting for transfers between devices, moved(): lax.ppermute(array, 'seq', [(i, i ^ step * CORES) for i in range(size)])  76.3 us
    ppermute x12, starting transfers between devices, along(): lax.ppermute(array, 'seq', [(i, i + plane) for i in range(size) if 0 <= i...  73.3 us
    ppermute x14, starting transfers between devices, moved(): lax.ppermute(array, 'seq', [(i, i ^ step * CORES) for i in range(size)])  68.4 us
    ppermute x12, waiting for transfers between devices, along(): lax.ppermute(array, 'seq', [(i, i + plane) for i in range(size) if 0 <= i...  54.4 us
    pallas_call x2, Pallas kernels, project_slots(): pl.pallas_call(functools.partial(slots_kernel, low, rows), out_shape=[jax...  37.9 us
    all_to_all x1, starting transfers between devices, per_device(): lax.all_to_all(column_out, 'seq', split_axis=0, concat_axis=0, tiled=True)  35.2 us
    pallas_call x1, Pallas kernels, band_heads(): pl.pallas_call(functools.partial(band_kernel, heads), out_shape=jax.Shape...  14.6 us
    ppermute x6, starting transfers between devices, twin_of(): return lax.ppermute(array, 'seq', [(i, i ^ 1) for i in range(size)])  12.4 us
  transfers between devices with their start and end apart: 36, of which 17 were waited for; matrix products, arithmetic and copies ran while one was open for 5% of the time, Pallas kernels for 14%

profile of v4, /device:TPU:31, one launch (start us, length us, event | category | flops | bytes accessed | tf_op | source)
XLA Modules:
  0.0 447.4 jit_solution(13907313120529489061)
XLA Ops:
  0.0 4.8 %copy_bitcast_fusion = bf16[32,3,8,3072]{3,2,1,0:T(8,128)(2,1)} fusion(bf16[3,256,3072]{2,1,0:T(8,128)(2,1)} %param.5), kind=kLoop, calls=%fused_computation | loop fusion | bytes 9437184 | tf_op jit(solution)/shard_map/transpose | solution.py:394
  4.8 6.2 %all-to-all-start = ((bf16[32,3,8,3072]{3,2,1,0:T(8,128)(2,1)}), bf16[32,3,8,3072]{3,2,1,0:T(8,128)(2,1)}, u32[]{:S(2)}, u32[]{:S(2)}) async-start(bf16[32,3,8,3072]{3,2,1,0:T(8,128)(2,1)} %copy_bitcast_fusion), calls=%async_computation | async-start | bytes 9437184 | tf_op jit(solution)/shard_map/all_to_all | solution.py:395
  11.0 2.1 slice.39
  13.6 2.7 slice_bitcast_fusion.1
  16.3 1.9 collective-permute-start.1
  18.9 1.4 slice_bitcast_fusion
  21.0 1.8 collective-permute-start.2
  26.7 3.7 maximum_select_fusion.refs_10_
  30.4 14.6 %band.1.refs_0_ = bf16[256,3072]{1,0:T(8,128)(2,1)} custom-call(s32[2]{0:T(128)} %pad_add_fusion.1.joined_ref, bf16[3,256,3072]{2,1,0:T(8,128)(2,1)} %own_ref.1, bf16[2,256,3072]{2,1,0:T(8,128)(2,1)} %copy-done.2, bf16[256,3072]{1,0:T(8,128)(2,1)} %collective-permute-done.1.keys_ref, bf16[256,3072]{1,0:T(8,128)(2,1)} %collective-permute-done.2.values_ref), custom_call_target="tpu_custom_call" | custom-call | flops 1610612736 | bytes 9437184 | tf_op jit(solution)/shard_map/band/pallas_call | solution.py:56
  45.0 59.3 %collective-permute-start.3 = (bf16[256,3072]{1,0:T(8,128)(2,1)}, bf16[256,3072]{1,0:T(8,128)(2,1)}, u32[]{:S(2)}, u32[]{:S(2)}) collective-permute-start(bf16[256,3072]{1,0:T(8,128)(2,1)} %band.1.refs_0_), channel_id=1, source_target_pairs={{0,2},{1,3},{2,0},{3,1},{4,6},{5,7},{6,4},{7,5},{8,10},{9,11},{10,... | collective-permute-start | bytes 4718600 | tf_op jit(solution)/shard_map/ppermute | solution.py:137
  104.3 10.2 %all-to-all-done.qkv_ref = bf16[32,3,8,3072]{3,2,1,0:T(8,128)(2,1)} async-done(((bf16[32,3,8,3072]{3,2,1,0:T(8,128)(2,1)}), bf16[32,3,8,3072]{3,2,1,0:T(8,128)(2,1)}, u32[]{:S(2)}, u32[]{:S(2)}) %all-to-all-start) | async-done | bytes 4718624 | tf_op jit(solution)/shard_map/all_to_all | solution.py:395
  114.5 1.3 slice.42
  115.8 25.3 %collective-permute-start.6 = (bf16[2,128,3072]{2,1,0:T(8,128)(2,1)}, bf16[2,128,3072]{2,1,0:T(8,128)(2,1)}, u32[]{:S(2)}, u32[]{:S(2)}) collective-permute-start(bf16[2,128,3072]{2,1,0:T(8,128)(2,1)} %slice.42), channel_id=1, source_target_pairs={{8,0},{9,1},{10,2},{11,3},{12,4},{13,5},{14,6},{15,7},{16,8},{17,9... | collective-permute-start | bytes 4718600 | tf_op jit(solution)/shard_map/ppermute | solution.py:385
  143.9 10.5 %strided.1 = bf16[32,8,3072]{2,1,0:T(8,128)(2,1)} custom-call(s32[256,1]{1,0:T(8,128)} %broadcast_in_dim_reshape.8.doc_row_ref, s32[1,256]{1,0:T(1,128)} %broadcast_in_dim_reshape.7.doc_col_ref, bf16[32,3,8,3072]{3,2,1,0:T(8,128)(2,1)} %all-to-all-done.qkv_ref), custom_call_target="tpu_custom_call" | custom-call | flops 805306368 | bytes 6291456 | tf_op jit(solution)/shard_map/strided/pallas_call | solution.py:115
  154.4 35.2 %all-to-all-start.1 = ((bf16[32,8,3072]{2,1,0:T(8,128)(2,1)}), bf16[32,8,3072]{2,1,0:T(8,128)(2,1)}, u32[]{:S(2)}, u32[]{:S(2)}) async-start(bf16[32,8,3072]{2,1,0:T(8,128)(2,1)} %strided.1), calls=%async_computation.1 | async-start | bytes 3145728 | tf_op jit(solution)/shard_map/all_to_all | solution.py:403
  191.7 10.0 %collective-permute-done.5 = bf16[2,128,3072]{2,1,0:T(8,128)(2,1)} collective-permute-done((bf16[2,128,3072]{2,1,0:T(8,128)(2,1)}, bf16[2,128,3072]{2,1,0:T(8,128)(2,1)}, u32[]{:S(2)}, u32[]{:S(2)}) %collective-permute-start.5) | collective-permute-done | bytes 1572896 | tf_op jit(solution)/shard_map/ppermute | solution.py:385
  203.1 14.0 %collective-permute-start.13 = (bf16[2,128,3072]{2,1,0:T(8,128)(2,1)}, bf16[2,128,3072]{2,1,0:T(8,128)(2,1)}, u32[]{:S(2)}, u32[]{:S(2)}) collective-permute-start(bf16[2,128,3072]{2,1,0:T(8,128)(2,1)} %collective-permute-done.6), channel_id=1, source_target_pairs={{8,0},{9,1},{10,2},{11,3},{12,4},{13,5},{14,6},{15,7},{16,8},{17,9... | collective-permute-start | bytes 4718600 | tf_op jit(solution)/shard_map/ppermute | solution.py:385
  217.1 24.5 %collective-permute-done.4.refs_2_ = bf16[256,3072]{1,0:T(8,128)(2,1)S(1)} collective-permute-done((bf16[256,3072]{1,0:T(8,128)(2,1)}, bf16[256,3072]{1,0:T(8,128)(2,1)S(1)}, u32[]{:S(2)}, u32[]{:S(2)}) %collective-permute-start.4) | collective-permute-done | bytes 1572896 | tf_op jit(solution)/shard_map/ppermute | solution.py:137
  241.8 1.3 collective-permute-start.7
  243.1 17.4 %collective-permute-done.8.refs_4_ = bf16[128,3072]{1,0:T(8,128)(2,1)S(1)} collective-permute-done((bf16[128,3072]{1,0:T(8,128)(2,1)S(1)}, bf16[128,3072]{1,0:T(8,128)(2,1)S(1)}, u32[]{:S(2)}, u32[]{:S(2)}) %collective-permute-start.8) | collective-permute-done | bytes 786464 | tf_op jit(solution)/shard_map/ppermute | solution.py:137
  261.5 1.3 collective-permute-start.23
  262.9 12.3 %collective-permute-start.17 = (bf16[2,64,3072]{2,1,0:T(8,128)(2,1)S(1)}, bf16[2,64,3072]{2,1,0:T(8,128)(2,1)}, u32[]{:S(2)}, u32[]{:S(2)}) collective-permute-start(bf16[2,64,3072]{2,1,0:T(8,128)(2,1)S(1)} %slice.45), channel_id=1, source_target_pairs={{8,0},{9,1},{10,2},{11,3},{12,4},{13,5},{14,6},{15,7},{16,8},{17,9... | collective-permute-start | bytes 2359304 | tf_op jit(solution)/shard_map/ppermute | solution.py:385
  276.5 4.1 collective-permute-start.22
  280.6 9.0 %collective-permute-done.17 = bf16[2,64,3072]{2,1,0:T(8,128)(2,1)} collective-permute-done((bf16[2,64,3072]{2,1,0:T(8,128)(2,1)S(1)}, bf16[2,64,3072]{2,1,0:T(8,128)(2,1)}, u32[]{:S(2)}, u32[]{:S(2)}) %collective-permute-start.17) | collective-permute-done | bytes 786464 | tf_op jit(solution)/shard_map/ppermute | solution.py:385
  289.6 5.1 %collective-permute-start.18 = (bf16[2,64,3072]{2,1,0:T(8,128)(2,1)}, bf16[2,64,3072]{2,1,0:T(8,128)(2,1)}, u32[]{:S(2)}, u32[]{:S(2)}) collective-permute-start(bf16[2,64,3072]{2,1,0:T(8,128)(2,1)} %collective-permute-done.17), channel_id=1, source_target_pairs={{8,0},{9,1},{10,2},{11,3},{12,4},{13,5},{14,6},{15,7},{16,8},{17,9... | collective-permute-start | bytes 2359304 | tf_op jit(solution)/shard_map/ppermute | solution.py:385
  294.7 28.0 %collective-permute-done.15 = bf16[2,64,3072]{2,1,0:T(8,128)(2,1)} collective-permute-done((bf16[2,64,3072]{2,1,0:T(8,128)(2,1)S(1)}, bf16[2,64,3072]{2,1,0:T(8,128)(2,1)}, u32[]{:S(2)}, u32[]{:S(2)}) %collective-permute-start.15) | collective-permute-done | bytes 786464 | tf_op jit(solution)/shard_map/ppermute | solution.py:385
  325.0 1.6 select_bitcast_fusion
  326.6 1.6 select_bitcast_fusion.1
  328.5 2.8 collective-permute-start.24
  331.3 1.6 broadcast_select_fusion.refs_12_
  332.8 7.4 %collective-permute-done.18 = bf16[2,64,3072]{2,1,0:T(8,128)(2,1)} collective-permute-done((bf16[2,64,3072]{2,1,0:T(8,128)(2,1)}, bf16[2,64,3072]{2,1,0:T(8,128)(2,1)}, u32[]{:S(2)}, u32[]{:S(2)}) %collective-permute-start.18) | collective-permute-done | bytes 786464 | tf_op jit(solution)/shard_map/ppermute | solution.py:385
  340.3 2.4 collective-permute-start.14
  343.9 2.2 collective-permute-start.19
  346.1 1.9 collective-permute-done.19.refs_13_
  348.0 10.0 %collective-permute-done.11.refs_7_ = bf16[256,3072]{1,0:T(8,128)(2,1)S(1)} collective-permute-done((bf16[256,3072]{1,0:T(8,128)(2,1)}, bf16[256,3072]{1,0:T(8,128)(2,1)S(1)}, u32[]{:S(2)}, u32[]{:S(2)}) %collective-permute-start.11) | collective-permute-done | bytes 1572896 | tf_op jit(solution)/shard_map/ppermute | solution.py:137
  360.7 4.6 %collective-permute-start.29 = (bf16[2,64,3072]{2,1,0:T(8,128)(2,1)}, bf16[2,64,3072]{2,1,0:T(8,128)(2,1)}, u32[]{:S(2)}, u32[]{:S(2)}) collective-permute-start(bf16[2,64,3072]{2,1,0:T(8,128)(2,1)} %collective-permute-done.18), channel_id=1, source_target_pairs={{8,0},{9,1},{10,2},{11,3},{12,4},{13,5},{14,6},{15,7},{16,8},{17,9... | collective-permute-start | bytes 2359304 | tf_op jit(solution)/shard_map/ppermute | solution.py:385
  365.2 1.5 collective-permute-start.28
  366.7 8.6 %collective-permute-done.21.refs_9_ = bf16[128,3072]{1,0:T(8,128)(2,1)S(1)} collective-permute-done((bf16[128,3072]{1,0:T(8,128)(2,1)S(1)}, bf16[128,3072]{1,0:T(8,128)(2,1)S(1)}, u32[]{:S(2)}, u32[]{:S(2)}) %collective-permute-start.21) | collective-permute-done | bytes 786464 | tf_op jit(solution)/shard_map/ppermute | solution.py:137
  377.2 23.3 %project.2 = (bf16[256,1024]{1,0:T(8,128)(2,1)}, bf16[256,1024]{1,0:T(8,128)(2,1)}, bf16[256,1024]{1,0:T(8,128)(2,1)}, bf16[256,1024]{1,0:T(8,128)(2,1)}) custom-call(s32[2]{0:T(128)} %pad_add_fusion.place_ref, bf16[256,3072]{1,0:T(8,128)(2,1)} %band.1.refs_0_, bf16[256,3072]{1,0:T(8,128)(2,1)} %collective-permute-done.3.refs_1_, ...), custom_call_target="tpu_custom_call" | custom-call | flops 12884901888 | bytes 27262976 | tf_op jit(solution)/shard_map/project/pallas_call | solution.py:302
  400.5 1.5 select_bitcast_fusion.2
  402.2 3.9 collective-permute-start.30
  407.3 1.5 collective-permute-start.27
  409.3 14.6 %project.3 = (bf16[256,512]{1,0:T(8,128)(2,1)}, bf16[256,512]{1,0:T(8,128)(2,1)}, bf16[256,512]{1,0:T(8,128)(2,1)}, bf16[256,512]{1,0:T(8,128)(2,1)}) custom-call(s32[2]{0:T(128)} %pad_add_fusion.place_ref, bf16[256,3072]{1,0:T(8,128)(2,1)} %band.1.refs_0_, bf16[256,3072]{1,0:T(8,128)(2,1)} %collective-permute-done.3.refs_1_, bf16[256,3072]{1,0:T(8,128)(2,1)} %copy-done.10, ...), custom_call_target="tpu_custom_call" | custom-call | flops 6442450944 | bytes 19922944 | tf_op jit(solution)/shard_map/project/pallas_call | solution.py:302
  425.1 1.5 collective-permute-start.33
  426.7 4.4 collective-permute-done.27.refs_3_
  431.1 5.6 %collective-permute-done.31.refs_5_ = bf16[256,512]{1,0:T(8,128)(2,1)S(1)} collective-permute-done((bf16[256,512]{1,0:T(8,128)(2,1)}, bf16[256,512]{1,0:T(8,128)(2,1)S(1)}, u32[]{:S(2)}, u32[]{:S(2)}) %collective-permute-start.31) | collective-permute-done | bytes 262176 | tf_op jit(solution)/shard_map/ppermute | solution.py:137
  437.8 4.5 %collective-permute-done.33.refs_7_ = bf16[256,512]{1,0:T(8,128)(2,1)S(1)} collective-permute-done((bf16[256,512]{1,0:T(8,128)(2,1)}, bf16[256,512]{1,0:T(8,128)(2,1)S(1)}, u32[]{:S(2)}, u32[]{:S(2)}) %collective-permute-start.33) | collective-permute-done | bytes 262176 | tf_op jit(solution)/shard_map/ppermute | solution.py:137
  443.1 4.3 assemble.1
  (99 shorter events, 26.3 us)
Async XLA Ops:
  4.8 109.6 %all-to-all-start = ((bf16[32,3,8,3072]{3,2,1,0:T(8,128)(2,1)}), bf16[32,3,8,3072]{3,2,1,0:T(8,128)(2,1)}, u32[]{:S(2)}, u32[]{:S(2)}) async-start(bf16[32,3,8,3072]{3,2,1,0:T(8,128)(2,1)} %copy_bitcast_fusion), calls=%async_computation | async-start | bytes 9437184 | tf_op jit(solution)/shard_map/all_to_all | solution.py:395
  13.1 5.7 %collective-permute-start = (bf16[2,256,3072]{2,1,0:T(8,128)(2,1)S(1)}, bf16[2,256,3072]{2,1,0:T(8,128)(2,1)S(1)}, u32[]{:S(2)}, u32[]{:S(2)}) collective-permute-start(bf16[2,256,3072]{2,1,0:T(8,128)(2,1)S(1)} %slice.39), channel_id=1, source_target_pairs={{0,1},{1,0},{2,3},{3,2},{4,5},{5,4},{6,7},{7,6},{8,9},{9,8},{10,11... | collective-permute-start | bytes 9437192 | tf_op jit(solution)/shard_map/ppermute | solution.py:388
  16.3 6.6 %copy-start = (bf16[2,3072,192]{1,2,0:T(8,128)(2,1)S(1)}, bf16[2,3072,192]{1,2,0:T(8,128)(2,1)}, u32[]{:S(2)}) copy-start(bf16[2,3072,192]{1,2,0:T(8,128)(2,1)} %param.6) | copy-start | bytes 7077892
  16.3 14.1 %collective-permute-start.1 = (bf16[256,3072]{1,0:T(8,128)(2,1)}, bf16[256,3072]{1,0:T(8,128)(2,1)}, u32[]{:S(2)}, u32[]{:S(2)}) collective-permute-start(bf16[256,3072]{1,0:T(8,128)(2,1)} %slice_bitcast_fusion.1), channel_id=1, source_target_pairs={{1,2},{3,4},{5,6},{7,8},{9,10},{11,12},{13,14},{15,16},{17,18},{19... | collective-permute-start | bytes 4718600 | tf_op jit(solution)/shard_map/ppermute | solution.py:392
  21.0 9.3 %collective-permute-start.2 = (bf16[256,3072]{1,0:T(8,128)(2,1)}, bf16[256,3072]{1,0:T(8,128)(2,1)}, u32[]{:S(2)}, u32[]{:S(2)}) collective-permute-start(bf16[256,3072]{1,0:T(8,128)(2,1)} %slice_bitcast_fusion), channel_id=1, source_target_pairs={{0,2},{2,4},{4,6},{6,8},{8,10},{10,12},{12,14},{14,16},{16,18},{18... | collective-permute-start | bytes 4718600 | tf_op jit(solution)/shard_map/ppermute | solution.py:393
  30.4 84.1 %copy-start.1 = (bf16[2,192,3072]{2,1,0:T(8,128)(2,1)S(1)}, bf16[2,192,3072]{2,1,0:T(8,128)(2,1)}, u32[]{:S(2)}) copy-start(bf16[2,192,3072]{2,1,0:T(8,128)(2,1)} %maximum_select_fusion.refs_10_) | copy-start | bytes 7077892
  45.0 145.5 %collective-permute-start.3 = (bf16[256,3072]{1,0:T(8,128)(2,1)}, bf16[256,3072]{1,0:T(8,128)(2,1)}, u32[]{:S(2)}, u32[]{:S(2)}) collective-permute-start(bf16[256,3072]{1,0:T(8,128)(2,1)} %band.1.refs_0_), channel_id=1, source_target_pairs={{0,2},{1,3},{2,0},{3,1},{4,6},{5,7},{6,4},{7,5},{8,10},{9,11},{10,... | collective-permute-start | bytes 4718600 | tf_op jit(solution)/shard_map/ppermute | solution.py:137
  115.8 75.9 %collective-permute-start.6 = (bf16[2,128,3072]{2,1,0:T(8,128)(2,1)}, bf16[2,128,3072]{2,1,0:T(8,128)(2,1)}, u32[]{:S(2)}, u32[]{:S(2)}) collective-permute-start(bf16[2,128,3072]{2,1,0:T(8,128)(2,1)} %slice.42), channel_id=1, source_target_pairs={{8,0},{9,1},{10,2},{11,3},{12,4},{13,5},{14,6},{15,7},{16,8},{17,9... | collective-permute-start | bytes 4718600 | tf_op jit(solution)/shard_map/ppermute | solution.py:385
  141.1 60.6 %collective-permute-start.5 = (bf16[2,128,3072]{2,1,0:T(8,128)(2,1)}, bf16[2,128,3072]{2,1,0:T(8,128)(2,1)}, u32[]{:S(2)}, u32[]{:S(2)}) collective-permute-start(bf16[2,128,3072]{2,1,0:T(8,128)(2,1)} %slice.42), channel_id=1, source_target_pairs={{0,8},{1,9},{2,10},{3,11},{4,12},{5,13},{6,14},{7,15},{8,16},{9,17... | collective-permute-start | bytes 4718600 | tf_op jit(solution)/shard_map/ppermute | solution.py:385
  154.4 107.1 %all-to-all-start.1 = ((bf16[32,8,3072]{2,1,0:T(8,128)(2,1)}), bf16[32,8,3072]{2,1,0:T(8,128)(2,1)}, u32[]{:S(2)}, u32[]{:S(2)}) async-start(bf16[32,8,3072]{2,1,0:T(8,128)(2,1)} %strided.1), calls=%async_computation.1 | async-start | bytes 3145728 | tf_op jit(solution)/shard_map/all_to_all | solution.py:403
  189.6 52.0 %collective-permute-start.4 = (bf16[256,3072]{1,0:T(8,128)(2,1)}, bf16[256,3072]{1,0:T(8,128)(2,1)S(1)}, u32[]{:S(2)}, u32[]{:S(2)}) collective-permute-start(bf16[256,3072]{1,0:T(8,128)(2,1)} %band.1.refs_0_), channel_id=1, source_target_pairs={{0,4},{1,5},{2,6},{3,7},{4,0},{5,1},{6,2},{7,3},{8,12},{9,13},{10,... | collective-permute-start | bytes 4718600 | tf_op jit(solution)/shard_map/ppermute | solution.py:137
  189.9 71.6 %collective-permute-start.9 = (bf16[2,192,3072]{2,1,0:T(8,128)(2,1)S(1)}, bf16[2,192,3072]{2,1,0:T(8,128)(2,1)}, u32[]{:S(2)}, u32[]{:S(2)}) collective-permute-start(bf16[2,192,3072]{2,1,0:T(8,128)(2,1)S(1)} %copy-done.1), channel_id=1, source_target_pairs={{0,1},{1,0},{2,3},{3,2},{4,5},{5,4},{6,7},{7,6},{8,9},{9,8},{10,11... | collective-permute-start | bytes 7077896 | tf_op jit(solution)/shard_map/ppermute | solution.py:388
  201.8 59.7 %collective-permute-start.12 = (bf16[2,128,3072]{2,1,0:T(8,128)(2,1)}, bf16[2,128,3072]{2,1,0:T(8,128)(2,1)}, u32[]{:S(2)}, u32[]{:S(2)}) collective-permute-start(bf16[2,128,3072]{2,1,0:T(8,128)(2,1)} %collective-permute-done.5), channel_id=1, source_target_pairs={{0,8},{1,9},{2,10},{3,11},{4,12},{5,13},{6,14},{7,15},{8,16},{9,17... | collective-permute-start | bytes 4718600 | tf_op jit(solution)/shard_map/ppermute | solution.py:385
  203.1 58.5 %collective-permute-start.13 = (bf16[2,128,3072]{2,1,0:T(8,128)(2,1)}, bf16[2,128,3072]{2,1,0:T(8,128)(2,1)}, u32[]{:S(2)}, u32[]{:S(2)}) collective-permute-start(bf16[2,128,3072]{2,1,0:T(8,128)(2,1)} %collective-permute-done.6), channel_id=1, source_target_pairs={{8,0},{9,1},{10,2},{11,3},{12,4},{13,5},{14,6},{15,7},{16,8},{17,9... | collective-permute-start | bytes 4718600 | tf_op jit(solution)/shard_map/ppermute | solution.py:385
  241.6 19.0 %copy-start.10 = (bf16[256,3072]{1,0:T(8,128)(2,1)}, bf16[256,3072]{1,0:T(8,128)(2,1)S(1)}, u32[]{:S(2)}) copy-start(bf16[256,3072]{1,0:T(8,128)(2,1)S(1)} %collective-permute-done.4.refs_2_) | copy-start | bytes 4718596
  241.6 18.9 %collective-permute-start.8 = (bf16[128,3072]{1,0:T(8,128)(2,1)S(1)}, bf16[128,3072]{1,0:T(8,128)(2,1)S(1)}, u32[]{:S(2)}, u32[]{:S(2)}) collective-permute-start(bf16[128,3072]{1,0:T(8,128)(2,1)S(1)} %slice.52), channel_id=1, source_target_pairs={{0,2},{1,3},{2,0},{3,1},{4,6},{5,7},{6,4},{7,5},{8,10},{9,11},{10,... | collective-permute-start | bytes 2359304 | tf_op jit(solution)/shard_map/ppermute | solution.py:137
  241.8 19.7 %collective-permute-start.7 = (bf16[128,3072]{1,0:T(8,128)(2,1)S(1)}, bf16[128,3072]{1,0:T(8,128)(2,1)}, u32[]{:S(2)}, u32[]{:S(2)}) collective-permute-start(bf16[128,3072]{1,0:T(8,128)(2,1)S(1)} %slice.51), channel_id=1, source_target_pairs={{0,4},{1,5},{2,6},{3,7},{4,0},{5,1},{6,2},{7,3},{8,12},{9,13},{10,... | collective-permute-start | bytes 2359304 | tf_op jit(solution)/shard_map/ppermute | solution.py:137
  261.5 62.5 %collective-permute-start.23 = (bf16[2,128,3072]{2,1,0:T(8,128)(2,1)}, bf16[2,128,3072]{2,1,0:T(8,128)(2,1)}, u32[]{:S(2)}, u32[]{:S(2)}) collective-permute-start(bf16[2,128,3072]{2,1,0:T(8,128)(2,1)} %collective-permute-done.12), channel_id=1, source_target_pairs={{0,8},{1,9},{2,10},{3,11},{4,12},{5,13},{6,14},{7,15},{8,16},{9,17... | collective-permute-start | bytes 4718600 | tf_op jit(solution)/shard_map/ppermute | solution.py:385
  262.9 26.7 %collective-permute-start.17 = (bf16[2,64,3072]{2,1,0:T(8,128)(2,1)S(1)}, bf16[2,64,3072]{2,1,0:T(8,128)(2,1)}, u32[]{:S(2)}, u32[]{:S(2)}) collective-permute-start(bf16[2,64,3072]{2,1,0:T(8,128)(2,1)S(1)} %slice.45), channel_id=1, source_target_pairs={{8,0},{9,1},{10,2},{11,3},{12,4},{13,5},{14,6},{15,7},{16,8},{17,9... | collective-permute-start | bytes 2359304 | tf_op jit(solution)/shard_map/ppermute | solution.py:385
  275.2 47.4 %collective-permute-start.15 = (bf16[2,64,3072]{2,1,0:T(8,128)(2,1)S(1)}, bf16[2,64,3072]{2,1,0:T(8,128)(2,1)}, u32[]{:S(2)}, u32[]{:S(2)}) collective-permute-start(bf16[2,64,3072]{2,1,0:T(8,128)(2,1)S(1)} %slice.45), channel_id=1, source_target_pairs={{0,8},{1,9},{2,10},{3,11},{4,12},{5,13},{6,14},{7,15},{8,16},{9,17... | collective-permute-start | bytes 2359304 | tf_op jit(solution)/shard_map/ppermute | solution.py:385
  276.5 50.1 %collective-permute-start.22 = (bf16[2,128,3072]{2,1,0:T(8,128)(2,1)}, bf16[2,128,3072]{2,1,0:T(8,128)(2,1)S(1)}, u32[]{:S(2)}, u32[]{:S(2)}) collective-permute-start(bf16[2,128,3072]{2,1,0:T(8,128)(2,1)} %collective-permute-done.13), channel_id=1, source_target_pairs={{8,0},{9,1},{10,2},{11,3},{12,4},{13,5},{14,6},{15,7},{16,8},{17,9... | collective-permute-start | bytes 4718600 | tf_op jit(solution)/shard_map/ppermute | solution.py:385
  289.6 50.7 %collective-permute-start.18 = (bf16[2,64,3072]{2,1,0:T(8,128)(2,1)}, bf16[2,64,3072]{2,1,0:T(8,128)(2,1)}, u32[]{:S(2)}, u32[]{:S(2)}) collective-permute-start(bf16[2,64,3072]{2,1,0:T(8,128)(2,1)} %collective-permute-done.17), channel_id=1, source_target_pairs={{8,0},{9,1},{10,2},{11,3},{12,4},{13,5},{14,6},{15,7},{16,8},{17,9... | collective-permute-start | bytes 2359304 | tf_op jit(solution)/shard_map/ppermute | solution.py:385
  322.6 20.0 %collective-permute-start.16 = (bf16[2,64,3072]{2,1,0:T(8,128)(2,1)}, bf16[2,64,3072]{2,1,0:T(8,128)(2,1)}, u32[]{:S(2)}, u32[]{:S(2)}) collective-permute-start(bf16[2,64,3072]{2,1,0:T(8,128)(2,1)} %collective-permute-done.15), channel_id=1, source_target_pairs={{0,8},{1,9},{2,10},{3,11},{4,12},{5,13},{6,14},{7,15},{8,16},{9,17... | collective-permute-start | bytes 2359304 | tf_op jit(solution)/shard_map/ppermute | solution.py:385
  323.9 34.1 %collective-permute-start.11 = (bf16[256,3072]{1,0:T(8,128)(2,1)}, bf16[256,3072]{1,0:T(8,128)(2,1)S(1)}, u32[]{:S(2)}, u32[]{:S(2)}) collective-permute-start(bf16[256,3072]{1,0:T(8,128)(2,1)} %bitcast.11.refs_5_), channel_id=1, source_target_pairs={{0,4},{1,5},{2,6},{3,7},{4,0},{5,1},{6,2},{7,3},{8,12},{9,13},{10,... | collective-permute-start | bytes 4718600 | tf_op jit(solution)/shard_map/ppermute | solution.py:137
  324.0 34.1 %collective-permute-start.10 = (bf16[256,3072]{1,0:T(8,128)(2,1)}, bf16[256,3072]{1,0:T(8,128)(2,1)S(1)}, u32[]{:S(2)}, u32[]{:S(2)}) collective-permute-start(bf16[256,3072]{1,0:T(8,128)(2,1)} %bitcast.11.refs_5_), channel_id=1, source_target_pairs={{0,2},{1,3},{2,0},{3,1},{4,6},{5,7},{6,4},{7,5},{8,10},{9,11},{10,... | collective-permute-start | bytes 4718600 | tf_op jit(solution)/shard_map/ppermute | solution.py:137
  328.5 48.7 %collective-permute-start.24 = (bf16[2,2,128,3072]{3,2,1,0:T(8,128)(2,1)S(1)}, bf16[2,2,128,3072]{3,2,1,0:T(8,128)(2,1)}, u32[]{:S(2)}, u32[]{:S(2)}) collective-permute-start(bf16[2,2,128,3072]{3,2,1,0:T(8,128)(2,1)S(1)} %pad_maximum_fusion.refs_14_), channel_id=1, source_target_pairs={{0,1},{1,0},{2,3},{3,2},{4,5},{5,4},{6,7},{7,6},{8,9},{9,8},{10,11... | collective-permute-start | bytes 9437192 | tf_op jit(solution)/shard_map/ppermute | solution.py:388
  332.8 25.3 %copy-start.4 = (bf16[2,128,3072]{2,1,0:T(8,128)(2,1)}, bf16[2,128,3072]{2,1,0:T(8,128)(2,1)S(1)}, u32[]{:S(2)}) copy-start(bf16[2,128,3072]{2,1,0:T(8,128)(2,1)S(1)} %broadcast_select_fusion.refs_12_) | copy-start | bytes 4718596
  340.3 17.8 %collective-permute-start.14 = (bf16[2,128,3072]{2,1,0:T(8,128)(2,1)S(1)}, bf16[2,128,3072]{2,1,0:T(8,128)(2,1)S(1)}, u32[]{:S(2)}, u32[]{:S(2)}) collective-permute-start(bf16[2,128,3072]{2,1,0:T(8,128)(2,1)S(1)} %broadcast_select_fusion.refs_12_), channel_id=1, source_target_pairs={{0,1},{1,0},{2,3},{3,2},{4,5},{5,4},{6,7},{7,6},{8,9},{9,8},{10,11... | collective-permute-start | bytes 4718600 | tf_op jit(solution)/shard_map/ppermute | solution.py:388
  343.9 14.3 %copy-start.6 = (bf16[2,64,3072]{2,1,0:T(8,128)(2,1)}, bf16[2,64,3072]{2,1,0:T(8,128)(2,1)S(1)}, u32[]{:S(2)}) copy-start(bf16[2,64,3072]{2,1,0:T(8,128)(2,1)S(1)} %broadcast_select_fusion.1.refs_12_) | copy-start | bytes 2359300
  343.9 4.1 collective-permute-start.19
  348.0 10.2 %copy-start.19 = (bf16[2,64,3072]{2,1,0:T(8,128)(2,1)}, bf16[2,64,3072]{2,1,0:T(8,128)(2,1)S(1)}, u32[]{:S(2)}) copy-start(bf16[2,64,3072]{2,1,0:T(8,128)(2,1)S(1)} %collective-permute-done.19.refs_13_) | copy-start | bytes 2359300
  358.1 17.2 %copy-start.12 = (bf16[256,3072]{1,0:T(8,128)(2,1)}, bf16[256,3072]{1,0:T(8,128)(2,1)S(1)}, u32[]{:S(2)}) copy-start(bf16[256,3072]{1,0:T(8,128)(2,1)S(1)} %collective-permute-done.10.refs_6_) | copy-start | bytes 4718596
  358.1 17.2 %copy-start.17 = (bf16[2,128,3072]{2,1,0:T(8,128)(2,1)}, bf16[2,128,3072]{2,1,0:T(8,128)(2,1)S(1)}, u32[]{:S(2)}) copy-start(bf16[2,128,3072]{2,1,0:T(8,128)(2,1)S(1)} %collective-permute-done.14.refs_13_) | copy-start | bytes 4718596
  359.2 16.1 %collective-permute-start.21 = (bf16[128,3072]{1,0:T(8,128)(2,1)S(1)}, bf16[128,3072]{1,0:T(8,128)(2,1)S(1)}, u32[]{:S(2)}, u32[]{:S(2)}) collective-permute-start(bf16[128,3072]{1,0:T(8,128)(2,1)S(1)} %slice.47), channel_id=1, source_target_pairs={{0,2},{1,3},{2,0},{3,1},{4,6},{5,7},{6,4},{7,5},{8,10},{9,11},{10,... | collective-permute-start | bytes 2359304 | tf_op jit(solution)/shard_map/ppermute | solution.py:137
  359.8 15.5 %collective-permute-start.20 = (bf16[128,3072]{1,0:T(8,128)(2,1)S(1)}, bf16[128,3072]{1,0:T(8,128)(2,1)S(1)}, u32[]{:S(2)}, u32[]{:S(2)}) collective-permute-start(bf16[128,3072]{1,0:T(8,128)(2,1)S(1)} %slice.46), channel_id=1, source_target_pairs={{0,4},{1,5},{2,6},{3,7},{4,0},{5,1},{6,2},{7,3},{8,12},{9,13},{10,... | collective-permute-start | bytes 2359304 | tf_op jit(solution)/shard_map/ppermute | solution.py:137
  360.7 39.8 %collective-permute-start.29 = (bf16[2,64,3072]{2,1,0:T(8,128)(2,1)}, bf16[2,64,3072]{2,1,0:T(8,128)(2,1)}, u32[]{:S(2)}, u32[]{:S(2)}) collective-permute-start(bf16[2,64,3072]{2,1,0:T(8,128)(2,1)} %collective-permute-done.18), channel_id=1, source_target_pairs={{8,0},{9,1},{10,2},{11,3},{12,4},{13,5},{14,6},{15,7},{16,8},{17,9... | collective-permute-start | bytes 2359304 | tf_op jit(solution)/shard_map/ppermute | solution.py:385
  365.2 35.3 %collective-permute-start.28 = (bf16[2,64,3072]{2,1,0:T(8,128)(2,1)}, bf16[2,64,3072]{2,1,0:T(8,128)(2,1)}, u32[]{:S(2)}, u32[]{:S(2)}) collective-permute-start(bf16[2,64,3072]{2,1,0:T(8,128)(2,1)} %collective-permute-done.16), channel_id=1, source_target_pairs={{0,8},{1,9},{2,10},{3,11},{4,12},{5,13},{6,14},{7,15},{8,16},{9,17... | collective-permute-start | bytes 2359304 | tf_op jit(solution)/shard_map/ppermute | solution.py:385
  402.2 7.1 %copy-start.5 = (bf16[2,2,64,3072]{3,2,1,0:T(8,128)(2,1)}, bf16[2,2,64,3072]{3,2,1,0:T(8,128)(2,1)S(1)}, u32[]{:S(2)}) copy-start(bf16[2,2,64,3072]{3,2,1,0:T(8,128)(2,1)S(1)} %pad_maximum_fusion.1.refs_14_) | copy-start | bytes 4718596
  402.2 7.1 %collective-permute-start.30 = (bf16[2,2,64,3072]{3,2,1,0:T(8,128)(2,1)S(1)}, bf16[2,2,64,3072]{3,2,1,0:T(8,128)(2,1)}, u32[]{:S(2)}, u32[]{:S(2)}) collective-permute-start(bf16[2,2,64,3072]{3,2,1,0:T(8,128)(2,1)S(1)} %pad_maximum_fusion.1.refs_14_), channel_id=1, source_target_pairs={{0,1},{1,0},{2,3},{3,2},{4,5},{5,4},{6,7},{7,6},{8,9},{9,8},{10,11... | collective-permute-start | bytes 4718600 | tf_op jit(solution)/shard_map/ppermute | solution.py:388
  406.2 19.0 %collective-permute-start.25 = (bf16[256,1024]{1,0:T(8,128)(2,1)}, bf16[256,1024]{1,0:T(8,128)(2,1)S(1)}, u32[]{:S(2)}, u32[]{:S(2)}) collective-permute-start(bf16[256,1024]{1,0:T(8,128)(2,1)} %get-tuple-element.59), channel_id=1, source_target_pairs={{0,2},{1,3},{2,0},{3,1},{4,6},{5,7},{6,4},{7,5},{8,10},{9,11},{10,... | collective-permute-start | bytes 1572872 | tf_op jit(solution)/shard_map/ppermute | solution.py:137
  406.8 19.9 %collective-permute-start.26 = (bf16[256,1024]{1,0:T(8,128)(2,1)}, bf16[256,1024]{1,0:T(8,128)(2,1)S(1)}, u32[]{:S(2)}, u32[]{:S(2)}) collective-permute-start(bf16[256,1024]{1,0:T(8,128)(2,1)} %get-tuple-element.60), channel_id=1, source_target_pairs={{0,4},{1,5},{2,6},{3,7},{4,0},{5,1},{6,2},{7,3},{8,12},{9,13},{10,... | collective-permute-start | bytes 1572872 | tf_op jit(solution)/shard_map/ppermute | solution.py:137
  407.3 23.8 %collective-permute-start.27 = (bf16[256,1024]{1,0:T(8,128)(2,1)}, bf16[256,1024]{1,0:T(8,128)(2,1)S(1)}, u32[]{:S(2)}, u32[]{:S(2)}) collective-permute-start(bf16[256,1024]{1,0:T(8,128)(2,1)} %get-tuple-element.61), channel_id=1, source_target_pairs={{0,6},{1,7},{2,4},{3,5},{4,2},{5,3},{6,0},{7,1},{8,14},{9,15},{10,... | collective-permute-start | bytes 1572872 | tf_op jit(solution)/shard_map/ppermute | solution.py:137
  423.9 12.7 %collective-permute-start.31 = (bf16[256,512]{1,0:T(8,128)(2,1)}, bf16[256,512]{1,0:T(8,128)(2,1)S(1)}, u32[]{:S(2)}, u32[]{:S(2)}) collective-permute-start(bf16[256,512]{1,0:T(8,128)(2,1)} %get-tuple-element.72), channel_id=1, source_target_pairs={{0,2},{1,3},{2,0},{3,1},{4,6},{5,7},{6,4},{7,5},{8,10},{9,11},{10,... | collective-permute-start | bytes 786440 | tf_op jit(solution)/shard_map/ppermute | solution.py:137
  424.6 13.2 %collective-permute-start.32 = (bf16[256,512]{1,0:T(8,128)(2,1)}, bf16[256,512]{1,0:T(8,128)(2,1)S(1)}, u32[]{:S(2)}, u32[]{:S(2)}) collective-permute-start(bf16[256,512]{1,0:T(8,128)(2,1)} %get-tuple-element.73), channel_id=1, source_target_pairs={{0,4},{1,5},{2,6},{3,7},{4,0},{5,1},{6,2},{7,3},{8,12},{9,13},{10,... | collective-permute-start | bytes 786440 | tf_op jit(solution)/shard_map/ppermute | solution.py:137
  425.1 17.2 %copy-start.7 = (bf16[256,1024]{1,0:T(8,128)(2,1)}, bf16[256,1024]{1,0:T(8,128)(2,1)S(1)}, u32[]{:S(2)}) copy-start(bf16[256,1024]{1,0:T(8,128)(2,1)S(1)} %collective-permute-done.25.refs_1_) | copy-start | bytes 1572868
  425.1 17.2 %collective-permute-start.33 = (bf16[256,512]{1,0:T(8,128)(2,1)}, bf16[256,512]{1,0:T(8,128)(2,1)S(1)}, u32[]{:S(2)}, u32[]{:S(2)}) collective-permute-start(bf16[256,512]{1,0:T(8,128)(2,1)} %get-tuple-element.74), channel_id=1, source_target_pairs={{0,6},{1,7},{2,4},{3,5},{4,2},{5,3},{6,0},{7,1},{8,14},{9,15},{10,... | collective-permute-start | bytes 786440 | tf_op jit(solution)/shard_map/ppermute | solution.py:137
  426.7 15.7 %copy-start.8 = (bf16[256,1024]{1,0:T(8,128)(2,1)}, bf16[256,1024]{1,0:T(8,128)(2,1)S(1)}, u32[]{:S(2)}) copy-start(bf16[256,1024]{1,0:T(8,128)(2,1)S(1)} %collective-permute-done.26.refs_2_) | copy-start | bytes 1572868
  431.1 11.3 %copy-start.9 = (bf16[256,1024]{1,0:T(8,128)(2,1)}, bf16[256,1024]{1,0:T(8,128)(2,1)S(1)}, u32[]{:S(2)}) copy-start(bf16[256,1024]{1,0:T(8,128)(2,1)S(1)} %collective-permute-done.27.refs_3_) | copy-start | bytes 1572868
  (10 other events, 22.8 us)

commit v5 on v4

--- a/solution.py
+++ b/solution.py
@@ -323,14 +323,17 @@
     )(place, *band_parts, *stride_parts, *slots)
 
 
-def assemble_kernel(cuts, mine_ref, *refs):
+def assemble_kernel(outer, cuts, mine_ref, *refs):
     out_ref = refs[-1]
     span = sum(cut[1] for cut in cuts)
-    for step in range(MID):
-        base = (mine_ref[0] ^ step) * span
-        for chunk, size, source, target in cuts:
-            at = pl.multiple_of(base + target, 128)
-            out_ref[:, pl.ds(at, size)] = refs[chunk * MID + step][:, source : source + size]
+    for z in range(outer):
+        for step in range(MID):
+            base = z * MID * span + (mine_ref[0] ^ step) * span
+            for chunk, size, source, target in cuts:
+                at = pl.multiple_of(base + target, 128)
+                block = refs[chunk * MID + step]
+                low = z * (block.shape[1] // outer) + source
+                out_ref[:, pl.ds(at, size)] = block[:, low : low + size]
 
 
 def assemble(mine, chunks, outer):
@@ -347,15 +350,16 @@
         picked = [lax.dynamic_index_in_dim(stacked, mine ^ m, 0, keepdims=False) for m in range(MID)]
         pieces = [picked[m][:, z * span : (z + 1) * span] for z in range(outer) for m in range(MID)]
         return jnp.concatenate(pieces, axis=1)
-    specs = [pl.BlockSpec((tokens, width), lambda z, mine: (0, z)) for width in widths for _ in range(MID)]
+    rows = tokens // 2
+    specs = [pl.BlockSpec((rows, outer * width), lambda r, mine: (r, 0)) for width in widths for _ in range(MID)]
     return pl.pallas_call(
-        functools.partial(assemble_kernel, cuts),
+        functools.partial(assemble_kernel, outer, cuts),
         out_shape=jax.ShapeDtypeStruct((tokens, MID * outer * span), jnp.bfloat16),
         grid_spec=pltpu.PrefetchScalarGridSpec(
             num_scalar_prefetch=1,
-            grid=(outer,),
+            grid=(2,),
             in_specs=specs,
-            out_specs=pl.BlockSpec((tokens, MID * span), lambda z, mine: (0, z)),
+            out_specs=pl.BlockSpec((rows, MID * outer * span), lambda r, mine: (r, 0)),
         ),
         name="assemble",
     )(mine.reshape(1), *[block for chunk in chunks for block in chunk])

time: 454 us -> 453 us (level)
  no operation moved by 1% of the time
where the time goes in v5:
time: 453 us; the launch traced here: 446 us
  starting transfers between devices  199 us (44%)
  waiting for transfers between devices  144 us (32%)
  Pallas kernels  66.4 us (15%)
  local copies, waits for them, and re-layouts  22.4 us (5%)
  other arithmetic  12.8 us (3%)
    ppermute x14, waiting for transfers between devices, moved(): lax.ppermute(array, 'seq', [(i, i ^ step * CORES) for i in range(size)])  76.3 us
    ppermute x12, starting transfers between devices, along(): lax.ppermute(array, 'seq', [(i, i + plane) for i in range(size) if 0 <= i...  73.3 us
    ppermute x14, starting transfers between devices, moved(): lax.ppermute(array, 'seq', [(i, i ^ step * CORES) for i in range(size)])  68.4 us
    ppermute x12, waiting for transfers between devices, along(): lax.ppermute(array, 'seq', [(i, i + plane) for i in range(size) if 0 <= i...  54.4 us
    pallas_call x2, Pallas kernels, project_slots(): pl.pallas_call(functools.partial(slots_kernel, low, rows), out_shape=[jax...  37.9 us
    all_to_all x1, starting transfers between devices, per_device(): lax.all_to_all(column_out, 'seq', split_axis=0, concat_axis=0, tiled=True)  35.2 us
    pallas_call x1, Pallas kernels, band_heads(): pl.pallas_call(functools.partial(band_kernel, heads), out_shape=jax.Shape...  14.6 us
    ppermute x6, starting transfers between devices, twin_of(): return lax.ppermute(array, 'seq', [(i, i ^ 1) for i in range(size)])  12.4 us
  transfers between devices with their start and end apart: 36, of which 17 were waited for; matrix products, arithmetic and copies ran while one was open for 5% of the time, Pallas kernels for 14%

profile of v5, /device:TPU:31, one launch (start us, length us, event | category | flops | bytes accessed | tf_op | source)
XLA Modules:
  0.0 446.4 jit_solution(7145125663623292396)
XLA Ops:
  0.0 4.8 %copy_bitcast_fusion = bf16[32,3,8,3072]{3,2,1,0:T(8,128)(2,1)} fusion(bf16[3,256,3072]{2,1,0:T(8,128)(2,1)} %param.5), kind=kLoop, calls=%fused_computation | loop fusion | bytes 9437184 | tf_op jit(solution)/shard_map/transpose | solution.py:398
  4.8 6.2 %all-to-all-start = ((bf16[32,3,8,3072]{3,2,1,0:T(8,128)(2,1)}), bf16[32,3,8,3072]{3,2,1,0:T(8,128)(2,1)}, u32[]{:S(2)}, u32[]{:S(2)}) async-start(bf16[32,3,8,3072]{3,2,1,0:T(8,128)(2,1)} %copy_bitcast_fusion), calls=%async_computation | async-start | bytes 9437184 | tf_op jit(solution)/shard_map/all_to_all | solution.py:399
  11.0 2.1 slice.39
  13.6 2.7 slice_bitcast_fusion.1
  16.3 1.9 collective-permute-start.1
  18.9 1.4 slice_bitcast_fusion
  21.0 1.8 collective-permute-start.2
  26.7 3.7 maximum_select_fusion.refs_10_
  30.4 14.6 %band.1.refs_0_ = bf16[256,3072]{1,0:T(8,128)(2,1)} custom-call(s32[2]{0:T(128)} %pad_add_fusion.1.joined_ref, bf16[3,256,3072]{2,1,0:T(8,128)(2,1)} %own_ref.1, bf16[2,256,3072]{2,1,0:T(8,128)(2,1)} %copy-done.2, bf16[256,3072]{1,0:T(8,128)(2,1)} %collective-permute-done.1.keys_ref, bf16[256,3072]{1,0:T(8,128)(2,1)} %collective-permute-done.2.values_ref), custom_call_target="tpu_custom_call" | custom-call | flops 1610612736 | bytes 9437184 | tf_op jit(solution)/shard_map/band/pallas_call | solution.py:56
  45.0 59.3 %collective-permute-start.3 = (bf16[256,3072]{1,0:T(8,128)(2,1)}, bf16[256,3072]{1,0:T(8,128)(2,1)}, u32[]{:S(2)}, u32[]{:S(2)}) collective-permute-start(bf16[256,3072]{1,0:T(8,128)(2,1)} %band.1.refs_0_), channel_id=1, source_target_pairs={{0,2},{1,3},{2,0},{3,1},{4,6},{5,7},{6,4},{7,5},{8,10},{9,11},{10,... | collective-permute-start | bytes 4718600 | tf_op jit(solution)/shard_map/ppermute | solution.py:137
  104.3 10.2 %all-to-all-done.qkv_ref = bf16[32,3,8,3072]{3,2,1,0:T(8,128)(2,1)} async-done(((bf16[32,3,8,3072]{3,2,1,0:T(8,128)(2,1)}), bf16[32,3,8,3072]{3,2,1,0:T(8,128)(2,1)}, u32[]{:S(2)}, u32[]{:S(2)}) %all-to-all-start) | async-done | bytes 4718624 | tf_op jit(solution)/shard_map/all_to_all | solution.py:399
  114.5 1.3 slice.42
  115.8 25.3 %collective-permute-start.6 = (bf16[2,128,3072]{2,1,0:T(8,128)(2,1)}, bf16[2,128,3072]{2,1,0:T(8,128)(2,1)}, u32[]{:S(2)}, u32[]{:S(2)}) collective-permute-start(bf16[2,128,3072]{2,1,0:T(8,128)(2,1)} %slice.42), channel_id=1, source_target_pairs={{8,0},{9,1},{10,2},{11,3},{12,4},{13,5},{14,6},{15,7},{16,8},{17,9... | collective-permute-start | bytes 4718600 | tf_op jit(solution)/shard_map/ppermute | solution.py:389
  143.9 10.5 %strided.1 = bf16[32,8,3072]{2,1,0:T(8,128)(2,1)} custom-call(s32[256,1]{1,0:T(8,128)} %broadcast_in_dim_reshape.8.doc_row_ref, s32[1,256]{1,0:T(1,128)} %broadcast_in_dim_reshape.7.doc_col_ref, bf16[32,3,8,3072]{3,2,1,0:T(8,128)(2,1)} %all-to-all-done.qkv_ref), custom_call_target="tpu_custom_call" | custom-call | flops 805306368 | bytes 6291456 | tf_op jit(solution)/shard_map/strided/pallas_call | solution.py:115
  154.4 35.2 %all-to-all-start.1 = ((bf16[32,8,3072]{2,1,0:T(8,128)(2,1)}), bf16[32,8,3072]{2,1,0:T(8,128)(2,1)}, u32[]{:S(2)}, u32[]{:S(2)}) async-start(bf16[32,8,3072]{2,1,0:T(8,128)(2,1)} %strided.1), calls=%async_computation.1 | async-start | bytes 3145728 | tf_op jit(solution)/shard_map/all_to_all | solution.py:407
  191.7 10.0 %collective-permute-done.5 = bf16[2,128,3072]{2,1,0:T(8,128)(2,1)} collective-permute-done((bf16[2,128,3072]{2,1,0:T(8,128)(2,1)}, bf16[2,128,3072]{2,1,0:T(8,128)(2,1)}, u32[]{:S(2)}, u32[]{:S(2)}) %collective-permute-start.5) | collective-permute-done | bytes 1572896 | tf_op jit(solution)/shard_map/ppermute | solution.py:389
  203.1 14.0 %collective-permute-start.13 = (bf16[2,128,3072]{2,1,0:T(8,128)(2,1)}, bf16[2,128,3072]{2,1,0:T(8,128)(2,1)}, u32[]{:S(2)}, u32[]{:S(2)}) collective-permute-start(bf16[2,128,3072]{2,1,0:T(8,128)(2,1)} %collective-permute-done.6), channel_id=1, source_target_pairs={{8,0},{9,1},{10,2},{11,3},{12,4},{13,5},{14,6},{15,7},{16,8},{17,9... | collective-permute-start | bytes 4718600 | tf_op jit(solution)/shard_map/ppermute | solution.py:389
  217.1 24.5 %collective-permute-done.4.refs_2_ = bf16[256,3072]{1,0:T(8,128)(2,1)S(1)} collective-permute-done((bf16[256,3072]{1,0:T(8,128)(2,1)}, bf16[256,3072]{1,0:T(8,128)(2,1)S(1)}, u32[]{:S(2)}, u32[]{:S(2)}) %collective-permute-start.4) | collective-permute-done | bytes 1572896 | tf_op jit(solution)/shard_map/ppermute | solution.py:137
  241.8 1.3 collective-permute-start.7
  243.1 17.4 %collective-permute-done.8.refs_4_ = bf16[128,3072]{1,0:T(8,128)(2,1)S(1)} collective-permute-done((bf16[128,3072]{1,0:T(8,128)(2,1)S(1)}, bf16[128,3072]{1,0:T(8,128)(2,1)S(1)}, u32[]{:S(2)}, u32[]{:S(2)}) %collective-permute-start.8) | collective-permute-done | bytes 786464 | tf_op jit(solution)/shard_map/ppermute | solution.py:137
  261.5 1.3 collective-permute-start.23
  262.9 12.3 %collective-permute-start.17 = (bf16[2,64,3072]{2,1,0:T(8,128)(2,1)S(1)}, bf16[2,64,3072]{2,1,0:T(8,128)(2,1)}, u32[]{:S(2)}, u32[]{:S(2)}) collective-permute-start(bf16[2,64,3072]{2,1,0:T(8,128)(2,1)S(1)} %slice.45), channel_id=1, source_target_pairs={{8,0},{9,1},{10,2},{11,3},{12,4},{13,5},{14,6},{15,7},{16,8},{17,9... | collective-permute-start | bytes 2359304 | tf_op jit(solution)/shard_map/ppermute | solution.py:389
  276.5 4.1 collective-permute-start.22
  280.6 9.0 %collective-permute-done.17 = bf16[2,64,3072]{2,1,0:T(8,128)(2,1)} collective-permute-done((bf16[2,64,3072]{2,1,0:T(8,128)(2,1)S(1)}, bf16[2,64,3072]{2,1,0:T(8,128)(2,1)}, u32[]{:S(2)}, u32[]{:S(2)}) %collective-permute-start.17) | collective-permute-done | bytes 786464 | tf_op jit(solution)/shard_map/ppermute | solution.py:389
  289.6 5.1 %collective-permute-start.18 = (bf16[2,64,3072]{2,1,0:T(8,128)(2,1)}, bf16[2,64,3072]{2,1,0:T(8,128)(2,1)}, u32[]{:S(2)}, u32[]{:S(2)}) collective-permute-start(bf16[2,64,3072]{2,1,0:T(8,128)(2,1)} %collective-permute-done.17), channel_id=1, source_target_pairs={{8,0},{9,1},{10,2},{11,3},{12,4},{13,5},{14,6},{15,7},{16,8},{17,9... | collective-permute-start | bytes 2359304 | tf_op jit(solution)/shard_map/ppermute | solution.py:389
  294.7 28.0 %collective-permute-done.15 = bf16[2,64,3072]{2,1,0:T(8,128)(2,1)} collective-permute-done((bf16[2,64,3072]{2,1,0:T(8,128)(2,1)S(1)}, bf16[2,64,3072]{2,1,0:T(8,128)(2,1)}, u32[]{:S(2)}, u32[]{:S(2)}) %collective-permute-start.15) | collective-permute-done | bytes 786464 | tf_op jit(solution)/shard_map/ppermute | solution.py:389
  325.0 1.6 select_bitcast_fusion
  326.6 1.6 select_bitcast_fusion.1
  328.5 2.8 collective-permute-start.24
  331.3 1.6 broadcast_select_fusion.refs_12_
  332.8 7.4 %collective-permute-done.18 = bf16[2,64,3072]{2,1,0:T(8,128)(2,1)} collective-permute-done((bf16[2,64,3072]{2,1,0:T(8,128)(2,1)}, bf16[2,64,3072]{2,1,0:T(8,128)(2,1)}, u32[]{:S(2)}, u32[]{:S(2)}) %collective-permute-start.18) | collective-permute-done | bytes 786464 | tf_op jit(solution)/shard_map/ppermute | solution.py:389
  340.3 2.4 collective-permute-start.14
  343.9 2.2 collective-permute-start.19
  346.1 1.9 collective-permute-done.19.refs_13_
  348.0 10.0 %collective-permute-done.11.refs_7_ = bf16[256,3072]{1,0:T(8,128)(2,1)S(1)} collective-permute-done((bf16[256,3072]{1,0:T(8,128)(2,1)}, bf16[256,3072]{1,0:T(8,128)(2,1)S(1)}, u32[]{:S(2)}, u32[]{:S(2)}) %collective-permute-start.11) | collective-permute-done | bytes 1572896 | tf_op jit(solution)/shard_map/ppermute | solution.py:137
  360.7 4.6 %collective-permute-start.29 = (bf16[2,64,3072]{2,1,0:T(8,128)(2,1)}, bf16[2,64,3072]{2,1,0:T(8,128)(2,1)}, u32[]{:S(2)}, u32[]{:S(2)}) collective-permute-start(bf16[2,64,3072]{2,1,0:T(8,128)(2,1)} %collective-permute-done.18), channel_id=1, source_target_pairs={{8,0},{9,1},{10,2},{11,3},{12,4},{13,5},{14,6},{15,7},{16,8},{17,9... | collective-permute-start | bytes 2359304 | tf_op jit(solution)/shard_map/ppermute | solution.py:389
  365.2 1.5 collective-permute-start.28
  366.7 8.6 %collective-permute-done.21.refs_9_ = bf16[128,3072]{1,0:T(8,128)(2,1)S(1)} collective-permute-done((bf16[128,3072]{1,0:T(8,128)(2,1)S(1)}, bf16[128,3072]{1,0:T(8,128)(2,1)S(1)}, u32[]{:S(2)}, u32[]{:S(2)}) %collective-permute-start.21) | collective-permute-done | bytes 786464 | tf_op jit(solution)/shard_map/ppermute | solution.py:137
  377.2 23.3 %project.2 = (bf16[256,1024]{1,0:T(8,128)(2,1)}, bf16[256,1024]{1,0:T(8,128)(2,1)}, bf16[256,1024]{1,0:T(8,128)(2,1)}, bf16[256,1024]{1,0:T(8,128)(2,1)}) custom-call(s32[2]{0:T(128)} %pad_add_fusion.place_ref, bf16[256,3072]{1,0:T(8,128)(2,1)} %band.1.refs_0_, bf16[256,3072]{1,0:T(8,128)(2,1)} %collective-permute-done.3.refs_1_, ...), custom_call_target="tpu_custom_call" | custom-call | flops 12884901888 | bytes 27262976 | tf_op jit(solution)/shard_map/project/pallas_call | solution.py:302
  400.5 1.5 select_bitcast_fusion.2
  402.2 3.9 collective-permute-start.30
  407.3 1.5 collective-permute-start.27
  409.3 14.6 %project.3 = (bf16[256,512]{1,0:T(8,128)(2,1)}, bf16[256,512]{1,0:T(8,128)(2,1)}, bf16[256,512]{1,0:T(8,128)(2,1)}, bf16[256,512]{1,0:T(8,128)(2,1)}) custom-call(s32[2]{0:T(128)} %pad_add_fusion.place_ref, bf16[256,3072]{1,0:T(8,128)(2,1)} %band.1.refs_0_, bf16[256,3072]{1,0:T(8,128)(2,1)} %collective-permute-done.3.refs_1_, bf16[256,3072]{1,0:T(8,128)(2,1)} %copy-done.10, ...), custom_call_target="tpu_custom_call" | custom-call | flops 6442450944 | bytes 19922944 | tf_op jit(solution)/shard_map/project/pallas_call | solution.py:302
  425.1 1.5 collective-permute-start.33
  426.7 4.4 collective-permute-done.27.refs_3_
  431.1 5.6 %collective-permute-done.31.refs_5_ = bf16[256,512]{1,0:T(8,128)(2,1)S(1)} collective-permute-done((bf16[256,512]{1,0:T(8,128)(2,1)}, bf16[256,512]{1,0:T(8,128)(2,1)S(1)}, u32[]{:S(2)}, u32[]{:S(2)}) %collective-permute-start.31) | collective-permute-done | bytes 262176 | tf_op jit(solution)/shard_map/ppermute | solution.py:137
  437.8 4.5 %collective-permute-done.33.refs_7_ = bf16[256,512]{1,0:T(8,128)(2,1)S(1)} collective-permute-done((bf16[256,512]{1,0:T(8,128)(2,1)}, bf16[256,512]{1,0:T(8,128)(2,1)S(1)}, u32[]{:S(2)}, u32[]{:S(2)}) %collective-permute-start.33) | collective-permute-done | bytes 262176 | tf_op jit(solution)/shard_map/ppermute | solution.py:137
  443.1 3.4 assemble.1
  (99 shorter events, 26.3 us)
Async XLA Ops:
  4.8 109.6 %all-to-all-start = ((bf16[32,3,8,3072]{3,2,1,0:T(8,128)(2,1)}), bf16[32,3,8,3072]{3,2,1,0:T(8,128)(2,1)}, u32[]{:S(2)}, u32[]{:S(2)}) async-start(bf16[32,3,8,3072]{3,2,1,0:T(8,128)(2,1)} %copy_bitcast_fusion), calls=%async_computation | async-start | bytes 9437184 | tf_op jit(solution)/shard_map/all_to_all | solution.py:399
  13.1 5.7 %collective-permute-start = (bf16[2,256,3072]{2,1,0:T(8,128)(2,1)S(1)}, bf16[2,256,3072]{2,1,0:T(8,128)(2,1)S(1)}, u32[]{:S(2)}, u32[]{:S(2)}) collective-permute-start(bf16[2,256,3072]{2,1,0:T(8,128)(2,1)S(1)} %slice.39), channel_id=1, source_target_pairs={{0,1},{1,0},{2,3},{3,2},{4,5},{5,4},{6,7},{7,6},{8,9},{9,8},{10,11... | collective-permute-start | bytes 9437192 | tf_op jit(solution)/shard_map/ppermute | solution.py:392
  16.3 6.6 %copy-start = (bf16[2,3072,192]{1,2,0:T(8,128)(2,1)S(1)}, bf16[2,3072,192]{1,2,0:T(8,128)(2,1)}, u32[]{:S(2)}) copy-start(bf16[2,3072,192]{1,2,0:T(8,128)(2,1)} %param.6) | copy-start | bytes 7077892
  16.3 14.1 %collective-permute-start.1 = (bf16[256,3072]{1,0:T(8,128)(2,1)}, bf16[256,3072]{1,0:T(8,128)(2,1)}, u32[]{:S(2)}, u32[]{:S(2)}) collective-permute-start(bf16[256,3072]{1,0:T(8,128)(2,1)} %slice_bitcast_fusion.1), channel_id=1, source_target_pairs={{1,2},{3,4},{5,6},{7,8},{9,10},{11,12},{13,14},{15,16},{17,18},{19... | collective-permute-start | bytes 4718600 | tf_op jit(solution)/shard_map/ppermute | solution.py:396
  21.0 9.3 %collective-permute-start.2 = (bf16[256,3072]{1,0:T(8,128)(2,1)}, bf16[256,3072]{1,0:T(8,128)(2,1)}, u32[]{:S(2)}, u32[]{:S(2)}) collective-permute-start(bf16[256,3072]{1,0:T(8,128)(2,1)} %slice_bitcast_fusion), channel_id=1, source_target_pairs={{0,2},{2,4},{4,6},{6,8},{8,10},{10,12},{12,14},{14,16},{16,18},{18... | collective-permute-start | bytes 4718600 | tf_op jit(solution)/shard_map/ppermute | solution.py:397
  30.4 84.1 %copy-start.1 = (bf16[2,192,3072]{2,1,0:T(8,128)(2,1)S(1)}, bf16[2,192,3072]{2,1,0:T(8,128)(2,1)}, u32[]{:S(2)}) copy-start(bf16[2,192,3072]{2,1,0:T(8,128)(2,1)} %maximum_select_fusion.refs_10_) | copy-start | bytes 7077892
  45.0 145.5 %collective-permute-start.3 = (bf16[256,3072]{1,0:T(8,128)(2,1)}, bf16[256,3072]{1,0:T(8,128)(2,1)}, u32[]{:S(2)}, u32[]{:S(2)}) collective-permute-start(bf16[256,3072]{1,0:T(8,128)(2,1)} %band.1.refs_0_), channel_id=1, source_target_pairs={{0,2},{1,3},{2,0},{3,1},{4,6},{5,7},{6,4},{7,5},{8,10},{9,11},{10,... | collective-permute-start | bytes 4718600 | tf_op jit(solution)/shard_map/ppermute | solution.py:137
  115.8 75.9 %collective-permute-start.6 = (bf16[2,128,3072]{2,1,0:T(8,128)(2,1)}, bf16[2,128,3072]{2,1,0:T(8,128)(2,1)}, u32[]{:S(2)}, u32[]{:S(2)}) collective-permute-start(bf16[2,128,3072]{2,1,0:T(8,128)(2,1)} %slice.42), channel_id=1, source_target_pairs={{8,0},{9,1},{10,2},{11,3},{12,4},{13,5},{14,6},{15,7},{16,8},{17,9... | collective-permute-start | bytes 4718600 | tf_op jit(solution)/shard_map/ppermute | solution.py:389
  141.1 60.6 %collective-permute-start.5 = (bf16[2,128,3072]{2,1,0:T(8,128)(2,1)}, bf16[2,128,3072]{2,1,0:T(8,128)(2,1)}, u32[]{:S(2)}, u32[]{:S(2)}) collective-permute-start(bf16[2,128,3072]{2,1,0:T(8,128)(2,1)} %slice.42), channel_id=1, source_target_pairs={{0,8},{1,9},{2,10},{3,11},{4,12},{5,13},{6,14},{7,15},{8,16},{9,17... | collective-permute-start | bytes 4718600 | tf_op jit(solution)/shard_map/ppermute | solution.py:389
  154.4 107.1 %all-to-all-start.1 = ((bf16[32,8,3072]{2,1,0:T(8,128)(2,1)}), bf16[32,8,3072]{2,1,0:T(8,128)(2,1)}, u32[]{:S(2)}, u32[]{:S(2)}) async-start(bf16[32,8,3072]{2,1,0:T(8,128)(2,1)} %strided.1), calls=%async_computation.1 | async-start | bytes 3145728 | tf_op jit(solution)/shard_map/all_to_all | solution.py:407
  189.6 52.0 %collective-permute-start.4 = (bf16[256,3072]{1,0:T(8,128)(2,1)}, bf16[256,3072]{1,0:T(8,128)(2,1)S(1)}, u32[]{:S(2)}, u32[]{:S(2)}) collective-permute-start(bf16[256,3072]{1,0:T(8,128)(2,1)} %band.1.refs_0_), channel_id=1, source_target_pairs={{0,4},{1,5},{2,6},{3,7},{4,0},{5,1},{6,2},{7,3},{8,12},{9,13},{10,... | collective-permute-start | bytes 4718600 | tf_op jit(solution)/shard_map/ppermute | solution.py:137
  189.9 71.6 %collective-permute-start.9 = (bf16[2,192,3072]{2,1,0:T(8,128)(2,1)S(1)}, bf16[2,192,3072]{2,1,0:T(8,128)(2,1)}, u32[]{:S(2)}, u32[]{:S(2)}) collective-permute-start(bf16[2,192,3072]{2,1,0:T(8,128)(2,1)S(1)} %copy-done.1), channel_id=1, source_target_pairs={{0,1},{1,0},{2,3},{3,2},{4,5},{5,4},{6,7},{7,6},{8,9},{9,8},{10,11... | collective-permute-start | bytes 7077896 | tf_op jit(solution)/shard_map/ppermute | solution.py:392
  201.8 59.7 %collective-permute-start.12 = (bf16[2,128,3072]{2,1,0:T(8,128)(2,1)}, bf16[2,128,3072]{2,1,0:T(8,128)(2,1)}, u32[]{:S(2)}, u32[]{:S(2)}) collective-permute-start(bf16[2,128,3072]{2,1,0:T(8,128)(2,1)} %collective-permute-done.5), channel_id=1, source_target_pairs={{0,8},{1,9},{2,10},{3,11},{4,12},{5,13},{6,14},{7,15},{8,16},{9,17... | collective-permute-start | bytes 4718600 | tf_op jit(solution)/shard_map/ppermute | solution.py:389
  203.1 58.5 %collective-permute-start.13 = (bf16[2,128,3072]{2,1,0:T(8,128)(2,1)}, bf16[2,128,3072]{2,1,0:T(8,128)(2,1)}, u32[]{:S(2)}, u32[]{:S(2)}) collective-permute-start(bf16[2,128,3072]{2,1,0:T(8,128)(2,1)} %collective-permute-done.6), channel_id=1, source_target_pairs={{8,0},{9,1},{10,2},{11,3},{12,4},{13,5},{14,6},{15,7},{16,8},{17,9... | collective-permute-start | bytes 4718600 | tf_op jit(solution)/shard_map/ppermute | solution.py:389
  241.6 19.0 %copy-start.10 = (bf16[256,3072]{1,0:T(8,128)(2,1)}, bf16[256,3072]{1,0:T(8,128)(2,1)S(1)}, u32[]{:S(2)}) copy-start(bf16[256,3072]{1,0:T(8,128)(2,1)S(1)} %collective-permute-done.4.refs_2_) | copy-start | bytes 4718596
  241.6 18.9 %collective-permute-start.8 = (bf16[128,3072]{1,0:T(8,128)(2,1)S(1)}, bf16[128,3072]{1,0:T(8,128)(2,1)S(1)}, u32[]{:S(2)}, u32[]{:S(2)}) collective-permute-start(bf16[128,3072]{1,0:T(8,128)(2,1)S(1)} %slice.52), channel_id=1, source_target_pairs={{0,2},{1,3},{2,0},{3,1},{4,6},{5,7},{6,4},{7,5},{8,10},{9,11},{10,... | collective-permute-start | bytes 2359304 | tf_op jit(solution)/shard_map/ppermute | solution.py:137
  241.8 19.7 %collective-permute-start.7 = (bf16[128,3072]{1,0:T(8,128)(2,1)S(1)}, bf16[128,3072]{1,0:T(8,128)(2,1)}, u32[]{:S(2)}, u32[]{:S(2)}) collective-permute-start(bf16[128,3072]{1,0:T(8,128)(2,1)S(1)} %slice.51), channel_id=1, source_target_pairs={{0,4},{1,5},{2,6},{3,7},{4,0},{5,1},{6,2},{7,3},{8,12},{9,13},{10,... | collective-permute-start | bytes 2359304 | tf_op jit(solution)/shard_map/ppermute | solution.py:137
  261.5 62.5 %collective-permute-start.23 = (bf16[2,128,3072]{2,1,0:T(8,128)(2,1)}, bf16[2,128,3072]{2,1,0:T(8,128)(2,1)}, u32[]{:S(2)}, u32[]{:S(2)}) collective-permute-start(bf16[2,128,3072]{2,1,0:T(8,128)(2,1)} %collective-permute-done.12), channel_id=1, source_target_pairs={{0,8},{1,9},{2,10},{3,11},{4,12},{5,13},{6,14},{7,15},{8,16},{9,17... | collective-permute-start | bytes 4718600 | tf_op jit(solution)/shard_map/ppermute | solution.py:389
  262.9 26.7 %collective-permute-start.17 = (bf16[2,64,3072]{2,1,0:T(8,128)(2,1)S(1)}, bf16[2,64,3072]{2,1,0:T(8,128)(2,1)}, u32[]{:S(2)}, u32[]{:S(2)}) collective-permute-start(bf16[2,64,3072]{2,1,0:T(8,128)(2,1)S(1)} %slice.45), channel_id=1, source_target_pairs={{8,0},{9,1},{10,2},{11,3},{12,4},{13,5},{14,6},{15,7},{16,8},{17,9... | collective-permute-start | bytes 2359304 | tf_op jit(solution)/shard_map/ppermute | solution.py:389
  275.2 47.4 %collective-permute-start.15 = (bf16[2,64,3072]{2,1,0:T(8,128)(2,1)S(1)}, bf16[2,64,3072]{2,1,0:T(8,128)(2,1)}, u32[]{:S(2)}, u32[]{:S(2)}) collective-permute-start(bf16[2,64,3072]{2,1,0:T(8,128)(2,1)S(1)} %slice.45), channel_id=1, source_target_pairs={{0,8},{1,9},{2,10},{3,11},{4,12},{5,13},{6,14},{7,15},{8,16},{9,17... | collective-permute-start | bytes 2359304 | tf_op jit(solution)/shard_map/ppermute | solution.py:389
  276.5 50.1 %collective-permute-start.22 = (bf16[2,128,3072]{2,1,0:T(8,128)(2,1)}, bf16[2,128,3072]{2,1,0:T(8,128)(2,1)S(1)}, u32[]{:S(2)}, u32[]{:S(2)}) collective-permute-start(bf16[2,128,3072]{2,1,0:T(8,128)(2,1)} %collective-permute-done.13), channel_id=1, source_target_pairs={{8,0},{9,1},{10,2},{11,3},{12,4},{13,5},{14,6},{15,7},{16,8},{17,9... | collective-permute-start | bytes 4718600 | tf_op jit(solution)/shard_map/ppermute | solution.py:389
  289.6 50.7 %collective-permute-start.18 = (bf16[2,64,3072]{2,1,0:T(8,128)(2,1)}, bf16[2,64,3072]{2,1,0:T(8,128)(2,1)}, u32[]{:S(2)}, u32[]{:S(2)}) collective-permute-start(bf16[2,64,3072]{2,1,0:T(8,128)(2,1)} %collective-permute-done.17), channel_id=1, source_target_pairs={{8,0},{9,1},{10,2},{11,3},{12,4},{13,5},{14,6},{15,7},{16,8},{17,9... | collective-permute-start | bytes 2359304 | tf_op jit(solution)/shard_map/ppermute | solution.py:389
  322.6 20.0 %collective-permute-start.16 = (bf16[2,64,3072]{2,1,0:T(8,128)(2,1)}, bf16[2,64,3072]{2,1,0:T(8,128)(2,1)}, u32[]{:S(2)}, u32[]{:S(2)}) collective-permute-start(bf16[2,64,3072]{2,1,0:T(8,128)(2,1)} %collective-permute-done.15), channel_id=1, source_target_pairs={{0,8},{1,9},{2,10},{3,11},{4,12},{5,13},{6,14},{7,15},{8,16},{9,17... | collective-permute-start | bytes 2359304 | tf_op jit(solution)/shard_map/ppermute | solution.py:389
  323.9 34.1 %collective-permute-start.11 = (bf16[256,3072]{1,0:T(8,128)(2,1)}, bf16[256,3072]{1,0:T(8,128)(2,1)S(1)}, u32[]{:S(2)}, u32[]{:S(2)}) collective-permute-start(bf16[256,3072]{1,0:T(8,128)(2,1)} %bitcast.11.refs_5_), channel_id=1, source_target_pairs={{0,4},{1,5},{2,6},{3,7},{4,0},{5,1},{6,2},{7,3},{8,12},{9,13},{10,... | collective-permute-start | bytes 4718600 | tf_op jit(solution)/shard_map/ppermute | solution.py:137
  324.0 34.1 %collective-permute-start.10 = (bf16[256,3072]{1,0:T(8,128)(2,1)}, bf16[256,3072]{1,0:T(8,128)(2,1)S(1)}, u32[]{:S(2)}, u32[]{:S(2)}) collective-permute-start(bf16[256,3072]{1,0:T(8,128)(2,1)} %bitcast.11.refs_5_), channel_id=1, source_target_pairs={{0,2},{1,3},{2,0},{3,1},{4,6},{5,7},{6,4},{7,5},{8,10},{9,11},{10,... | collective-permute-start | bytes 4718600 | tf_op jit(solution)/shard_map/ppermute | solution.py:137
  328.5 48.7 %collective-permute-start.24 = (bf16[2,2,128,3072]{3,2,1,0:T(8,128)(2,1)S(1)}, bf16[2,2,128,3072]{3,2,1,0:T(8,128)(2,1)}, u32[]{:S(2)}, u32[]{:S(2)}) collective-permute-start(bf16[2,2,128,3072]{3,2,1,0:T(8,128)(2,1)S(1)} %pad_maximum_fusion.refs_14_), channel_id=1, source_target_pairs={{0,1},{1,0},{2,3},{3,2},{4,5},{5,4},{6,7},{7,6},{8,9},{9,8},{10,11... | collective-permute-start | bytes 9437192 | tf_op jit(solution)/shard_map/ppermute | solution.py:392
  332.8 25.3 %copy-start.4 = (bf16[2,128,3072]{2,1,0:T(8,128)(2,1)}, bf16[2,128,3072]{2,1,0:T(8,128)(2,1)S(1)}, u32[]{:S(2)}) copy-start(bf16[2,128,3072]{2,1,0:T(8,128)(2,1)S(1)} %broadcast_select_fusion.refs_12_) | copy-start | bytes 4718596
  340.3 17.8 %collective-permute-start.14 = (bf16[2,128,3072]{2,1,0:T(8,128)(2,1)S(1)}, bf16[2,128,3072]{2,1,0:T(8,128)(2,1)S(1)}, u32[]{:S(2)}, u32[]{:S(2)}) collective-permute-start(bf16[2,128,3072]{2,1,0:T(8,128)(2,1)S(1)} %broadcast_select_fusion.refs_12_), channel_id=1, source_target_pairs={{0,1},{1,0},{2,3},{3,2},{4,5},{5,4},{6,7},{7,6},{8,9},{9,8},{10,11... | collective-permute-start | bytes 4718600 | tf_op jit(solution)/shard_map/ppermute | solution.py:392
  343.9 14.3 %copy-start.6 = (bf16[2,64,3072]{2,1,0:T(8,128)(2,1)}, bf16[2,64,3072]{2,1,0:T(8,128)(2,1)S(1)}, u32[]{:S(2)}) copy-start(bf16[2,64,3072]{2,1,0:T(8,128)(2,1)S(1)} %broadcast_select_fusion.1.refs_12_) | copy-start | bytes 2359300
  343.9 4.1 collective-permute-start.19
  348.0 10.2 %copy-start.19 = (bf16[2,64,3072]{2,1,0:T(8,128)(2,1)}, bf16[2,64,3072]{2,1,0:T(8,128)(2,1)S(1)}, u32[]{:S(2)}) copy-start(bf16[2,64,3072]{2,1,0:T(8,128)(2,1)S(1)} %collective-permute-done.19.refs_13_) | copy-start | bytes 2359300
  358.1 17.2 %copy-start.12 = (bf16[256,3072]{1,0:T(8,128)(2,1)}, bf16[256,3072]{1,0:T(8,128)(2,1)S(1)}, u32[]{:S(2)}) copy-start(bf16[256,3072]{1,0:T(8,128)(2,1)S(1)} %collective-permute-done.10.refs_6_) | copy-start | bytes 4718596
  358.1 17.2 %copy-start.17 = (bf16[2,128,3072]{2,1,0:T(8,128)(2,1)}, bf16[2,128,3072]{2,1,0:T(8,128)(2,1)S(1)}, u32[]{:S(2)}) copy-start(bf16[2,128,3072]{2,1,0:T(8,128)(2,1)S(1)} %collective-permute-done.14.refs_13_) | copy-start | bytes 4718596
  359.2 16.1 %collective-permute-start.21 = (bf16[128,3072]{1,0:T(8,128)(2,1)S(1)}, bf16[128,3072]{1,0:T(8,128)(2,1)S(1)}, u32[]{:S(2)}, u32[]{:S(2)}) collective-permute-start(bf16[128,3072]{1,0:T(8,128)(2,1)S(1)} %slice.47), channel_id=1, source_target_pairs={{0,2},{1,3},{2,0},{3,1},{4,6},{5,7},{6,4},{7,5},{8,10},{9,11},{10,... | collective-permute-start | bytes 2359304 | tf_op jit(solution)/shard_map/ppermute | solution.py:137
  359.8 15.5 %collective-permute-start.20 = (bf16[128,3072]{1,0:T(8,128)(2,1)S(1)}, bf16[128,3072]{1,0:T(8,128)(2,1)S(1)}, u32[]{:S(2)}, u32[]{:S(2)}) collective-permute-start(bf16[128,3072]{1,0:T(8,128)(2,1)S(1)} %slice.46), channel_id=1, source_target_pairs={{0,4},{1,5},{2,6},{3,7},{4,0},{5,1},{6,2},{7,3},{8,12},{9,13},{10,... | collective-permute-start | bytes 2359304 | tf_op jit(solution)/shard_map/ppermute | solution.py:137
  360.7 39.8 %collective-permute-start.29 = (bf16[2,64,3072]{2,1,0:T(8,128)(2,1)}, bf16[2,64,3072]{2,1,0:T(8,128)(2,1)}, u32[]{:S(2)}, u32[]{:S(2)}) collective-permute-start(bf16[2,64,3072]{2,1,0:T(8,128)(2,1)} %collective-permute-done.18), channel_id=1, source_target_pairs={{8,0},{9,1},{10,2},{11,3},{12,4},{13,5},{14,6},{15,7},{16,8},{17,9... | collective-permute-start | bytes 2359304 | tf_op jit(solution)/shard_map/ppermute | solution.py:389
  365.2 35.3 %collective-permute-start.28 = (bf16[2,64,3072]{2,1,0:T(8,128)(2,1)}, bf16[2,64,3072]{2,1,0:T(8,128)(2,1)}, u32[]{:S(2)}, u32[]{:S(2)}) collective-permute-start(bf16[2,64,3072]{2,1,0:T(8,128)(2,1)} %collective-permute-done.16), channel_id=1, source_target_pairs={{0,8},{1,9},{2,10},{3,11},{4,12},{5,13},{6,14},{7,15},{8,16},{9,17... | collective-permute-start | bytes 2359304 | tf_op jit(solution)/shard_map/ppermute | solution.py:389
  402.2 7.1 %copy-start.5 = (bf16[2,2,64,3072]{3,2,1,0:T(8,128)(2,1)}, bf16[2,2,64,3072]{3,2,1,0:T(8,128)(2,1)S(1)}, u32[]{:S(2)}) copy-start(bf16[2,2,64,3072]{3,2,1,0:T(8,128)(2,1)S(1)} %pad_maximum_fusion.1.refs_14_) | copy-start | bytes 4718596
  402.2 7.1 %collective-permute-start.30 = (bf16[2,2,64,3072]{3,2,1,0:T(8,128)(2,1)S(1)}, bf16[2,2,64,3072]{3,2,1,0:T(8,128)(2,1)}, u32[]{:S(2)}, u32[]{:S(2)}) collective-permute-start(bf16[2,2,64,3072]{3,2,1,0:T(8,128)(2,1)S(1)} %pad_maximum_fusion.1.refs_14_), channel_id=1, source_target_pairs={{0,1},{1,0},{2,3},{3,2},{4,5},{5,4},{6,7},{7,6},{8,9},{9,8},{10,11... | collective-permute-start | bytes 4718600 | tf_op jit(solution)/shard_map/ppermute | solution.py:392
  406.2 19.0 %collective-permute-start.25 = (bf16[256,1024]{1,0:T(8,128)(2,1)}, bf16[256,1024]{1,0:T(8,128)(2,1)S(1)}, u32[]{:S(2)}, u32[]{:S(2)}) collective-permute-start(bf16[256,1024]{1,0:T(8,128)(2,1)} %get-tuple-element.59), channel_id=1, source_target_pairs={{0,2},{1,3},{2,0},{3,1},{4,6},{5,7},{6,4},{7,5},{8,10},{9,11},{10,... | collective-permute-start | bytes 1572872 | tf_op jit(solution)/shard_map/ppermute | solution.py:137
  406.8 19.9 %collective-permute-start.26 = (bf16[256,1024]{1,0:T(8,128)(2,1)}, bf16[256,1024]{1,0:T(8,128)(2,1)S(1)}, u32[]{:S(2)}, u32[]{:S(2)}) collective-permute-start(bf16[256,1024]{1,0:T(8,128)(2,1)} %get-tuple-element.60), channel_id=1, source_target_pairs={{0,4},{1,5},{2,6},{3,7},{4,0},{5,1},{6,2},{7,3},{8,12},{9,13},{10,... | collective-permute-start | bytes 1572872 | tf_op jit(solution)/shard_map/ppermute | solution.py:137
  407.3 23.8 %collective-permute-start.27 = (bf16[256,1024]{1,0:T(8,128)(2,1)}, bf16[256,1024]{1,0:T(8,128)(2,1)S(1)}, u32[]{:S(2)}, u32[]{:S(2)}) collective-permute-start(bf16[256,1024]{1,0:T(8,128)(2,1)} %get-tuple-element.61), channel_id=1, source_target_pairs={{0,6},{1,7},{2,4},{3,5},{4,2},{5,3},{6,0},{7,1},{8,14},{9,15},{10,... | collective-permute-start | bytes 1572872 | tf_op jit(solution)/shard_map/ppermute | solution.py:137
  423.9 12.7 %collective-permute-start.31 = (bf16[256,512]{1,0:T(8,128)(2,1)}, bf16[256,512]{1,0:T(8,128)(2,1)S(1)}, u32[]{:S(2)}, u32[]{:S(2)}) collective-permute-start(bf16[256,512]{1,0:T(8,128)(2,1)} %get-tuple-element.72), channel_id=1, source_target_pairs={{0,2},{1,3},{2,0},{3,1},{4,6},{5,7},{6,4},{7,5},{8,10},{9,11},{10,... | collective-permute-start | bytes 786440 | tf_op jit(solution)/shard_map/ppermute | solution.py:137
  424.6 13.2 %collective-permute-start.32 = (bf16[256,512]{1,0:T(8,128)(2,1)}, bf16[256,512]{1,0:T(8,128)(2,1)S(1)}, u32[]{:S(2)}, u32[]{:S(2)}) collective-permute-start(bf16[256,512]{1,0:T(8,128)(2,1)} %get-tuple-element.73), channel_id=1, source_target_pairs={{0,4},{1,5},{2,6},{3,7},{4,0},{5,1},{6,2},{7,3},{8,12},{9,13},{10,... | collective-permute-start | bytes 786440 | tf_op jit(solution)/shard_map/ppermute | solution.py:137
  425.1 17.2 %copy-start.7 = (bf16[256,1024]{1,0:T(8,128)(2,1)}, bf16[256,1024]{1,0:T(8,128)(2,1)S(1)}, u32[]{:S(2)}) copy-start(bf16[256,1024]{1,0:T(8,128)(2,1)S(1)} %collective-permute-done.25.refs_1_) | copy-start | bytes 1572868
  425.1 17.2 %collective-permute-start.33 = (bf16[256,512]{1,0:T(8,128)(2,1)}, bf16[256,512]{1,0:T(8,128)(2,1)S(1)}, u32[]{:S(2)}, u32[]{:S(2)}) collective-permute-start(bf16[256,512]{1,0:T(8,128)(2,1)} %get-tuple-element.74), channel_id=1, source_target_pairs={{0,6},{1,7},{2,4},{3,5},{4,2},{5,3},{6,0},{7,1},{8,14},{9,15},{10,... | collective-permute-start | bytes 786440 | tf_op jit(solution)/shard_map/ppermute | solution.py:137
  426.7 15.7 %copy-start.8 = (bf16[256,1024]{1,0:T(8,128)(2,1)}, bf16[256,1024]{1,0:T(8,128)(2,1)S(1)}, u32[]{:S(2)}) copy-start(bf16[256,1024]{1,0:T(8,128)(2,1)S(1)} %collective-permute-done.26.refs_2_) | copy-start | bytes 1572868
  431.1 11.3 %copy-start.9 = (bf16[256,1024]{1,0:T(8,128)(2,1)}, bf16[256,1024]{1,0:T(8,128)(2,1)S(1)}, u32[]{:S(2)}) copy-start(bf16[256,1024]{1,0:T(8,128)(2,1)S(1)} %collective-permute-done.27.refs_3_) | copy-start | bytes 1572868
  (10 other events, 22.8 us)
